TPU v7x, 128 devices: a whole 4x4x4 slice. The times are simulated.
128 devices in a mesh: dp: 4 (over z), section: 4 (over y), expert: 8 (over x, core).
Axes of the slice: x: 4, y: 4, z: 4, core: 2. Of those that a mesh axis runs over, the one named last changes fastest.
Arguments:
- tokens: bfloat16 [4096, 5120], P(('dp', 'expert')), may hold values from -6 to 6
- cotangent: bfloat16 [4096, 5120], P(('dp', 'expert')), may hold values from -6 to 6
- norm_gain: float32 [4, 5120], P('section'), may hold values from 0.25 to 1.75
- route_gates: float32 [4, 4096, 6], P('section', ('dp', 'expert')), may hold values from 0.5 to 2
- expert_ids: int32 [4, 4096, 6], P('section', ('dp', 'expert')), may hold values from 0 to 159, as said below
- expert_map: int32 [4, 8], P('section'), may hold values from 0 to 7, each once within a row
- w_gate: bfloat16 [4, 8, 5120, 768], P('section', 'expert', 'dp'), may hold values from -0.078125 to 0.078125
- w_up: bfloat16 [4, 8, 5120, 768], P('section', 'expert', 'dp'), may hold values from -0.078125 to 0.078125
- w_down: bfloat16 [4, 8, 768, 5120], P('section', 'expert', None, 'dp'), may hold values from -0.21875 to 0.21875
Outputs:
- layer_out: bfloat16 [4, 4096, 5120], P('section', ('dp', 'expert'))
- input_grad: bfloat16 [4, 4096, 5120], P('section', ('dp', 'expert'))
- grad_gate: bfloat16 [4, 8, 5120, 768], P('section', 'expert', 'dp')
- grad_up: bfloat16 [4, 8, 5120, 768], P('section', 'expert', 'dp')
- grad_down: bfloat16 [4, 8, 768, 5120], P('section', 'expert', None, 'dp')
Inputs may be any that keep to these rules, and one draw needn't show every extreme that they name: `expert_ids`: each token names 6 different experts on each layer. The held experts are those below 8. Split the 128 tokens of one index pair of dp and expert in order into 4 equal blocks: in each block each held expert is named by at most 2 tokens, and on every layer one held expert is named by exactly 2 tokens of every block, so by 8 tokens of every such pair. `expert_map`: each layer's row names every held expert once.
All inputs are finite; a program needn't handle non-finite values.
Results may differ from a plain program's by a relative error of at most 0.03.
Values may be sent and summed in bfloat16 or wider, within the bound.
No kernel may reach another device: no remote copies, remote signals or barrier semaphores. Data moves between devices by JAX's collectives and lax.ppermute only.
A program may use at most 128 MiB of HBM per device.

v0:
```python
import jax
import jax.numpy as jnp
from jax import lax
from jax.sharding import PartitionSpec as P

CAP = 8


def from_behind(value, axis, steps):
    count = lax.axis_size(axis)
    leading, last = (max(0, -steps), min(count, count - steps))
    return lax.ppermute(value, axis, [(source, source + steps) for source in range(leading, last)])


def route_tables(route_ids, route_weights, held_experts, capacity):
    matches = route_ids[:, :, None] == held_experts[None, None, :]
    chosen = jnp.any(matches, axis=1)
    weights = jnp.sum(jnp.where(matches, route_weights[:, :, None], 0.0), axis=1)
    position = jnp.cumsum(chosen.astype(jnp.int32), axis=0) - 1
    slot_ids = jnp.arange(capacity, dtype=jnp.int32)
    placed = chosen[:, :, None] & (position[:, :, None] == slot_ids[None, None, :])
    return (placed.astype(jnp.bfloat16), weights)


def deliver(buffer):
    flat_buffer = buffer.reshape((-1,) + buffer.shape[2:])
    exchanged = lax.all_to_all(
        flat_buffer, ("dp", "expert"), split_axis=0, concat_axis=0, tiled=True
    )
    return exchanged.reshape(buffer.shape)


def gate_backward(hidden_grad, gate_pre, up_pre):
    sigmoid_gate = jax.nn.sigmoid(gate_pre)
    gate_grad = (
        hidden_grad * up_pre * sigmoid_gate * (1.0 + gate_pre * (1.0 - sigmoid_gate))
    ).astype(jnp.bfloat16)
    up_grad = (hidden_grad * gate_pre * sigmoid_gate).astype(jnp.bfloat16)
    return (gate_grad, up_grad)


def local(tokens, cotangent, norm_gain, route_gates, expert_ids, expert_map, w_gate, w_up, w_down):
    section_index = lax.axis_index("section")
    section_count = lax.axis_size("section")
    dp_groups = lax.axis_size("dp")
    held_experts = expert_map[0]
    route_rows = expert_ids[0]
    gate_rows = route_gates[0]
    norm_scale = norm_gain[0][None, :]
    gate_weight = w_gate[0, 0]
    up_weight = w_up[0, 0]
    down_weight = w_down[0, 0]
    model_width = tokens.shape[1]
    slice_width = gate_weight.shape[0]
    contract_first = (((0,), (0,)), ((), ()))
    contract_second = (((1,), (1,)), ((), ()))
    dispatch, token_weight = route_tables(route_rows, gate_rows, held_experts, CAP)
    current = tokens
    stored = None
    for step_index in range(section_count):
        forward_rows_here = current.shape[0]
        forward_wide_in = current.astype(jnp.float32)
        forward_inv_rms = lax.rsqrt(
            jnp.mean(forward_wide_in * forward_wide_in, axis=1, keepdims=True) + 1e-06
        )
        normed = (forward_wide_in * forward_inv_rms * norm_scale).astype(jnp.bfloat16)
        forward_outgoing = jnp.einsum(
            "tpc,tqd->qpcd",
            dispatch,
            normed.reshape(forward_rows_here, dp_groups, slice_width),
            preferred_element_type=jnp.float32,
        ).astype(jnp.bfloat16)
        forward_slot_rows = deliver(forward_outgoing).reshape(-1, slice_width)
        gate_part = jnp.dot(forward_slot_rows, gate_weight, preferred_element_type=jnp.float32)
        up_part = jnp.dot(forward_slot_rows, up_weight, preferred_element_type=jnp.float32)
        forward_gate_pre = lax.psum(gate_part.astype(jnp.bfloat16), "dp").astype(jnp.float32)
        forward_up_pre = lax.psum(up_part.astype(jnp.bfloat16), "dp").astype(jnp.float32)
        forward_activated = (
            forward_gate_pre * jax.nn.sigmoid(forward_gate_pre) * forward_up_pre
        ).astype(jnp.bfloat16)
        expert_out = jnp.dot(
            forward_activated, down_weight, preferred_element_type=jnp.float32
        ).astype(jnp.bfloat16)
        forward_returned = deliver(expert_out.reshape(forward_outgoing.shape))
        picked = jnp.einsum(
            "tpc,qpcd->tpqd", dispatch, forward_returned, preferred_element_type=jnp.bfloat16
        )
        combined = jnp.sum(
            token_weight[:, :, None, None] * picked.astype(jnp.float32), axis=1
        ).reshape(forward_rows_here, model_width)
        result = (forward_wide_in + combined).astype(jnp.bfloat16)
        result, saved_state = (
            result,
            (
                current,
                forward_inv_rms,
                forward_slot_rows,
                forward_gate_pre,
                forward_up_pre,
                forward_activated,
            ),
        )
        if step_index == 0:
            stored = (result, saved_state)
        else:
            stored = jax.tree.map(
                lambda latest, earlier: jnp.where(section_index == step_index, latest, earlier),
                (result, saved_state),
                stored,
            )
        if step_index + 1 < section_count:
            current = from_behind(result, "section", 1)
    layer_result, saved_state = stored
    incoming = cotangent
    collected = None
    for step_index in range(section_count):
        layer_in, inv_rms, slot_rows, gate_pre, up_pre, activated = saved_state
        rows_here = incoming.shape[0]
        experts_here = dispatch.shape[1]
        grad_wide = incoming.astype(jnp.float32)
        scaled = (token_weight[:, :, None] * grad_wide[:, None, :]).astype(jnp.bfloat16)
        scaled = scaled.reshape(rows_here, experts_here, dp_groups, slice_width)
        outgoing = jnp.einsum(
            "tpc,tpqd->qpcd", dispatch, scaled, preferred_element_type=jnp.bfloat16
        )
        slot_grad = deliver(outgoing).reshape(-1, slice_width)
        backward_down_grad = lax.dot_general(
            activated, slot_grad, contract_first, preferred_element_type=jnp.float32
        )
        hidden_part = lax.dot_general(
            slot_grad, down_weight, contract_second, preferred_element_type=jnp.float32
        )
        hidden_grad = lax.psum(hidden_part.astype(jnp.bfloat16), "dp").astype(jnp.float32)
        gate_grad, up_grad = gate_backward(hidden_grad, gate_pre, up_pre)
        backward_gate_wgrad = lax.dot_general(
            slot_rows, gate_grad, contract_first, preferred_element_type=jnp.float32
        )
        backward_up_wgrad = lax.dot_general(
            slot_rows, up_grad, contract_first, preferred_element_type=jnp.float32
        )
        slot_back = (
            lax.dot_general(
                gate_grad, gate_weight, contract_second, preferred_element_type=jnp.float32
            )
            + lax.dot_general(
                up_grad, up_weight, contract_second, preferred_element_type=jnp.float32
            )
        ).astype(jnp.bfloat16)
        returned = deliver(slot_back.reshape(outgoing.shape))
        normed_grad = jnp.einsum(
            "tpc,qpcd->tqd", dispatch, returned, preferred_element_type=jnp.float32
        ).reshape(rows_here, model_width)
        wide_in = layer_in.astype(jnp.float32)
        scaled_grad = normed_grad * norm_scale
        through_norm = inv_rms * (
            scaled_grad
            - wide_in * inv_rms * inv_rms * jnp.mean(scaled_grad * wide_in, axis=1, keepdims=True)
        )
        grad_in = (grad_wide + through_norm).astype(jnp.bfloat16)
        weight_grads = (backward_gate_wgrad, backward_up_wgrad, backward_down_grad)
        if step_index == 0:
            collected = (grad_in, weight_grads)
        else:
            collected = jax.tree.map(
                lambda latest, earlier: jnp.where(
                    section_index == section_count - 1 - step_index, latest, earlier
                ),
                (grad_in, weight_grads),
                collected,
            )
        if step_index + 1 < section_count:
            incoming = from_behind(grad_in, "section", -1)
    grad_in, weight_grads = collected
    gate_wgrad, up_wgrad, down_grad = weight_grads
    return (
        layer_result[None],
        grad_in[None],
        gate_wgrad.astype(jnp.bfloat16)[None, None],
        up_wgrad.astype(jnp.bfloat16)[None, None],
        down_grad.astype(jnp.bfloat16)[None, None],
    )


def solution(mesh):
    return jax.shard_map(
        local,
        mesh=mesh,
        in_specs=(
            P(("dp", "expert"), None),
            P(("dp", "expert"), None),
            P("section", None),
            P("section", ("dp", "expert"), None),
            P("section", ("dp", "expert"), None),
            P("section", None),
            P("section", "expert", "dp", None),
            P("section", "expert", "dp", None),
            P("section", "expert", None, "dp"),
        ),
        out_specs=(
            P("section", ("dp", "expert"), None),
            P("section", ("dp", "expert"), None),
            P("section", "expert", "dp", None),
            P("section", "expert", "dp", None),
            P("section", "expert", None, "dp"),
        ),
        check_vma=False,
    )
```

profile of v0, /device:TPU:1, one launch (start us, length us, event | category | flops | bytes accessed | tf_op | source)
XLA Modules:
  0.0 934.9 jit_solution(3443919449083149505)
XLA Ops:
  18.6 22.1 %all_to_all.80 = bf16[32,8,1280]{2,1,0:T(8,128)(2,1)S(1)} all-to-all(bf16[32,8,1280]{2,1,0:T(8,128)(2,1)S(1)} %bitcast.294), channel_id=1, replica_groups=mesh['dp'=4,'section'=4,'expert'=8] {'dp','expert'}, dimensions={0} | all-to-all | bytes 1310720 | tf_op jit(solution)/shard_map/all_to_all | solution.py:27
  44.0 40.7 %all-reduce.24.cloned.1.call-done = (bf16[256,768]{1,0:T(8,128)(2,1)}, bf16[256,768]{1,0:T(8,128)(2,1)}) async-done(((bf16[256,768]{1,0:T(8,128)(2,1)}, bf16[256,768]{1,0:T(8,128)(2,1)}), (bf16[256,768]{1,0:T(8,128)(2,1)}, bf16[256,768]{1,0:T(8,128)(2,1)})) %all-reduce.24.cloned.1.call-update) | async-done | bytes 786448 | tf_op jit(solution)/shard_map/psum | solution.py:77
  87.5 9.0 all-to-all-start.1
  96.7 12.7 %all-to-all-done.1 = bf16[32,8,1280]{2,1,0:T(8,128)(2,1)} async-done(((bf16[32,8,1280]{2,1,0:T(8,128)(2,1)}), bf16[32,8,1280]{2,1,0:T(8,128)(2,1)}, u32[]{:S(2)}, u32[]{:S(2)}) %all-to-all-start.1) | async-done | bytes 655392 | tf_op jit(solution)/shard_map/all_to_all | solution.py:27
  109.4 6.3 fusion.3
  124.2 27.5 %collective-permute-done = bf16[128,5120]{1,0:T(8,128)(2,1)S(1)} collective-permute-done((bf16[128,5120]{1,0:T(8,128)(2,1)S(1)}, bf16[128,5120]{1,0:T(8,128)(2,1)S(1)}, u32[]{:S(2)}, u32[]{:S(2)}) %collective-permute-start) | collective-permute-done | bytes 1310752 | tf_op jit(solution)/shard_map/ppermute | solution.py:12
  159.0 17.6 %all_to_all.81 = bf16[32,8,1280]{2,1,0:T(8,128)(2,1)S(1)} all-to-all(bf16[32,8,1280]{2,1,0:T(8,128)(2,1)S(1)} %bitcast.295), channel_id=1, replica_groups=mesh['dp'=4,'section'=4,'expert'=8] {'dp','expert'}, dimensions={0} | all-to-all | bytes 1310720 | tf_op jit(solution)/shard_map/all_to_all | solution.py:27
  180.3 41.3 %all-reduce.22.cloned.1.call-done = (bf16[256,768]{1,0:T(8,128)(2,1)}, bf16[256,768]{1,0:T(8,128)(2,1)}) async-done(((bf16[256,768]{1,0:T(8,128)(2,1)}, bf16[256,768]{1,0:T(8,128)(2,1)}), (bf16[256,768]{1,0:T(8,128)(2,1)}, bf16[256,768]{1,0:T(8,128)(2,1)})) %all-reduce.22.cloned.1.call-update) | async-done | bytes 786448 | tf_op jit(solution)/shard_map/psum | solution.py:77
  223.5 21.6 %all_to_all.82 = bf16[32,8,1280]{2,1,0:T(8,128)(2,1)S(1)} all-to-all(bf16[32,8,1280]{2,1,0:T(8,128)(2,1)S(1)} %fusion.76), channel_id=1, replica_groups=mesh['dp'=4,'section'=4,'expert'=8] {'dp','expert'}, dimensions={0} | all-to-all | bytes 1310720 | tf_op jit(solution)/shard_map/all_to_all | solution.py:27
  259.0 27.5 %collective-permute-done.1 = bf16[128,5120]{1,0:T(8,128)(2,1)S(1)} collective-permute-done((bf16[128,5120]{1,0:T(8,128)(2,1)S(1)}, bf16[128,5120]{1,0:T(8,128)(2,1)S(1)}, u32[]{:S(2)}, u32[]{:S(2)}) %collective-permute-start.1) | collective-permute-done | bytes 1310752 | tf_op jit(solution)/shard_map/ppermute | solution.py:12
  293.8 17.6 %all_to_all.83 = bf16[32,8,1280]{2,1,0:T(8,128)(2,1)S(1)} all-to-all(bf16[32,8,1280]{2,1,0:T(8,128)(2,1)S(1)} %bitcast.296), channel_id=1, replica_groups=mesh['dp'=4,'section'=4,'expert'=8] {'dp','expert'}, dimensions={0} | all-to-all | bytes 1310720 | tf_op jit(solution)/shard_map/all_to_all | solution.py:27
  314.8 41.6 %all-reduce.20.cloned.1.call-done = (bf16[256,768]{1,0:T(8,128)(2,1)}, bf16[256,768]{1,0:T(8,128)(2,1)}) async-done(((bf16[256,768]{1,0:T(8,128)(2,1)}, bf16[256,768]{1,0:T(8,128)(2,1)}), (bf16[256,768]{1,0:T(8,128)(2,1)}, bf16[256,768]{1,0:T(8,128)(2,1)})) %all-reduce.20.cloned.1.call-update) | async-done | bytes 786448 | tf_op jit(solution)/shard_map/psum | solution.py:77
  358.3 21.6 %all_to_all.84 = bf16[32,8,1280]{2,1,0:T(8,128)(2,1)S(1)} all-to-all(bf16[32,8,1280]{2,1,0:T(8,128)(2,1)S(1)} %fusion.77), channel_id=1, replica_groups=mesh['dp'=4,'section'=4,'expert'=8] {'dp','expert'}, dimensions={0} | all-to-all | bytes 1310720 | tf_op jit(solution)/shard_map/all_to_all | solution.py:27
  408.4 14.2 %collective-permute-done.2 = bf16[128,5120]{1,0:T(8,128)(2,1)S(1)} collective-permute-done((bf16[128,5120]{1,0:T(8,128)(2,1)}, bf16[128,5120]{1,0:T(8,128)(2,1)S(1)}, u32[]{:S(2)}, u32[]{:S(2)}) %collective-permute-start.2) | collective-permute-done | bytes 1310752 | tf_op jit(solution)/shard_map/ppermute | solution.py:12
  438.2 10.2 %all-to-all-done.6 = bf16[32,8,1280]{2,1,0:T(8,128)(2,1)S(1)} async-done(((bf16[32,8,1280]{2,1,0:T(8,128)(2,1)}), bf16[32,8,1280]{2,1,0:T(8,128)(2,1)S(1)}, u32[]{:S(2)}, u32[]{:S(2)}) %all-to-all-start.6) | async-done | bytes 655392 | tf_op jit(solution)/shard_map/all_to_all | solution.py:27
  453.3 44.2 %all-reduce.18.cloned.1.call-done = (bf16[256,768]{1,0:T(8,128)(2,1)}, bf16[256,768]{1,0:T(8,128)(2,1)}, bf16[256,768]{1,0:T(8,128)(2,1)}) async-done(((bf16[256,768]{1,0:T(8,128)(2,1)}, bf16[256,768]{1,0:T(8,128)(2,1)}, bf16[256,768]{1,0:T(8,128)(2,1)}), (bf16[256,768]{1,0:T(8,128)(2,1)}, bf16[256,768]{1,0:T(8,128)(2,1)}, bf16[256,768]{1,0:T(8,128)(2,1)})) %all-reduce.18.cloned.1.call-update) | async-done | bytes 1179664 | tf_op jit(solution)/shard_map/psum | solution.py:77
  503.8 21.2 %all_to_all.85 = bf16[32,8,1280]{2,1,0:T(8,128)(2,1)S(1)} all-to-all(bf16[32,8,1280]{2,1,0:T(8,128)(2,1)S(1)} %fusion.74), channel_id=1, replica_groups=mesh['dp'=4,'section'=4,'expert'=8] {'dp','expert'}, dimensions={0} | all-to-all | bytes 1310720 | tf_op jit(solution)/shard_map/all_to_all | solution.py:27
  529.9 30.4 %collective-permute-done.3 = bf16[128,5120]{1,0:T(8,128)(2,1)} collective-permute-done((bf16[128,5120]{1,0:T(8,128)(2,1)S(1)}, bf16[128,5120]{1,0:T(8,128)(2,1)}, u32[]{:S(2)}, u32[]{:S(2)}) %collective-permute-start.3) | collective-permute-done | bytes 1310752 | tf_op jit(solution)/shard_map/ppermute | solution.py:12
  567.7 17.6 %all_to_all.86 = bf16[32,8,1280]{2,1,0:T(8,128)(2,1)S(1)} all-to-all(bf16[32,8,1280]{2,1,0:T(8,128)(2,1)S(1)} %bitcast.306), channel_id=1, replica_groups=mesh['dp'=4,'section'=4,'expert'=8] {'dp','expert'}, dimensions={0} | all-to-all | bytes 1310720 | tf_op jit(solution)/shard_map/all_to_all | solution.py:27
  587.6 38.1 %all-reduce.12.cloned.1.call-done = bf16[256,768]{1,0:T(8,128)(2,1)} async-done(((bf16[256,768]{1,0:T(8,128)(2,1)}), bf16[256,768]{1,0:T(8,128)(2,1)}) %all-reduce.12.cloned.1.call-update) | async-done | bytes 393232 | tf_op jit(solution)/shard_map/psum | solution.py:133
  631.1 21.7 %all_to_all.87 = bf16[32,8,1280]{2,1,0:T(8,128)(2,1)S(1)} all-to-all(bf16[32,8,1280]{2,1,0:T(8,128)(2,1)S(1)} %fusion.73), channel_id=1, replica_groups=mesh['dp'=4,'section'=4,'expert'=8] {'dp','expert'}, dimensions={0} | all-to-all | bytes 1310720 | tf_op jit(solution)/shard_map/all_to_all | solution.py:27
  668.3 20.6 %collective-permute-done.4 = bf16[128,5120]{1,0:T(8,128)(2,1)} collective-permute-done((bf16[128,5120]{1,0:T(8,128)(2,1)}, bf16[128,5120]{1,0:T(8,128)(2,1)}, u32[]{:S(2)}, u32[]{:S(2)}) %collective-permute-start.4) | collective-permute-done | bytes 1310752 | tf_op jit(solution)/shard_map/ppermute | solution.py:12
  697.2 5.5 all-to-all-start.12
  706.6 6.4 fusion
  722.7 37.8 %all-reduce.14.cloned.1.call-done = bf16[256,768]{1,0:T(8,128)(2,1)} async-done(((bf16[256,768]{1,0:T(8,128)(2,1)}), bf16[256,768]{1,0:T(8,128)(2,1)}) %all-reduce.14.cloned.1.call-update) | async-done | bytes 393232 | tf_op jit(solution)/shard_map/psum | solution.py:133
  766.7 9.1 all-to-all-start.13
  780.9 7.8 all-to-all-done.13
  800.5 24.5 %collective-permute-done.5 = bf16[128,5120]{1,0:T(8,128)(2,1)} collective-permute-done((bf16[128,5120]{1,0:T(8,128)(2,1)S(1)}, bf16[128,5120]{1,0:T(8,128)(2,1)}, u32[]{:S(2)}, u32[]{:S(2)}) %collective-permute-start.5) | collective-permute-done | bytes 1310752 | tf_op jit(solution)/shard_map/ppermute | solution.py:12
  845.0 6.8 all-to-all-done.14
  861.5 30.8 %all-reduce.16.cloned.1.call-done = bf16[256,768]{1,0:T(8,128)(2,1)} async-done(((bf16[256,768]{1,0:T(8,128)(2,1)}), bf16[256,768]{1,0:T(8,128)(2,1)}) %all-reduce.16.cloned.1.call-update) | async-done | bytes 393232 | tf_op jit(solution)/shard_map/psum | solution.py:133
  898.6 9.5 %all-to-all-start.15 = ((bf16[32,8,1280]{2,1,0:T(8,128)(2,1)}), bf16[32,8,1280]{2,1,0:T(8,128)(2,1)}, u32[]{:S(2)}, u32[]{:S(2)}) async-start(bf16[32,8,1280]{2,1,0:T(8,128)(2,1)} %fusion.71), calls=%async_computation.15 | async-start | bytes 1310720 | tf_op jit(solution)/shard_map/all_to_all | solution.py:27
  913.6 7.3 all-to-all-done.15
  (277 shorter events, 248.5 us)
Async XLA Ops:
  7.2 77.6 %copy-start = (bf16[1,1,768,1280]{3,2,1,0:T(8,128)(2,1)S(1)}, bf16[1,1,768,1280]{3,2,1,0:T(8,128)(2,1)}, u32[]{:S(2)}) copy-start(bf16[1,1,768,1280]{3,2,1,0:T(8,128)(2,1)} %param.17) | copy-start | bytes 5898244
  7.2 77.5 %all-reduce.24.cloned.1.call-start = ((), (), s32[]{:S(2)}) async-start(), calls=%async_computation.22 | async-start | bytes 1572864 | tf_op jit(solution)/shard_map/psum | solution.py:77
  16.8 23.9 %copy-start.61 = (bf16[1,1,1280,768]{3,2,1,0:T(8,128)(2,1)S(1)}, bf16[1,1,1280,768]{3,2,1,0:T(8,128)(2,1)}, u32[]{:S(2)}) copy-start(bf16[1,1,1280,768]{3,2,1,0:T(8,128)(2,1)} %param.16) | copy-start | bytes 5898244
  87.5 21.9 %all-to-all-start.1 = ((bf16[32,8,1280]{2,1,0:T(8,128)(2,1)}), bf16[32,8,1280]{2,1,0:T(8,128)(2,1)}, u32[]{:S(2)}, u32[]{:S(2)}) async-start(bf16[32,8,1280]{2,1,0:T(8,128)(2,1)} %fusion.75), calls=%async_computation.1 | async-start | bytes 1310720 | tf_op jit(solution)/shard_map/all_to_all | solution.py:27
  96.5 125.1 %all-reduce.22.cloned.1.call-start = ((), (), s32[]{:S(2)}) async-start(), calls=%async_computation.21 | async-start | bytes 1572864 | tf_op jit(solution)/shard_map/psum | solution.py:77
  119.0 33.1 %copy-start.50 = (f32[1,5120]{1,0:T(1,128)S(1)}, f32[1,5120]{1,0:T(1,128)}, u32[]{:S(2)}) copy-start(f32[1,5120]{1,0:T(1,128)} %param.11) | copy-start | bytes 61444
  121.0 30.8 %copy-start.30 = (bf16[128,5120]{1,0:T(8,128)(2,1)}, bf16[128,5120]{1,0:T(8,128)(2,1)S(1)}, u32[]{:S(2)}) copy-start(bf16[128,5120]{1,0:T(8,128)(2,1)S(1)} %fusion.29) | copy-start | bytes 3932164
  121.0 30.7 %collective-permute-start = (bf16[128,5120]{1,0:T(8,128)(2,1)S(1)}, bf16[128,5120]{1,0:T(8,128)(2,1)S(1)}, u32[]{:S(2)}, u32[]{:S(2)}) collective-permute-start(bf16[128,5120]{1,0:T(8,128)(2,1)S(1)} %fusion.29), channel_id=1, source_target_pairs={{0,8},{8,16},{16,24},{1,9},{9,17},{17,25},{2,10},{10,18},{18,26},{... | collective-permute-start | bytes 3932168 | tf_op jit(solution)/shard_map/ppermute | solution.py:12
  151.7 102.0 %copy-start.13 = (bf16[128,5120]{1,0:T(8,128)(2,1)}, bf16[128,5120]{1,0:T(8,128)(2,1)S(1)}, u32[]{:S(2)}) copy-start(bf16[128,5120]{1,0:T(8,128)(2,1)S(1)} %collective-permute-done) | copy-start | bytes 3932164
  180.0 176.4 %all-reduce.20.cloned.1.call-start = ((), (), s32[]{:S(2)}) async-start(), calls=%async_computation.20 | async-start | bytes 1572864 | tf_op jit(solution)/shard_map/psum | solution.py:77
  255.8 30.8 %copy-start.31 = (bf16[128,5120]{1,0:T(8,128)(2,1)}, bf16[128,5120]{1,0:T(8,128)(2,1)S(1)}, u32[]{:S(2)}) copy-start(bf16[128,5120]{1,0:T(8,128)(2,1)S(1)} %fusion.33) | copy-start | bytes 3932164
  255.8 30.7 %collective-permute-start.1 = (bf16[128,5120]{1,0:T(8,128)(2,1)S(1)}, bf16[128,5120]{1,0:T(8,128)(2,1)S(1)}, u32[]{:S(2)}, u32[]{:S(2)}) collective-permute-start(bf16[128,5120]{1,0:T(8,128)(2,1)S(1)} %fusion.33), channel_id=1, source_target_pairs={{0,8},{8,16},{16,24},{1,9},{9,17},{17,25},{2,10},{10,18},{18,26},{... | collective-permute-start | bytes 3932168 | tf_op jit(solution)/shard_map/ppermute | solution.py:12
  286.5 102.0 %copy-start.15 = (bf16[128,5120]{1,0:T(8,128)(2,1)}, bf16[128,5120]{1,0:T(8,128)(2,1)S(1)}, u32[]{:S(2)}) copy-start(bf16[128,5120]{1,0:T(8,128)(2,1)S(1)} %collective-permute-done.1) | copy-start | bytes 3932164
  391.6 31.0 %collective-permute-start.2 = (bf16[128,5120]{1,0:T(8,128)(2,1)}, bf16[128,5120]{1,0:T(8,128)(2,1)S(1)}, u32[]{:S(2)}, u32[]{:S(2)}) collective-permute-start(bf16[128,5120]{1,0:T(8,128)(2,1)} %fusion.37), channel_id=1, source_target_pairs={{0,8},{8,16},{16,24},{1,9},{9,17},{17,25},{2,10},{10,18},{18,26},{... | collective-permute-start | bytes 3932168 | tf_op jit(solution)/shard_map/ppermute | solution.py:12
  403.5 27.2 %all-to-all-start.8 = ((bf16[32,8,1280]{2,1,0:T(8,128)(2,1)}), bf16[32,8,1280]{2,1,0:T(8,128)(2,1)}, u32[]{:S(2)}, u32[]{:S(2)}) async-start(bf16[32,8,1280]{2,1,0:T(8,128)(2,1)} %bitcast.302), calls=%async_computation.8 | async-start | bytes 1310720 | tf_op jit(solution)/shard_map/all_to_all | solution.py:27
  430.6 17.8 %all-to-all-start.6 = ((bf16[32,8,1280]{2,1,0:T(8,128)(2,1)}), bf16[32,8,1280]{2,1,0:T(8,128)(2,1)S(1)}, u32[]{:S(2)}, u32[]{:S(2)}) async-start(bf16[32,8,1280]{2,1,0:T(8,128)(2,1)} %bitcast.38), calls=%async_computation.6 | async-start | bytes 1310720 | tf_op jit(solution)/shard_map/all_to_all | solution.py:27
  435.6 61.8 %all-reduce.18.cloned.1.call-start = ((), (), s32[]{:S(2)}) async-start(), calls=%async_computation.19 | async-start | bytes 2359296 | tf_op jit(solution)/shard_map/psum | solution.py:77
  451.8 45.7 %copy-start.48 = (bf16[256,768]{1,0:T(8,128)(2,1)S(1)}, bf16[256,768]{1,0:T(8,128)(2,1)}, u32[]{:S(2)}) copy-start(bf16[256,768]{1,0:T(8,128)(2,1)} %get-tuple-element.12) | copy-start | bytes 1179652
  451.8 45.7 %copy-start.49 = (bf16[256,768]{1,0:T(8,128)(2,1)S(1)}, bf16[256,768]{1,0:T(8,128)(2,1)}, u32[]{:S(2)}) copy-start(bf16[256,768]{1,0:T(8,128)(2,1)} %get-tuple-element.13) | copy-start | bytes 1179652
  453.2 172.5 %all-reduce.12.cloned.1.call-start = ((), (), s32[]{:S(2)}) async-start(), calls=%async_computation.16 | async-start | bytes 786432 | tf_op jit(solution)/shard_map/psum | solution.py:133
  503.0 22.2 %copy-start.14 = (bf16[128,5120]{1,0:T(8,128)(2,1)S(1)}, bf16[128,5120]{1,0:T(8,128)(2,1)}, u32[]{:S(2)}) copy-start(bf16[128,5120]{1,0:T(8,128)(2,1)} %copy-done.13) | copy-start | bytes 3932164
  503.0 22.2 %copy-start.16 = (bf16[128,5120]{1,0:T(8,128)(2,1)S(1)}, bf16[128,5120]{1,0:T(8,128)(2,1)}, u32[]{:S(2)}) copy-start(bf16[128,5120]{1,0:T(8,128)(2,1)} %copy-done.15) | copy-start | bytes 3932164
  528.4 31.8 %collective-permute-start.3 = (bf16[128,5120]{1,0:T(8,128)(2,1)S(1)}, bf16[128,5120]{1,0:T(8,128)(2,1)}, u32[]{:S(2)}, u32[]{:S(2)}) collective-permute-start(bf16[128,5120]{1,0:T(8,128)(2,1)S(1)} %fusion.50), channel_id=1, source_target_pairs={{8,0},{16,8},{24,16},{9,1},{17,9},{25,17},{10,2},{18,10},{26,18},{... | collective-permute-start | bytes 3932168 | tf_op jit(solution)/shard_map/ppermute | solution.py:12
  656.9 32.1 %collective-permute-start.4 = (bf16[128,5120]{1,0:T(8,128)(2,1)}, bf16[128,5120]{1,0:T(8,128)(2,1)}, u32[]{:S(2)}, u32[]{:S(2)}) collective-permute-start(bf16[128,5120]{1,0:T(8,128)(2,1)} %fusion.54), channel_id=1, source_target_pairs={{8,0},{16,8},{24,16},{9,1},{17,9},{25,17},{10,2},{18,10},{26,18},{... | collective-permute-start | bytes 3932168 | tf_op jit(solution)/shard_map/ppermute | solution.py:12
  660.9 36.2 %all-to-all-start.7 = ((bf16[32,8,1280]{2,1,0:T(8,128)(2,1)}), bf16[32,8,1280]{2,1,0:T(8,128)(2,1)}, u32[]{:S(2)}, u32[]{:S(2)}) async-start(bf16[32,8,1280]{2,1,0:T(8,128)(2,1)} %fusion.78), calls=%async_computation.7 | async-start | bytes 1310720 | tf_op jit(solution)/shard_map/all_to_all | solution.py:27
  697.2 19.0 %all-to-all-start.12 = ((bf16[32,8,1280]{2,1,0:T(8,128)(2,1)}), bf16[32,8,1280]{2,1,0:T(8,128)(2,1)}, u32[]{:S(2)}, u32[]{:S(2)}) async-start(bf16[32,8,1280]{2,1,0:T(8,128)(2,1)} %bitcast.303), calls=%async_computation.12 | async-start | bytes 1310720 | tf_op jit(solution)/shard_map/all_to_all | solution.py:27
  702.7 57.7 %all-reduce.14.cloned.1.call-start = ((), (), s32[]{:S(2)}) async-start(), calls=%async_computation.17 | async-start | bytes 786432 | tf_op jit(solution)/shard_map/psum | solution.py:133
  766.7 22.0 %all-to-all-start.13 = ((bf16[32,8,1280]{2,1,0:T(8,128)(2,1)}), bf16[32,8,1280]{2,1,0:T(8,128)(2,1)}, u32[]{:S(2)}, u32[]{:S(2)}) async-start(bf16[32,8,1280]{2,1,0:T(8,128)(2,1)} %fusion.72), calls=%async_computation.13 | async-start | bytes 1310720 | tf_op jit(solution)/shard_map/all_to_all | solution.py:27
  792.9 32.1 %collective-permute-start.5 = (bf16[128,5120]{1,0:T(8,128)(2,1)S(1)}, bf16[128,5120]{1,0:T(8,128)(2,1)}, u32[]{:S(2)}, u32[]{:S(2)}) collective-permute-start(bf16[128,5120]{1,0:T(8,128)(2,1)S(1)} %fusion.58), channel_id=1, source_target_pairs={{8,0},{16,8},{24,16},{9,1},{17,9},{25,17},{10,2},{18,10},{26,18},{... | collective-permute-start | bytes 3932168 | tf_op jit(solution)/shard_map/ppermute | solution.py:12
  833.3 18.5 %all-to-all-start.14 = ((bf16[32,8,1280]{2,1,0:T(8,128)(2,1)}), bf16[32,8,1280]{2,1,0:T(8,128)(2,1)}, u32[]{:S(2)}, u32[]{:S(2)}) async-start(bf16[32,8,1280]{2,1,0:T(8,128)(2,1)} %bitcast.304), calls=%async_computation.14 | async-start | bytes 1310720 | tf_op jit(solution)/shard_map/all_to_all | solution.py:27
  838.8 53.5 %all-reduce.16.cloned.1.call-start = ((), (), s32[]{:S(2)}) async-start(), calls=%async_computation.18 | async-start | bytes 786432 | tf_op jit(solution)/shard_map/psum | solution.py:133
  898.6 22.3 %all-to-all-start.15 = ((bf16[32,8,1280]{2,1,0:T(8,128)(2,1)}), bf16[32,8,1280]{2,1,0:T(8,128)(2,1)}, u32[]{:S(2)}, u32[]{:S(2)}) async-start(bf16[32,8,1280]{2,1,0:T(8,128)(2,1)} %fusion.71), calls=%async_computation.15 | async-start | bytes 1310720 | tf_op jit(solution)/shard_map/all_to_all | solution.py:27
  (59 other events, 226.6 us)
Sparse Core Ops, SparseCore 0:
  44.1 40.5 all-reduce.23
  180.2 41.4 all-reduce.21
  314.9 41.4 all-reduce.19
  453.4 44.0 all-reduce.17
  587.7 37.9 all-reduce.11
  718.9 41.5 all-reduce.13
  854.5 37.7 all-reduce.15
where the time goes:
time: 946 us; the launch traced here: 935 us
  waiting for transfers between devices  464 us (49%)
  blocking collectives  161 us (17%)
  matrix products  121 us (13%)
  starting transfers between devices  68.5 us (7%)
  local copies, waits for them, and re-layouts  57.2 us (6%)
  other arithmetic  47.1 us (5%)
  between operations  15.4 us (2%)
    psum x4, waiting for transfers between devices, local(): lax.psum(up_part.astype(jnp.bfloat16), 'dp').astype(jnp.float32)  168 us
    all_to_all x8, blocking collectives, deliver(): lax.all_to_all(flat_buffer, ('dp', 'expert'), split_axis=0, concat_axis=0...  161 us
    ppermute x6, waiting for transfers between devices, from_behind(): lax.ppermute(value, axis, [(source, source + steps) for source in range(l...  145 us
    psum x3, waiting for transfers between devices, local(): lax.psum(hidden_part.astype(jnp.bfloat16), 'dp').astype(jnp.float32)  107 us
    all_to_all x8, starting transfers between devices, deliver(): lax.all_to_all(flat_buffer, ('dp', 'expert'), split_axis=0, concat_axis=0...  53.3 us
    all_to_all x8, waiting for transfers between devices, deliver(): lax.all_to_all(flat_buffer, ('dp', 'expert'), split_axis=0, concat_axis=0...  44.9 us
    dot_general x4, matrix products, local(): jnp.einsum('tpc,qpcd->tpqd', dispatch, forward_returned, preferred_elemen...  23.6 us
  transfers between devices with their start and end apart: 21, of which 18 were waited for; matrix products, arithmetic and copies ran while one was open for 8% of the time, Pallas kernels for 0%

commit v1 on v0

v1 whole, which is shorter than its diff:
```python
import jax
import jax.numpy as jnp
from jax import lax
from jax.experimental import pallas as pl
from jax.experimental.pallas import tpu as pltpu
from jax.sharding import PartitionSpec as P

CAP = 8
EPS = 1e-06
BF = jnp.bfloat16
F32 = jnp.float32


def ring(value, axis, steps):
    count = lax.axis_size(axis)
    return lax.ppermute(value, axis, [(i, (i + steps) % count) for i in range(count)])


def hop(value, steps):
    count = lax.axis_size("section")
    pairs = [(i, i + steps) for i in range(count) if 0 <= i + steps < count]
    return lax.ppermute(value, "section", pairs)


def hop_back(value, steps, k):
    sections, experts = lax.axis_size("section"), lax.axis_size("expert")
    pairs = [
        (s * experts + e, (s + steps) * experts + (e - k) % experts)
        for s in range(sections)
        if 0 <= s + steps < sections
        for e in range(experts)
    ]
    return lax.ppermute(value, ("section", "expert"), pairs)


def mm(a, b, ca=1, cb=0):
    return lax.dot_general(a, b, (((ca,), (cb,)), ((), ())), preferred_element_type=F32)


def split(x):
    hi = lax.reduce_precision(x, 8, 7)
    mid = lax.reduce_precision(x - hi, 8, 7)
    low = x - hi - mid
    return [hi.astype(BF), mid.astype(BF), low.astype(BF)]


def from_lanes(x, at):
    return sum(x[:, at + i : at + i + 1].astype(F32) for i in range(3))


TILE = 256


def nt(a, b):
    return lax.dot_general(a, b, (((1,), (1,)), ((), ())), preferred_element_type=F32)


def tiles(extent):
    return [(i, min(TILE, extent - i)) for i in range(0, extent, TILE)]


def lane_pack(x):
    hi = x.astype(BF).astype(F32)
    mid = (x - hi).astype(BF).astype(F32)
    low = x - hi - mid
    lane = lax.broadcasted_iota(jnp.int32, (x.shape[0], 128), 1)
    return jnp.where(lane == 0, hi, jnp.where(lane == 1, mid, jnp.where(lane == 2, low, 0.0)))


def lane_sum(x):
    lane = lax.broadcasted_iota(jnp.int32, x.shape, 1)
    return jnp.sum(jnp.where(lane < 3, x.astype(F32), 0.0), axis=1, keepdims=True)


def regroup(refs, at, size, groups):
    loaded = [ref[:, at : at + size].astype(F32) for ref in refs]
    return [jnp.concatenate([x[j * CAP : (j + 1) * CAP] for x in loaded], axis=0) for j in range(groups)]


def put_blocks(value, refs, at, size, groups):
    experts = len(refs)
    own = experts * CAP
    for k, ref in enumerate(refs):
        rows = [value[j * own + k * CAP : j * own + (k + 1) * CAP] for j in range(groups)]
        ref[:, at : at + size] = jnp.concatenate(rows, axis=0).astype(BF)


def call(kernel, ins, outs, scratch=(), flops=0):
    moved = sum(x.size * x.dtype.itemsize for x in ins) + sum(o.size * o.dtype.itemsize for o in outs)
    return pl.pallas_call(
        kernel,
        out_shape=tuple(outs),
        in_specs=[pl.BlockSpec(memory_space=pltpu.VMEM)] * len(ins),
        out_specs=tuple(pl.BlockSpec(memory_space=pltpu.VMEM) for _ in outs),
        scratch_shapes=list(scratch),
        cost_estimate=pl.CostEstimate(flops=flops, bytes_accessed=moved, transcendentals=0),
    )(*ins)


def shape(dtype, *dims):
    return jax.ShapeDtypeStruct(dims, dtype)


def owner(state, back, tables, send_table, scale, experts):
    count, width = state.shape
    slots = send_table.shape[0]
    block = slots // experts

    def kernel(*refs):
        state_ref, refs = refs[0], refs[1:]
        back_refs, refs = refs[: len(back)], refs[len(back) :]
        table_refs, refs = refs[: len(tables)], refs[len(tables) :]
        send_ref, refs = refs[0], refs[1:]
        if scale is not None:
            scale_ref, refs = refs[0], refs[1:]
        new_ref, out_refs = refs[0], refs[1:]
        for at, size in tiles(width):
            rows = jnp.concatenate([ref[:, at : at + size] for ref in back_refs], axis=0)
            total = state_ref[:, at : at + size].astype(F32)
            for table_ref in table_refs:
                total = total + mm(table_ref[...], rows)
            new = total.astype(BF)
            new_ref[:, at : at + size] = new
            picked = mm(send_ref[...], new)
            if scale is not None:
                picked = picked * scale_ref[...]
            picked = picked.astype(BF)
            for k in range(experts):
                out_refs[k][:, at : at + size] = picked[k * block : (k + 1) * block]

    ins = [state, *back, *tables, send_table] + ([] if scale is None else [scale])
    outs = [shape(BF, count, width)] + [shape(BF, block, width)] * experts
    res = call(kernel, ins, outs, flops=2 * count * slots * width * (1 + len(tables)))
    return res[0], res[1:]


def forward_in(blocks, gain, gate_w, up_w, groups):
    experts = len(blocks)
    block, width = blocks[0].shape
    own, slots = experts * CAP, experts * block
    hidden = gate_w.shape[1]

    def kernel(*refs):
        block_refs, refs = refs[:experts], refs[experts:]
        gain_ref, gate_ref, up_ref, slot_ref, own_ref = refs[:5]
        part_refs, scaled_ref = refs[5:-1], refs[-1]
        squares = [jnp.zeros((own, 1), F32) for _ in range(groups)]
        for at, size in tiles(width):
            for j, x in enumerate(regroup(block_refs, at, size, groups)):
                slot_ref[j * own : (j + 1) * own, at : at + size] = x.astype(BF)
                scaled_ref[j * own : (j + 1) * own, at : at + size] = (x * gain_ref[:, at : at + size]).astype(BF)
                squares[j] = squares[j] + jnp.sum(x * x, axis=1, keepdims=True)
        for base, w_ref in ((0, gate_ref), (hidden, up_ref)):
            for at, size in tiles(hidden):
                part = mm(scaled_ref[...], w_ref[:, at : at + size])
                own_ref[:, base + at : base + at + size] = part[:own]
                for j in range(1, groups):
                    part_refs[j - 1][:, base + at : base + at + size] = part[j * own : (j + 1) * own].astype(BF)
        own_ref[:, 2 * hidden :] = lane_pack(squares[0])
        for j in range(1, groups):
            part_refs[j - 1][:, 2 * hidden :] = lane_pack(squares[j]).astype(BF)

    outs = [shape(BF, slots, width), shape(F32, own, 2 * hidden + 128)]
    outs += [shape(BF, own, 2 * hidden + 128)] * (groups - 1)
    res = call(
        kernel,
        [*blocks, gain, gate_w, up_w],
        outs,
        [pltpu.VMEM((slots, width), BF)],
        flops=4 * slots * width * hidden,
    )
    return res[0], res[1], res[2:]


def forward_act(first, parts, model):
    own, span = first.shape
    hidden = (span - 128) // 2

    def kernel(*refs):
        first_ref = refs[0]
        part_refs = refs[1 : 1 + len(parts)]
        pay_ref, gate_ref, up_ref = refs[1 + len(parts) :]
        square = lane_sum(first_ref[:, 2 * hidden :])
        for ref in part_refs:
            square = square + lane_sum(ref[:, 2 * hidden :])
        inv = lax.rsqrt(square / model + EPS)
        for at, size in tiles(hidden):
            gate = first_ref[:, at : at + size]
            up = first_ref[:, hidden + at : hidden + at + size]
            for ref in part_refs:
                gate = gate + ref[:, at : at + size].astype(F32)
                up = up + ref[:, hidden + at : hidden + at + size].astype(F32)
            gate, up = inv * gate, inv * up
            gate_ref[:, at : at + size] = gate
            up_ref[:, at : at + size] = up
            pay_ref[:, at : at + size] = (gate * jax.nn.sigmoid(gate) * up).astype(BF)
        pay_ref[:, hidden:] = lane_pack(inv).astype(BF)

    outs = [shape(BF, own, hidden + 128), shape(F32, own, hidden), shape(F32, own, hidden)]
    return call(kernel, [first, *parts], outs)


def forward_out(gathered, down_w, experts):
    groups = len(gathered)
    own, span = gathered[0].shape
    hidden, width = down_w.shape
    slots = groups * own

    def kernel(*refs):
        gathered_refs, refs = refs[:groups], refs[groups:]
        down_ref, all_ref, out_ref = refs[:3]
        block_refs = refs[3:]
        for j, ref in enumerate(gathered_refs):
            all_ref[j * own : (j + 1) * own, :] = ref[...]
        for at, size in tiles(width):
            part = mm(all_ref[:, :hidden], down_ref[:, at : at + size])
            out_ref[:, at : at + size] = part.astype(BF)
            put_blocks(part, block_refs, at, size, groups)

    outs = [shape(BF, slots, span), shape(BF, slots, width)] + [shape(BF, groups * CAP, width)] * experts
    res = call(kernel, [*gathered, down_w], outs, flops=2 * slots * hidden * width)
    return res[0], res[1], res[2:]


def backward_in(blocks, down_w, groups):
    experts = len(blocks)
    block, width = blocks[0].shape
    own, slots = experts * CAP, experts * block
    hidden = down_w.shape[0]

    def kernel(*refs):
        block_refs, refs = refs[:experts], refs[experts:]
        down_ref, grad_ref, own_ref = refs[:3]
        part_refs = refs[3:]
        for at, size in tiles(width):
            for j, x in enumerate(regroup(block_refs, at, size, groups)):
                grad_ref[j * own : (j + 1) * own, at : at + size] = x.astype(BF)
        for at, size in tiles(hidden):
            part = nt(grad_ref[...], down_ref[at : at + size, :])
            own_ref[:, at : at + size] = part[:own]
            for j in range(1, groups):
                part_refs[j - 1][:, at : at + size] = part[j * own : (j + 1) * own].astype(BF)

    outs = [shape(BF, slots, width), shape(F32, own, hidden)] + [shape(BF, own, hidden)] * (groups - 1)
    res = call(kernel, [*blocks, down_w], outs, flops=2 * slots * width * hidden)
    return res[0], res[1], res[2:]


def backward_act(first, parts, gate_pre, up_pre):
    own, hidden = first.shape

    def kernel(*refs):
        first_ref = refs[0]
        part_refs = refs[1 : 1 + len(parts)]
        gate_ref, up_ref, pay_ref = refs[1 + len(parts) :]
        inner = jnp.zeros((own, 1), F32)
        for at, size in tiles(hidden):
            hid = first_ref[:, at : at + size]
            for ref in part_refs:
                hid = hid + ref[:, at : at + size].astype(F32)
            gate, up = gate_ref[:, at : at + size], up_ref[:, at : at + size]
            sig = jax.nn.sigmoid(gate)
            gate_grad = (hid * up * sig * (1.0 + gate * (1.0 - sig))).astype(BF)
            up_grad = (hid * gate * sig).astype(BF)
            pay_ref[:, at : at + size] = gate_grad
            pay_ref[:, hidden + at : hidden + at + size] = up_grad
            both = gate_grad.astype(F32) * gate + up_grad.astype(F32) * up
            inner = inner + jnp.sum(both, axis=1, keepdims=True)
        pay_ref[:, 2 * hidden :] = lane_pack(inner).astype(BF)

    outs = [shape(BF, own, 2 * hidden + 128)]
    return call(kernel, [first, *parts, gate_pre, up_pre], outs)[0]


def backward_out(gathered, kept, slot, gain, gate_w, up_w, experts, model):
    groups = len(gathered)
    own, span = gathered[0].shape
    width, hidden = gate_w.shape
    slots = groups * own

    def kernel(*refs):
        gathered_refs, refs = refs[:groups], refs[groups:]
        kept_ref, slot_ref, gain_ref, gate_ref, up_ref, all_ref, given_ref = refs[:7]
        block_refs = refs[7:]
        for j, ref in enumerate(gathered_refs):
            all_ref[j * own : (j + 1) * own, :] = ref[...]
        inv = lane_sum(kept_ref[:, hidden:])
        lean = lane_sum(all_ref[:, 2 * hidden :]) * inv * inv / model
        for at, size in tiles(width):
            part = nt(all_ref[:, :hidden], gate_ref[at : at + size, :])
            part = part + nt(all_ref[:, hidden : 2 * hidden], up_ref[at : at + size, :])
            given = inv * gain_ref[:, at : at + size] * part - slot_ref[:, at : at + size].astype(F32) * lean
            given_ref[:, at : at + size] = given.astype(BF)
            put_blocks(given, block_refs, at, size, groups)

    outs = [shape(BF, slots, span), shape(BF, slots, width)] + [shape(BF, groups * CAP, width)] * experts
    res = call(
        kernel, [*gathered, kept, slot, gain, gate_w, up_w], outs, flops=4 * slots * hidden * width
    )
    return res[0], res[1], res[2:]


def local(tokens, cotangent, norm_gain, route_gates, expert_ids, expert_map, w_gate, w_up, w_down):
    section = lax.axis_index("section")
    d = lax.axis_index("dp")
    me = lax.axis_index("expert")
    sections, groups, experts = lax.axis_size("section"), lax.axis_size("dp"), lax.axis_size("expert")
    gate_w, up_w, down_w = w_gate[0, 0], w_up[0, 0], w_down[0, 0]
    rows, model = tokens.shape
    width, hidden = gate_w.shape
    own = experts * CAP
    slots = groups * own
    block = groups * CAP
    gain = lax.dynamic_slice(norm_gain, (0, d * width), (1, width))

    matches = expert_ids[0][:, :, None] == expert_map[0][None, None, :]
    chosen = jnp.any(matches, axis=1)
    weight = jnp.sum(jnp.where(matches, route_gates[0][:, :, None], 0.0), axis=1)
    lower = lax.broadcasted_iota(jnp.int32, (rows, rows), 0) > lax.broadcasted_iota(jnp.int32, (rows, rows), 1)
    before = mm(lower.astype(BF), chosen.astype(BF))
    code = jnp.where(chosen, before, -1.0)
    turn = (
        lax.broadcasted_iota(jnp.int32, (experts, experts), 0)
        == (lax.broadcasted_iota(jnp.int32, (experts, experts), 1) + me) % experts
    )
    pick = lambda x: jnp.sum(jnp.where(turn[None], x[:, :, None], 0.0), axis=1)
    mine = jnp.concatenate([pick(code), pick(weight)], axis=1)
    all_groups = [mine] + [None] * (groups - 1)
    for j in range(1, groups):
        all_groups[groups - j] = ring(mine, "dp", j)
    here = jnp.concatenate(all_groups, axis=0)
    behind = hop(here, 1)
    ahead = hop(here, -1)

    def spread(table, per, count):
        total = table.shape[0]
        col = lax.broadcasted_iota(jnp.int32, (experts, count), 1)
        wide = (col // per == lax.broadcasted_iota(jnp.int32, (experts, count), 0)).astype(BF)
        codes = table[:, :experts].astype(BF)
        weights = split(table[:, experts:])
        slot_col = lax.broadcasted_iota(jnp.int32, (total, count), 1)
        tok_row = lax.broadcasted_iota(jnp.int32, (total, count), 0)
        hit_back = (mm(codes, wide) == (slot_col % CAP).astype(F32)) & ((slot_col // CAP) % (per // CAP) == tok_row // rows)
        slot_row = lax.broadcasted_iota(jnp.int32, (count, total), 0)
        tok_col = lax.broadcasted_iota(jnp.int32, (count, total), 1)
        hit_out = (mm(wide, codes, 0, 1) == (slot_row % CAP).astype(F32)) & ((slot_row // CAP) % (per // CAP) == tok_col // rows)

        def weighted():
            return [jnp.where(hit_back, mm(w, wide), 0.0).astype(BF) for w in weights[:2]]

        def slot_weight():
            full = sum(mm(wide, w, 0, 1) for w in weights)
            return jnp.sum(jnp.where(hit_out, full, 0.0), axis=1, keepdims=True)

        return hit_out, hit_back, weighted, slot_weight

    hit_out, hit_back, own_weighted, own_slot_weight = spread(mine, CAP, own)
    own_out, own_back = hit_out.astype(BF), hit_back.astype(BF)
    own_w = own_weighted()
    own_r = own_slot_weight()
    hit_out, _, _, here_slot_weight = spread(here, block, slots)
    send_table = hit_out.astype(BF)
    send_r = here_slot_weight()
    _, _, behind_weighted, _ = spread(behind, block, slots)
    behind_w = behind_weighted()
    _, hit_back, _, _ = spread(ahead, block, slots)
    ahead_t = hit_back.astype(BF)

    def cut(value, j):
        return lax.dynamic_slice_in_dim(value, ((d + j) % groups) * width, width, axis=1)

    def to_slices(value):
        out = [cut(value, 0)] + [None] * (groups - 1)
        for j in range(1, groups):
            out[groups - j] = ring(cut(value, j), "dp", j)
        return out

    def to_rows(parts):
        return [parts[0]] + [ring(parts[j], "dp", j) for j in range(1, groups)]

    def absolute(parts):
        stacked = jnp.stack(parts)
        return jnp.concatenate(
            [lax.dynamic_index_in_dim(stacked, (d - b) % groups, 0, keepdims=False) for b in range(groups)], axis=1
        )

    def by_expert(value):
        shaped = value.reshape(groups, experts, CAP, value.shape[-1])
        return [shaped[:, k].reshape(block, value.shape[-1]) for k in range(experts)]

    def to_experts(blocks):
        return [blocks[0]] + [ring(blocks[k], "expert", k) for k in range(1, experts)]

    def first_rows(value, scale):
        picked = mm(own_out, value)
        picked = picked.astype(BF) if scale is None else (scale * picked).astype(BF)
        return to_experts(by_expert(jnp.concatenate(to_slices(picked), axis=0)))

    def reduce_groups(parts):
        return [ring(part, "dp", j + 1) for j, part in enumerate(parts)]

    def gather_groups(value):
        out = [value] + [None] * (groups - 1)
        for j in range(1, groups):
            out[groups - j] = ring(value, "dp", j)
        return out

    def keep(at, latest, earlier):
        if earlier is None:
            return latest
        return jax.tree.map(lambda a, b: jnp.where(section == at, a, b), latest, earlier)

    def finish(state, moved, tables):
        base = to_rows([state[j * rows : (j + 1) * rows] for j in range(groups)])
        parts = jnp.concatenate(to_rows([moved[j * own : (j + 1) * own] for j in range(groups)]), axis=1)
        blocks = [parts[k * CAP : (k + 1) * CAP] for k in range(experts)]
        back = jnp.concatenate([blocks[0]] + [ring(blocks[k], "expert", -k) for k in range(1, experts)], axis=0)
        added = sum(mm(t, back) for t in tables)
        return absolute(
            [(base[j].astype(F32) + added[:, j * width : (j + 1) * width]).astype(BF) for j in range(groups)]
        )

    received = first_rows(tokens, None)
    state = jnp.concatenate(to_slices(tokens), axis=0)
    early = first_rows(cotangent, own_r)
    incoming = jnp.concatenate(to_slices(cotangent), axis=0)

    saved, base, back = None, None, None
    for step in range(sections):
        if step:
            state, picked = owner(base, back, behind_w, send_table, None, experts)
            received = to_experts(picked)
        if step + 1 < sections:
            base = state if step == 0 else hop(state, 1)
        slot, first, parts = forward_in(received, gain, gate_w, up_w, groups)
        parts = reduce_groups(parts)
        payload, gate_pre, up_pre = forward_act(first, parts, model)
        gathered = gather_groups(payload)
        kept, out, blocks = forward_out(gathered, down_w, experts)
        if step + 1 < sections:
            back = [hop_back(blocks[k], 1, k) for k in range(experts)]
        saved = keep(step, (slot, gate_pre, up_pre, kept, out, state), saved)

    slot, gate_pre, up_pre, kept, out, state = saved
    layer_result = finish(state, out, own_w)

    final = None
    base, state = incoming, incoming
    for step in range(sections):
        at = sections - 1 - step
        if step == 0:
            received = early
        else:
            state, picked = owner(base, back, [ahead_t], send_table, send_r, experts)
            received = to_experts(picked)
            if step + 1 < sections:
                base = hop(state, -1)
        grad, first, parts = backward_in(received, down_w, groups)
        parts = reduce_groups(parts)
        payload = backward_act(first, parts, gate_pre, up_pre)
        gathered = gather_groups(payload)
        grads, given, blocks = backward_out(gathered, kept, slot, gain, gate_w, up_w, experts, model)
        if step + 1 < sections:
            back = [hop_back(blocks[k], -1, k) for k in range(experts)]
        final = keep(at, (grad, grads, given, state), final)

    grad, grads, given, state = final
    grad_in = finish(state, given, [own_back])
    inv_all = from_lanes(kept, hidden)
    normed = (slot.astype(F32) * inv_all * gain).astype(BF)
    down_grad = mm(kept[:, :hidden], grad, 0, 0).astype(BF)
    gate_wgrad = mm(normed, grads[:, :hidden], 0, 0).astype(BF)
    up_wgrad = mm(normed, grads[:, hidden : 2 * hidden], 0, 0).astype(BF)
    return (
        layer_result[None],
        grad_in[None],
        gate_wgrad[None, None],
        up_wgrad[None, None],
        down_grad[None, None],
    )


def solution(mesh):
    return jax.shard_map(
        local,
        mesh=mesh,
        in_specs=(
            P(("dp", "expert"), None),
            P(("dp", "expert"), None),
            P("section", None),
            P("section", ("dp", "expert"), None),
            P("section", ("dp", "expert"), None),
            P("section", None),
            P("section", "expert", "dp", None),
            P("section", "expert", "dp", None),
            P("section", "expert", None, "dp"),
        ),
        out_specs=(
            P("section", ("dp", "expert"), None),
            P("section", ("dp", "expert"), None),
            P("section", "expert", "dp", None),
            P("section", "expert", "dp", None),
            P("section", "expert", None, "dp"),
        ),
        check_vma=False,
    )
```

time: 946 us -> 691 us (0.73)
  the two profiles are of different devices: /device:TPU:1 before, /device:TPU:16 now
where the time goes in v1:
time: 691 us; the launch traced here: 679 us
  starting transfers between devices  305 us (44%)
  waiting for transfers between devices  178 us (26%)
  Pallas kernels  111 us (16%)
  local copies, waits for them, and re-layouts  36.1 us (5%)
  other arithmetic  23.2 us (3%)
  matrix products  22.5 us (3%)
    ppermute x145, starting transfers between devices, ring(): lax.ppermute(value, axis, [(i, (i + steps) % count) for i in range(count)])  186 us
    ppermute x145, waiting for transfers between devices, ring(): lax.ppermute(value, axis, [(i, (i + steps) % count) for i in range(count)])  131 us
    pallas_call x30, Pallas kernels, call(): pl.pallas_call(kernel, out_shape=tuple(outs), in_specs=[pl.BlockSpec(memo...  111 us
    ppermute x48, starting transfers between devices, hop_back(): return lax.ppermute(value, ('section', 'expert'), pairs)  104 us
    ppermute x48, waiting for transfers between devices, hop_back(): return lax.ppermute(value, ('section', 'expert'), pairs)  46.5 us
    unnamed x464, local copies, waits for them, and re-layouts  26.6 us
    dot_general x22, matrix products, mm(): lax.dot_general(a, b, (((ca,), (cb,)), ((), ())), preferred_element_type=...  22.5 us
    ppermute x6, starting transfers between devices, hop(): return lax.ppermute(value, 'section', pairs)  15.2 us
  transfers between devices with their start and end apart: 199, of which 68 were waited for; matrix products, arithmetic and copies ran while one was open for 8% of the time, Pallas kernels for 14%

profile of v1, /device:TPU:16, one launch (start us, length us, event | category | flops | bytes accessed | tf_op | source)
XLA Modules:
  0.0 679.2 jit_solution(16176475515131076283)
XLA Ops:
  16.5 5.3 collective-permute-done.5
  38.3 4.5 shard_map.128
  52.4 4.9 collective-permute-done.14.refs_2_
  65.8 8.5 %collective-permute-done.16.refs_1_ = bf16[64,896]{1,0:T(8,128)(2,1)S(1)} collective-permute-done((bf16[64,896]{1,0:T(8,128)(2,1)}, bf16[64,896]{1,0:T(8,128)(2,1)S(1)}, u32[]{:S(2)}, u32[]{:S(2)}) %collective-permute-start.16) | collective-permute-done | bytes 114720 | tf_op jit(solution)/shard_map/ppermute | solution.py:16
  108.2 5.2 shard_map.131
  126.2 4.5 shard_map.132
  134.2 10.4 %collective-permute-done.39.refs_1_ = bf16[64,1664]{1,0:T(8,128)(2,1)S(1)} collective-permute-done((bf16[64,1664]{1,0:T(8,128)(2,1)}, bf16[64,1664]{1,0:T(8,128)(2,1)S(1)}, u32[]{:S(2)}, u32[]{:S(2)}) %collective-permute-start.39) | collective-permute-done | bytes 213024 | tf_op jit(solution)/shard_map/ppermute | solution.py:16
  152.4 4.0 collective-permute-done.42.refs_1_
  187.9 5.2 shard_map.135
  202.6 4.4 collective-permute-start.128
  207.1 4.5 shard_map.136
  221.2 4.2 collective-permute-done.62.refs_2_
  239.0 4.3 collective-permute-start.110
  281.2 5.2 shard_map.139
  301.9 4.6 shard_map.140
  312.9 7.1 %collective-permute-done.82.refs_1_ = bf16[64,1664]{1,0:T(8,128)(2,1)S(1)} collective-permute-done((bf16[64,1664]{1,0:T(8,128)(2,1)}, bf16[64,1664]{1,0:T(8,128)(2,1)S(1)}, u32[]{:S(2)}, u32[]{:S(2)}) %collective-permute-start.82) | collective-permute-done | bytes 213024 | tf_op jit(solution)/shard_map/ppermute | solution.py:16
  350.2 5.1 shard_map.145
  358.4 4.2 collective-permute-start.121
  383.6 3.8 shard_map.146
  421.8 8.2 %collective-permute-done.140.refs_1_ = bf16[64,1664]{1,0:T(8,128)(2,1)S(1)} collective-permute-done((bf16[64,1664]{1,0:T(8,128)(2,1)}, bf16[64,1664]{1,0:T(8,128)(2,1)S(1)}, u32[]{:S(2)}, u32[]{:S(2)}) %collective-permute-start.140) | collective-permute-done | bytes 213024 | tf_op jit(solution)/shard_map/ppermute | solution.py:16
  433.7 5.1 shard_map.149
  448.6 20.2 %collective-permute-done.143.refs_1_ = bf16[32,1280]{1,0:T(8,128)(2,1)S(1)} collective-permute-done((bf16[32,1280]{1,0:T(8,128)(2,1)}, bf16[32,1280]{1,0:T(8,128)(2,1)S(1)}, u32[]{:S(2)}, u32[]{:S(2)}) %collective-permute-start.143) | collective-permute-done | bytes 81952 | tf_op jit(solution)/shard_map/ppermute | solution.py:33
  468.8 5.9 collective-permute-start.147
  489.6 3.8 shard_map.150
  518.4 10.0 %collective-permute-done.159.refs_1_ = bf16[64,768]{1,0:T(8,128)(2,1)S(1)} collective-permute-done((bf16[64,768]{1,0:T(8,128)(2,1)}, bf16[64,768]{1,0:T(8,128)(2,1)S(1)}, u32[]{:S(2)}, u32[]{:S(2)}) %collective-permute-start.159) | collective-permute-done | bytes 98336 | tf_op jit(solution)/shard_map/ppermute | solution.py:16
  551.3 5.2 shard_map.153
  601.4 5.3 collective-permute-start.181
  620.1 11.1 %collective-permute-done.183.refs_1_ = bf16[64,1664]{1,0:T(8,128)(2,1)S(1)} collective-permute-done((bf16[64,1664]{1,0:T(8,128)(2,1)}, bf16[64,1664]{1,0:T(8,128)(2,1)S(1)}, u32[]{:S(2)}, u32[]{:S(2)}) %collective-permute-start.183) | collective-permute-done | bytes 213024 | tf_op jit(solution)/shard_map/ppermute | solution.py:16
  631.9 5.1 shard_map.157
  637.2 5.7 collective-permute-start.188
  664.2 5.0 collective-permute-done.192
  669.9 5.4 collective-permute-done.194
  (943 shorter events, 478.7 us)
Async XLA Ops:
  3.8 20.9 %collective-permute-start.29 = (f32[128,16]{0,1:T(8,128)S(1)}, f32[128,16]{0,1:T(8,128)S(1)}, u32[]{:S(2)}, u32[]{:S(2)}) collective-permute-start(f32[128,16]{0,1:T(8,128)S(1)} %pad_maximum_fusion.9), channel_id=1, source_target_pairs={{0,32},{32,64},{64,96},{96,0},{1,33},{33,65},{65,97},{97,1},{2,34}... | collective-permute-start | bytes 24584 | tf_op jit(solution)/shard_map/ppermute | solution.py:16
  5.8 21.2 %collective-permute-start.28 = (f32[128,16]{0,1:T(8,128)S(1)}, f32[128,16]{0,1:T(8,128)S(1)}, u32[]{:S(2)}, u32[]{:S(2)}) collective-permute-start(f32[128,16]{0,1:T(8,128)S(1)} %pad_maximum_fusion.9), channel_id=1, source_target_pairs={{0,64},{32,96},{64,0},{96,32},{1,65},{33,97},{65,1},{97,33},{2,66}... | collective-permute-start | bytes 24584 | tf_op jit(solution)/shard_map/ppermute | solution.py:16
  33.1 55.3 %collective-permute-start.2 = (bf16[128,1280]{1,0:T(8,128)(2,1)S(1)}, bf16[128,1280]{1,0:T(8,128)(2,1)S(1)}, u32[]{:S(2)}, u32[]{:S(2)}) collective-permute-start(bf16[128,1280]{1,0:T(8,128)(2,1)S(1)} %get-tuple-element.380), channel_id=1, source_target_pairs={{0,32},{32,64},{64,96},{96,0},{1,33},{33,65},{65,97},{97,1},{2,34}... | collective-permute-start | bytes 983048 | tf_op jit(solution)/shard_map/ppermute | solution.py:16
  34.4 29.0 %collective-permute-start.30 = (f32[512,16]{0,1:T(8,128)S(1)}, f32[512,16]{0,1:T(8,128)S(1)}, u32[]{:S(2)}, u32[]{:S(2)}) collective-permute-start(f32[512,16]{0,1:T(8,128)S(1)} %get-tuple-element.350), channel_id=1, source_target_pairs={{0,8},{8,16},{16,24},{1,9},{9,17},{17,25},{2,10},{10,18},{18,26},{... | collective-permute-start | bytes 98312 | tf_op jit(solution)/shard_map/ppermute | solution.py:22
  51.6 40.0 %collective-permute-start.1 = (bf16[128,1280]{1,0:T(8,128)(2,1)S(1)}, bf16[128,1280]{1,0:T(8,128)(2,1)S(1)}, u32[]{:S(2)}, u32[]{:S(2)}) collective-permute-start(bf16[128,1280]{1,0:T(8,128)(2,1)S(1)} %get-tuple-element.378), channel_id=1, source_target_pairs={{0,64},{32,96},{64,0},{96,32},{1,65},{33,97},{65,1},{97,33},{2,66}... | collective-permute-start | bytes 983048 | tf_op jit(solution)/shard_map/ppermute | solution.py:16
  57.3 36.2 %collective-permute-start = (bf16[128,1280]{1,0:T(8,128)(2,1)S(1)}, bf16[128,1280]{1,0:T(8,128)(2,1)S(1)}, u32[]{:S(2)}, u32[]{:S(2)}) collective-permute-start(bf16[128,1280]{1,0:T(8,128)(2,1)S(1)} %get-tuple-element.379), channel_id=1, source_target_pairs={{0,96},{32,0},{64,32},{96,64},{1,97},{33,1},{65,33},{97,65},{2,98}... | collective-permute-start | bytes 983048 | tf_op jit(solution)/shard_map/ppermute | solution.py:16
  122.6 65.3 %collective-permute-start.31 = (bf16[512,1280]{1,0:T(8,128)(2,1)}, bf16[512,1280]{1,0:T(8,128)(2,1)}, u32[]{:S(2)}, u32[]{:S(2)}) collective-permute-start(bf16[512,1280]{1,0:T(8,128)(2,1)} %get-tuple-element.188), channel_id=1, source_target_pairs={{0,8},{8,16},{16,24},{1,9},{9,17},{17,25},{2,10},{10,18},{18,26},{... | collective-permute-start | bytes 3932168 | tf_op jit(solution)/shard_map/ppermute | solution.py:22
  202.6 30.7 %collective-permute-start.128 = (bf16[512,16]{0,1:T(8,128)(2,1)}, bf16[512,16]{0,1:T(8,128)(2,1)}, u32[]{:S(2)}, u32[]{:S(2)}) collective-permute-start(bf16[512,16]{0,1:T(8,128)(2,1)} %get-tuple-element.349), channel_id=1, source_target_pairs={{8,0},{16,8},{24,16},{9,1},{17,9},{25,17},{10,2},{18,10},{26,18},{... | collective-permute-start | bytes 49160 | tf_op jit(solution)/shard_map/ppermute | solution.py:22
  212.8 21.8 %collective-permute-start.107 = (bf16[32,1280]{1,0:T(8,128)(2,1)}, bf16[32,1280]{1,0:T(8,128)(2,1)}, u32[]{:S(2)}, u32[]{:S(2)}) collective-permute-start(bf16[32,1280]{1,0:T(8,128)(2,1)} %get-tuple-element.399), channel_id=1, source_target_pairs={{0,1},{1,2},{2,3},{3,4},{4,5},{5,6},{6,7},{7,0},{8,9},{9,10},{10,1... | collective-permute-start | bytes 245768 | tf_op jit(solution)/shard_map/ppermute | solution.py:16
  214.5 66.0 %collective-permute-start.53 = (bf16[512,1280]{1,0:T(8,128)(2,1)}, bf16[512,1280]{1,0:T(8,128)(2,1)}, u32[]{:S(2)}, u32[]{:S(2)}) collective-permute-start(bf16[512,1280]{1,0:T(8,128)(2,1)} %get-tuple-element.210), channel_id=1, source_target_pairs={{0,8},{8,16},{16,24},{1,9},{9,17},{17,25},{2,10},{10,18},{18,26},{... | collective-permute-start | bytes 3932168 | tf_op jit(solution)/shard_map/ppermute | solution.py:22
  265.6 22.1 %collective-permute-start.103 = (bf16[128,1280]{1,0:T(8,128)(2,1)S(1)}, bf16[128,1280]{1,0:T(8,128)(2,1)S(1)}, u32[]{:S(2)}, u32[]{:S(2)}) collective-permute-start(bf16[128,1280]{1,0:T(8,128)(2,1)S(1)} %copy-done.38), channel_id=1, source_target_pairs={{0,32},{32,64},{64,96},{96,0},{1,33},{33,65},{65,97},{97,1},{2,34}... | collective-permute-start | bytes 983048 | tf_op jit(solution)/shard_map/ppermute | solution.py:16
  267.9 19.8 %collective-permute-start.102 = (bf16[128,1280]{1,0:T(8,128)(2,1)S(1)}, bf16[128,1280]{1,0:T(8,128)(2,1)S(1)}, u32[]{:S(2)}, u32[]{:S(2)}) collective-permute-start(bf16[128,1280]{1,0:T(8,128)(2,1)S(1)} %get-tuple-element.367), channel_id=1, source_target_pairs={{0,64},{32,96},{64,0},{96,32},{1,65},{33,97},{65,1},{97,33},{2,66}... | collective-permute-start | bytes 983048 | tf_op jit(solution)/shard_map/ppermute | solution.py:16
  298.6 30.2 %collective-permute-start.114 = (bf16[64,768]{1,0:T(8,128)(2,1)}, bf16[64,768]{1,0:T(8,128)(2,1)}, u32[]{:S(2)}, u32[]{:S(2)}) collective-permute-start(bf16[64,768]{1,0:T(8,128)(2,1)} %get-tuple-element.251), channel_id=1, source_target_pairs={{0,32},{32,64},{64,96},{96,0},{1,33},{33,65},{65,97},{97,1},{2,34}... | collective-permute-start | bytes 294920 | tf_op jit(solution)/shard_map/ppermute | solution.py:16
  298.8 31.1 %collective-permute-start.115 = (bf16[64,768]{1,0:T(8,128)(2,1)}, bf16[64,768]{1,0:T(8,128)(2,1)}, u32[]{:S(2)}, u32[]{:S(2)}) collective-permute-start(bf16[64,768]{1,0:T(8,128)(2,1)} %get-tuple-element.252), channel_id=1, source_target_pairs={{0,64},{32,96},{64,0},{96,32},{1,65},{33,97},{65,1},{97,33},{2,66}... | collective-permute-start | bytes 294920 | tf_op jit(solution)/shard_map/ppermute | solution.py:16
  347.0 20.2 %collective-permute-start.89 = (bf16[64,1280]{1,0:T(8,128)(2,1)}, bf16[64,1280]{1,0:T(8,128)(2,1)S(1)}, u32[]{:S(2)}, u32[]{:S(2)}) collective-permute-start(bf16[64,1280]{1,0:T(8,128)(2,1)} %get-tuple-element.415), channel_id=1, source_target_pairs={{0,64},{32,96},{64,0},{96,32},{1,65},{33,97},{65,1},{97,33},{2,66}... | collective-permute-start | bytes 491528 | tf_op jit(solution)/shard_map/ppermute | solution.py:16
  348.7 20.4 %collective-permute-start.88 = (bf16[64,1280]{1,0:T(8,128)(2,1)S(1)}, bf16[64,1280]{1,0:T(8,128)(2,1)S(1)}, u32[]{:S(2)}, u32[]{:S(2)}) collective-permute-start(bf16[64,1280]{1,0:T(8,128)(2,1)S(1)} %get-tuple-element.416), channel_id=1, source_target_pairs={{0,32},{32,64},{64,96},{96,0},{1,33},{33,65},{65,97},{97,1},{2,34}... | collective-permute-start | bytes 491528 | tf_op jit(solution)/shard_map/ppermute | solution.py:16
  390.0 19.6 %collective-permute-start.91 = (bf16[8,5120]{1,0:T(8,128)(2,1)S(1)}, bf16[8,5120]{1,0:T(8,128)(2,1)S(1)}, u32[]{:S(2)}, u32[]{:S(2)}) collective-permute-start(bf16[8,5120]{1,0:T(8,128)(2,1)S(1)} %get-tuple-element.411), channel_id=1, source_target_pairs={{0,7},{1,0},{2,1},{3,2},{4,3},{5,4},{6,5},{7,6},{8,15},{9,8},{10,9... | collective-permute-start | bytes 245768 | tf_op jit(solution)/shard_map/ppermute | solution.py:16
  397.9 23.9 %collective-permute-start.92 = (bf16[8,5120]{1,0:T(8,128)(2,1)S(1)}, bf16[8,5120]{1,0:T(8,128)(2,1)S(1)}, u32[]{:S(2)}, u32[]{:S(2)}) collective-permute-start(bf16[8,5120]{1,0:T(8,128)(2,1)S(1)} %get-tuple-element.410), channel_id=1, source_target_pairs={{0,6},{1,7},{2,0},{3,1},{4,2},{5,3},{6,4},{7,5},{8,14},{9,15},{10,... | collective-permute-start | bytes 245768 | tf_op jit(solution)/shard_map/ppermute | solution.py:16
  400.2 40.6 %collective-permute-start.93 = (bf16[8,5120]{1,0:T(8,128)(2,1)}, bf16[8,5120]{1,0:T(8,128)(2,1)}, u32[]{:S(2)}, u32[]{:S(2)}) collective-permute-start(bf16[8,5120]{1,0:T(8,128)(2,1)} %get-tuple-element.409), channel_id=1, source_target_pairs={{0,5},{1,6},{2,7},{3,0},{4,1},{5,2},{6,3},{7,4},{8,13},{9,14},{10,... | collective-permute-start | bytes 245768 | tf_op jit(solution)/shard_map/ppermute | solution.py:16
  410.9 33.8 %collective-permute-start.94 = (bf16[8,5120]{1,0:T(8,128)(2,1)}, bf16[8,5120]{1,0:T(8,128)(2,1)}, u32[]{:S(2)}, u32[]{:S(2)}) collective-permute-start(bf16[8,5120]{1,0:T(8,128)(2,1)} %get-tuple-element.408), channel_id=1, source_target_pairs={{0,4},{1,5},{2,6},{3,7},{4,0},{5,1},{6,2},{7,3},{8,12},{9,13},{10,... | collective-permute-start | bytes 245768 | tf_op jit(solution)/shard_map/ppermute | solution.py:16
  430.9 57.7 %collective-permute-start.129 = (bf16[512,1280]{1,0:T(8,128)(2,1)S(1)}, bf16[512,1280]{1,0:T(8,128)(2,1)S(1)}, u32[]{:S(2)}, u32[]{:S(2)}) collective-permute-start(bf16[512,1280]{1,0:T(8,128)(2,1)S(1)} %copy-done.19), channel_id=1, source_target_pairs={{8,0},{16,8},{24,16},{9,1},{17,9},{25,17},{10,2},{18,10},{26,18},{... | collective-permute-start | bytes 3932168 | tf_op jit(solution)/shard_map/ppermute | solution.py:22
  438.8 30.0 %collective-permute-start.143 = (bf16[32,1280]{1,0:T(8,128)(2,1)}, bf16[32,1280]{1,0:T(8,128)(2,1)S(1)}, u32[]{:S(2)}, u32[]{:S(2)}) collective-permute-start(bf16[32,1280]{1,0:T(8,128)(2,1)} %get-tuple-element.291), channel_id=1, source_target_pairs={{8,0},{9,1},{10,2},{11,3},{12,4},{13,5},{14,6},{15,7},{16,8},{17,9... | collective-permute-start | bytes 245768 | tf_op jit(solution)/shard_map/ppermute | solution.py:33
  441.7 34.0 %collective-permute-start.144 = (bf16[32,1280]{1,0:T(8,128)(2,1)}, bf16[32,1280]{1,0:T(8,128)(2,1)S(1)}, u32[]{:S(2)}, u32[]{:S(2)}) collective-permute-start(bf16[32,1280]{1,0:T(8,128)(2,1)} %get-tuple-element.292), channel_id=1, source_target_pairs={{8,7},{9,0},{10,1},{11,2},{12,3},{13,4},{14,5},{15,6},{16,15},{17,... | collective-permute-start | bytes 245768 | tf_op jit(solution)/shard_map/ppermute | solution.py:33
  444.7 31.2 %collective-permute-start.145 = (bf16[32,1280]{1,0:T(8,128)(2,1)}, bf16[32,1280]{1,0:T(8,128)(2,1)S(1)}, u32[]{:S(2)}, u32[]{:S(2)}) collective-permute-start(bf16[32,1280]{1,0:T(8,128)(2,1)} %get-tuple-element.293), channel_id=1, source_target_pairs={{8,6},{9,7},{10,0},{11,1},{12,2},{13,3},{14,4},{15,5},{16,14},{17,... | collective-permute-start | bytes 245768 | tf_op jit(solution)/shard_map/ppermute | solution.py:33
  446.6 31.2 %collective-permute-start.146 = (bf16[32,1280]{1,0:T(8,128)(2,1)}, bf16[32,1280]{1,0:T(8,128)(2,1)S(1)}, u32[]{:S(2)}, u32[]{:S(2)}) collective-permute-start(bf16[32,1280]{1,0:T(8,128)(2,1)} %get-tuple-element.294), channel_id=1, source_target_pairs={{8,5},{9,6},{10,7},{11,0},{12,1},{13,2},{14,3},{15,4},{16,13},{17,... | collective-permute-start | bytes 245768 | tf_op jit(solution)/shard_map/ppermute | solution.py:33
  503.7 35.7 %collective-permute-start.100 = (bf16[128,1280]{1,0:T(8,128)(2,1)}, bf16[128,1280]{1,0:T(8,128)(2,1)}, u32[]{:S(2)}, u32[]{:S(2)}) collective-permute-start(bf16[128,1280]{1,0:T(8,128)(2,1)} %get-tuple-element.375), channel_id=1, source_target_pairs={{0,96},{32,0},{64,32},{96,64},{1,97},{33,1},{65,33},{97,65},{2,98}... | collective-permute-start | bytes 983048 | tf_op jit(solution)/shard_map/ppermute | solution.py:16
  507.1 32.4 %collective-permute-start.99 = (bf16[128,1280]{1,0:T(8,128)(2,1)}, bf16[128,1280]{1,0:T(8,128)(2,1)}, u32[]{:S(2)}, u32[]{:S(2)}) collective-permute-start(bf16[128,1280]{1,0:T(8,128)(2,1)} %get-tuple-element.376), channel_id=1, source_target_pairs={{0,64},{32,96},{64,0},{96,32},{1,65},{33,97},{65,1},{97,33},{2,66}... | collective-permute-start | bytes 983048 | tf_op jit(solution)/shard_map/ppermute | solution.py:16
  507.4 33.0 %collective-permute-start.98 = (bf16[128,1280]{1,0:T(8,128)(2,1)}, bf16[128,1280]{1,0:T(8,128)(2,1)}, u32[]{:S(2)}, u32[]{:S(2)}) collective-permute-start(bf16[128,1280]{1,0:T(8,128)(2,1)} %get-tuple-element.374), channel_id=1, source_target_pairs={{0,32},{32,64},{64,96},{96,0},{1,33},{33,65},{65,97},{97,1},{2,34}... | collective-permute-start | bytes 983048 | tf_op jit(solution)/shard_map/ppermute | solution.py:16
  528.5 50.9 %collective-permute-start.151 = (bf16[512,1280]{1,0:T(8,128)(2,1)}, bf16[512,1280]{1,0:T(8,128)(2,1)}, u32[]{:S(2)}, u32[]{:S(2)}) collective-permute-start(bf16[512,1280]{1,0:T(8,128)(2,1)} %get-tuple-element.299), channel_id=1, source_target_pairs={{8,0},{16,8},{24,16},{9,1},{17,9},{25,17},{10,2},{18,10},{26,18},{... | collective-permute-start | bytes 3932168 | tf_op jit(solution)/shard_map/ppermute | solution.py:22
  607.7 68.1 %collective-permute-start.198 = (bf16[128,1280]{1,0:T(8,128)(2,1)}, bf16[128,1280]{1,0:T(8,128)(2,1)}, u32[]{:S(2)}, u32[]{:S(2)}) collective-permute-start(bf16[128,1280]{1,0:T(8,128)(2,1)} %get-tuple-element.364), channel_id=1, source_target_pairs={{0,96},{32,0},{64,32},{96,64},{1,97},{33,1},{65,33},{97,65},{2,98}... | collective-permute-start | bytes 983048 | tf_op jit(solution)/shard_map/ppermute | solution.py:16
  608.3 67.5 %collective-permute-start.197 = (bf16[128,1280]{1,0:T(8,128)(2,1)}, bf16[128,1280]{1,0:T(8,128)(2,1)}, u32[]{:S(2)}, u32[]{:S(2)}) collective-permute-start(bf16[128,1280]{1,0:T(8,128)(2,1)} %get-tuple-element.365), channel_id=1, source_target_pairs={{0,64},{32,96},{64,0},{96,32},{1,65},{33,97},{65,1},{97,33},{2,66}... | collective-permute-start | bytes 983048 | tf_op jit(solution)/shard_map/ppermute | solution.py:16
  649.1 26.7 %collective-permute-start.196 = (bf16[128,1280]{1,0:T(8,128)(2,1)S(1)}, bf16[128,1280]{1,0:T(8,128)(2,1)S(1)}, u32[]{:S(2)}, u32[]{:S(2)}) collective-permute-start(bf16[128,1280]{1,0:T(8,128)(2,1)S(1)} %copy-done.39), channel_id=1, source_target_pairs={{0,32},{32,64},{64,96},{96,0},{1,33},{33,65},{65,97},{97,1},{2,34}... | collective-permute-start | bytes 983048 | tf_op jit(solution)/shard_map/ppermute | solution.py:16
  (392 other events, 3675.3 us)

commit v2 on v1

--- a/solution.py
+++ b/solution.py
@@ -4,6 +4,7 @@
 from jax.experimental import pallas as pl
 from jax.experimental.pallas import tpu as pltpu
 from jax.sharding import PartitionSpec as P
+
 
 CAP = 8
 EPS = 1e-06
@@ -202,7 +203,7 @@
 
 def forward_out(gathered, down_w, experts):
     groups = len(gathered)
-    own, span = gathered[0].shape
+    own, span = gathered[0].shape[0], down_w.shape[0] + 128
     hidden, width = down_w.shape
     slots = groups * own
 
@@ -211,7 +212,7 @@
         down_ref, all_ref, out_ref = refs[:3]
         block_refs = refs[3:]
         for j, ref in enumerate(gathered_refs):
-            all_ref[j * own : (j + 1) * own, :] = ref[...]
+            all_ref[j * own : (j + 1) * own, :] = ref[:, :span]
         for at, size in tiles(width):
             part = mm(all_ref[:, :hidden], down_ref[:, at : at + size])
             out_ref[:, at : at + size] = part.astype(BF)
@@ -246,13 +247,17 @@
     return res[0], res[1], res[2:]
 
 
-def backward_act(first, parts, gate_pre, up_pre):
+def backward_act(first, parts, gate_pre, up_pre, lead=None):
     own, hidden = first.shape
+    skip = 0 if lead is None else lead.shape[1]
 
     def kernel(*refs):
         first_ref = refs[0]
         part_refs = refs[1 : 1 + len(parts)]
-        gate_ref, up_ref, pay_ref = refs[1 + len(parts) :]
+        gate_ref, up_ref, whole_ref = refs[1 + len(parts) : 4 + len(parts)] if lead is None else refs[2 + len(parts) :]
+        if lead is not None:
+            whole_ref[:, :skip] = refs[1 + len(parts)][...]
+        pay_ref = whole_ref.at[:, skip:]
         inner = jnp.zeros((own, 1), F32)
         for at, size in tiles(hidden):
             hid = first_ref[:, at : at + size]
@@ -268,22 +273,24 @@
             inner = inner + jnp.sum(both, axis=1, keepdims=True)
         pay_ref[:, 2 * hidden :] = lane_pack(inner).astype(BF)
 
-    outs = [shape(BF, own, 2 * hidden + 128)]
-    return call(kernel, [first, *parts, gate_pre, up_pre], outs)[0]
+    outs = [shape(BF, own, skip + 2 * hidden + 128)]
+    return call(kernel, [first, *parts] + ([] if lead is None else [lead]) + [gate_pre, up_pre], outs)[0]
 
 
 def backward_out(gathered, kept, slot, gain, gate_w, up_w, experts, model):
     groups = len(gathered)
-    own, span = gathered[0].shape
+    own = gathered[0].shape[0]
     width, hidden = gate_w.shape
     slots = groups * own
+    span = 2 * hidden + 128
+    skip = gathered[0].shape[1] - span
 
     def kernel(*refs):
         gathered_refs, refs = refs[:groups], refs[groups:]
         kept_ref, slot_ref, gain_ref, gate_ref, up_ref, all_ref, given_ref = refs[:7]
         block_refs = refs[7:]
         for j, ref in enumerate(gathered_refs):
-            all_ref[j * own : (j + 1) * own, :] = ref[...]
+            all_ref[j * own : (j + 1) * own, :] = ref[:, skip:]
         inv = lane_sum(kept_ref[:, hidden:])
         lean = lane_sum(all_ref[:, 2 * hidden :]) * inv * inv / model
         for at, size in tiles(width):
@@ -300,7 +307,7 @@
     return res[0], res[1], res[2:]
 
 
-def local(tokens, cotangent, norm_gain, route_gates, expert_ids, expert_map, w_gate, w_up, w_down):
+def stack(tokens, cotangent, norm_gain, route_gates, expert_ids, expert_map, w_gate, w_up, w_down):
     section = lax.axis_index("section")
     d = lax.axis_index("dp")
     me = lax.axis_index("expert")
@@ -325,14 +332,8 @@
     )
     pick = lambda x: jnp.sum(jnp.where(turn[None], x[:, :, None], 0.0), axis=1)
     mine = jnp.concatenate([pick(code), pick(weight)], axis=1)
-    all_groups = [mine] + [None] * (groups - 1)
-    for j in range(1, groups):
-        all_groups[groups - j] = ring(mine, "dp", j)
-    here = jnp.concatenate(all_groups, axis=0)
-    behind = hop(here, 1)
-    ahead = hop(here, -1)
-
-    def spread(table, per, count):
+
+    def spread(table, per, count, turned):
         total = table.shape[0]
         col = lax.broadcasted_iota(jnp.int32, (experts, count), 1)
         wide = (col // per == lax.broadcasted_iota(jnp.int32, (experts, count), 0)).astype(BF)
@@ -340,10 +341,10 @@
         weights = split(table[:, experts:])
         slot_col = lax.broadcasted_iota(jnp.int32, (total, count), 1)
         tok_row = lax.broadcasted_iota(jnp.int32, (total, count), 0)
-        hit_back = (mm(codes, wide) == (slot_col % CAP).astype(F32)) & ((slot_col // CAP) % (per // CAP) == tok_row // rows)
+        hit_back = (mm(codes, wide) == (slot_col % CAP).astype(F32)) & (((slot_col // CAP) % (per // CAP) + turned) % (per // CAP) == tok_row // rows)
         slot_row = lax.broadcasted_iota(jnp.int32, (count, total), 0)
         tok_col = lax.broadcasted_iota(jnp.int32, (count, total), 1)
-        hit_out = (mm(wide, codes, 0, 1) == (slot_row % CAP).astype(F32)) & ((slot_row // CAP) % (per // CAP) == tok_col // rows)
+        hit_out = (mm(wide, codes, 0, 1) == (slot_row % CAP).astype(F32)) & (((slot_row // CAP) % (per // CAP) + turned) % (per // CAP) == tok_col // rows)
 
         def weighted():
             return [jnp.where(hit_back, mm(w, wide), 0.0).astype(BF) for w in weights[:2]]
@@ -354,17 +355,19 @@
 
         return hit_out, hit_back, weighted, slot_weight
 
-    hit_out, hit_back, own_weighted, own_slot_weight = spread(mine, CAP, own)
+    hit_out, hit_back, own_weighted, own_slot_weight = spread(mine, CAP, own, 0)
     own_out, own_back = hit_out.astype(BF), hit_back.astype(BF)
     own_w = own_weighted()
     own_r = own_slot_weight()
-    hit_out, _, _, here_slot_weight = spread(here, block, slots)
-    send_table = hit_out.astype(BF)
-    send_r = here_slot_weight()
-    _, _, behind_weighted, _ = spread(behind, block, slots)
-    behind_w = behind_weighted()
-    _, hit_back, _, _ = spread(ahead, block, slots)
-    ahead_t = hit_back.astype(BF)
+
+    def after(value, gate):
+        return lax.optimization_barrier((value, gate))[0]
+
+    def narrow(value):
+        return lax.all_to_all(value, "dp", split_axis=1, concat_axis=0, tiled=True)
+
+    def broad(value):
+        return lax.all_to_all(value, "dp", split_axis=0, concat_axis=1, tiled=True)
 
     def cut(value, j):
         return lax.dynamic_slice_in_dim(value, ((d + j) % groups) * width, width, axis=1)
@@ -391,10 +394,12 @@
     def to_experts(blocks):
         return [blocks[0]] + [ring(blocks[k], "expert", k) for k in range(1, experts)]
 
-    def first_rows(value, scale):
+    def first_cut(value, scale):
         picked = mm(own_out, value)
-        picked = picked.astype(BF) if scale is None else (scale * picked).astype(BF)
-        return to_experts(by_expert(jnp.concatenate(to_slices(picked), axis=0)))
+        return to_slices(picked.astype(BF) if scale is None else (scale * picked).astype(BF))
+
+    def first_blocks(parts):
+        return by_expert(jnp.concatenate(parts, axis=0))
 
     def reduce_groups(parts):
         return [ring(part, "dp", j + 1) for j, part in enumerate(parts)]
@@ -410,62 +415,121 @@
             return latest
         return jax.tree.map(lambda a, b: jnp.where(section == at, a, b), latest, earlier)
 
-    def finish(state, moved, tables):
-        base = to_rows([state[j * rows : (j + 1) * rows] for j in range(groups)])
-        parts = jnp.concatenate(to_rows([moved[j * own : (j + 1) * own] for j in range(groups)]), axis=1)
-        blocks = [parts[k * CAP : (k + 1) * CAP] for k in range(experts)]
-        back = jnp.concatenate([blocks[0]] + [ring(blocks[k], "expert", -k) for k in range(1, experts)], axis=0)
-        added = sum(mm(t, back) for t in tables)
-        return absolute(
-            [(base[j].astype(F32) + added[:, j * width : (j + 1) * width]).astype(BF) for j in range(groups)]
-        )
-
-    received = first_rows(tokens, None)
-    state = jnp.concatenate(to_slices(tokens), axis=0)
-    early = first_rows(cotangent, own_r)
-    incoming = jnp.concatenate(to_slices(cotangent), axis=0)
-
-    saved, base, back = None, None, None
+    def own_parts(moved):
+        return to_rows([moved[j * own : (j + 1) * own] for j in range(groups)])
+
+    def own_rows(parts):
+        whole = absolute(parts)
+        blocks = [whole[k * CAP : (k + 1) * CAP] for k in range(experts)]
+        return jnp.concatenate([blocks[0]] + [ring(blocks[k], "expert", -k) for k in range(1, experts)], axis=0)
+
+    def finish(base, rows_back, tables):
+        return (base.astype(F32) + sum(mm(t, rows_back) for t in tables)).astype(BF)
+
+    start_parts = first_cut(tokens, None)
+    received = to_experts(first_blocks(start_parts))
+    codes = after(mine, start_parts)
+    codes = [codes] + [ring(codes, "dp", j) for j in range(1, groups)]
+    received, codes = lax.optimization_barrier((received, codes))
+    stacked = jnp.stack(codes)
+    here = jnp.concatenate(
+        [lax.dynamic_index_in_dim(stacked, (d - b) % groups, 0, keepdims=False) for b in range(groups)], axis=0
+    )
+    behind, ahead = hop(here, 1), hop(here, -1)
+    hit_out, _, _, here_slot_weight = spread(here, block, slots, d)
+    send_table = hit_out.astype(BF)
+    send_r = here_slot_weight()
+    _, _, behind_weighted, _ = spread(behind, block, slots, d)
+    behind_w = behind_weighted()
+    _, hit_back, _, _ = spread(ahead, block, slots, d)
+    ahead_t = hit_back.astype(BF)
+
+    saved, base, back, fills = None, None, None, {}
     for step in range(sections):
+        final_step = step + 1 == sections
         if step:
             state, picked = owner(base, back, behind_w, send_table, None, experts)
             received = to_experts(picked)
-        if step + 1 < sections:
-            base = state if step == 0 else hop(state, 1)
+        if final_step:
+            grad0, first0, parts0 = backward_in(after(fills["early"], picked), down_w, groups)
+            parts0 = reduce_groups(parts0)
+            received, parts0 = lax.optimization_barrier((received, parts0))
+        elif step:
+            base = hop(state, 1)
+        if step == 2:
+            received, fills["cut"] = lax.optimization_barrier((received, fills["cut"]))
         slot, first, parts = forward_in(received, gain, gate_w, up_w, groups)
+        if step == 2:
+            fills["early"] = to_experts(first_blocks(after(fills["cut"], parts)))
         parts = reduce_groups(parts)
+        if step == 0:
+            parts, behind, ahead = lax.optimization_barrier((parts, behind, ahead))
         payload, gate_pre, up_pre = forward_act(first, parts, model)
+        if final_step:
+            break
         gathered = gather_groups(payload)
+        if step == 2:
+            gathered, fills["early"] = lax.optimization_barrier((gathered, fills["early"]))
         kept, out, blocks = forward_out(gathered, down_w, experts)
-        if step + 1 < sections:
-            back = [hop_back(blocks[k], 1, k) for k in range(experts)]
+        if step == 0:
+            base = narrow(after(tokens, blocks))
+            state = base
+        if step == 1:
+            fills["cut"] = first_cut(after(cotangent, blocks), own_r)
+        if step == 2:
+            incoming = narrow(after(cotangent, blocks))
+        back = [hop_back(blocks[k], 1, k) for k in range(experts)]
+        if step == 2:
+            back, incoming = lax.optimization_barrier((back, incoming))
         saved = keep(step, (slot, gate_pre, up_pre, kept, out, state), saved)
 
-    slot, gate_pre, up_pre, kept, out, state = saved
-    layer_result = finish(state, out, own_w)
-
+    at = sections - 1
+    slot, gate_pre, up_pre, fwd_state = keep(
+        at, (slot, gate_pre, up_pre, state), (saved[0], saved[1], saved[2], saved[5])
+    )
     final = None
     base, state = incoming, incoming
     for step in range(sections):
         at = sections - 1 - step
         if step == 0:
-            received = early
+            grad = grad0
+            payload = backward_act(first0, parts0, gate_pre, up_pre, payload)
         else:
             state, picked = owner(base, back, [ahead_t], send_table, send_r, experts)
             received = to_experts(picked)
             if step + 1 < sections:
                 base = hop(state, -1)
-        grad, first, parts = backward_in(received, down_w, groups)
-        parts = reduce_groups(parts)
-        payload = backward_act(first, parts, gate_pre, up_pre)
+            else:
+                last = broad(jnp.where(section == at, state, final[-1]))
+            if step == 2:
+                received, fills["out"] = lax.optimization_barrier((received, fills["out"]))
+            grad, first, parts = backward_in(received, down_w, groups)
+            if step == 2:
+                rows_back = own_rows(after(fills["out"], parts))
+            parts = reduce_groups(parts)
+            if step == 3:
+                parts, last = lax.optimization_barrier((parts, last))
+            payload = backward_act(first, parts, gate_pre, up_pre)
         gathered = gather_groups(payload)
+        if step == 0:
+            kept, out, _ = forward_out(gathered, down_w, experts)
+            kept, fwd_out = keep(at, (kept, out), saved[3:5])
+        if step == 2:
+            gathered, rows_back = lax.optimization_barrier((gathered, rows_back))
         grads, given, blocks = backward_out(gathered, kept, slot, gain, gate_w, up_w, experts, model)
         if step + 1 < sections:
+            if step == 0:
+                fills["base"] = broad(after(fwd_state, blocks))
+            if step == 1:
+                fills["out"] = own_parts(after(fwd_out, blocks))
             back = [hop_back(blocks[k], -1, k) for k in range(experts)]
+            if step == 0:
+                back, fills["base"] = lax.optimization_barrier((back, fills["base"]))
         final = keep(at, (grad, grads, given, state), final)
 
+    layer_result = finish(fills["base"], rows_back, own_w)
     grad, grads, given, state = final
-    grad_in = finish(state, given, [own_back])
+    grad_in = finish(last, own_rows(own_parts(given)), [own_back])
     inv_all = from_lanes(kept, hidden)
     normed = (slot.astype(F32) * inv_all * gain).astype(BF)
     down_grad = mm(kept[:, :hidden], grad, 0, 0).astype(BF)
@@ -482,7 +546,7 @@
 
 def solution(mesh):
     return jax.shard_map(
-        local,
+        stack,
         mesh=mesh,
         in_specs=(
             P(("dp", "expert"), None),

time: 691 us -> 692 us (level)
  the two profiles are of different devices: /device:TPU:16 before, /device:TPU:1 now
where the time goes in v2:
time: 692 us; the launch traced here: 680 us
  starting transfers between devices  294 us (42%)
  waiting for transfers between devices  202 us (29%)
  Pallas kernels  112 us (16%)
  local copies, waits for them, and re-layouts  32.7 us (5%)
  matrix products  22.8 us (3%)
  other arithmetic  13.2 us (2%)
    ppermute x130, starting transfers between devices, ring(): lax.ppermute(value, axis, [(i, (i + steps) % count) for i in range(count)])  173 us
    ppermute x130, waiting for transfers between devices, ring(): lax.ppermute(value, axis, [(i, (i + steps) % count) for i in range(count)])  153 us
    pallas_call x30, Pallas kernels, call(): pl.pallas_call(kernel, out_shape=tuple(outs), in_specs=[pl.BlockSpec(memo...  112 us
    ppermute x48, starting transfers between devices, hop_back(): return lax.ppermute(value, ('section', 'expert'), pairs)  90 us
    ppermute x48, waiting for transfers between devices, hop_back(): return lax.ppermute(value, ('section', 'expert'), pairs)  42.7 us
    unnamed x474, local copies, waits for them, and re-layouts  23 us
    dot_general x22, matrix products, mm(): lax.dot_general(a, b, (((ca,), (cb,)), ((), ())), preferred_element_type=...  22.8 us
    ppermute x6, starting transfers between devices, hop(): return lax.ppermute(value, 'section', pairs)  15.6 us
  transfers between devices with their start and end apart: 188, of which 85 were waited for; matrix products, arithmetic and copies ran while one was open for 5% of the time, Pallas kernels for 6%

profile of v2, /device:TPU:1, one launch (start us, length us, event | category | flops | bytes accessed | tf_op | source)
XLA Modules:
  0.0 680.4 jit_solution(12721791182844322434)
XLA Ops:
  14.5 4.4 collective-permute-done.1
  39.4 4.5 shard_map.128
  63.6 4.3 collective-permute-done.18.refs_1_
  85.8 4.2 collective-permute-start.22
  89.9 5.0 collective-permute-start.23
  109.0 5.2 shard_map.131
  127.7 4.5 collective-permute-start.29
  132.9 4.5 shard_map.132
  144.6 5.5 collective-permute-done.38.refs_2_
  189.1 5.2 shard_map.135
  209.2 4.5 shard_map.136
  221.6 3.9 collective-permute-start.74
  277.3 5.6 shard_map.139
  306.1 4.6 shard_map.141
  315.1 8.7 %collective-permute-done.93.refs_1_ = bf16[64,1664]{1,0:T(8,128)(2,1)S(1)} collective-permute-done((bf16[64,1664]{1,0:T(8,128)(2,1)}, bf16[64,1664]{1,0:T(8,128)(2,1)S(1)}, u32[]{:S(2)}, u32[]{:S(2)}) %collective-permute-start.93) | collective-permute-done | bytes 213024 | tf_op jit(solution)/shard_map/ppermute | solution.py:17
  335.8 12.1 %collective-permute-done.96.refs_1_ = bf16[64,2560]{1,0:T(8,128)(2,1)S(1)} collective-permute-done((bf16[64,2560]{1,0:T(8,128)(2,1)}, bf16[64,2560]{1,0:T(8,128)(2,1)S(1)}, u32[]{:S(2)}, u32[]{:S(2)}) %collective-permute-start.96) | collective-permute-done | bytes 327712 | tf_op jit(solution)/shard_map/ppermute | solution.py:17
  348.0 4.1 collective-permute-done.98.refs_3_
  357.4 5.2 shard_map.145
  431.1 6.3 collective-permute-done.120.refs_3_
  437.4 5.1 shard_map.149
  447.9 16.5 %collective-permute-done.121.refs_1_ = bf16[32,1280]{1,0:T(8,128)(2,1)S(1)} collective-permute-done((bf16[32,1280]{1,0:T(8,128)(2,1)}, bf16[32,1280]{1,0:T(8,128)(2,1)S(1)}, u32[]{:S(2)}, u32[]{:S(2)}) %collective-permute-start.121) | collective-permute-done | bytes 81952 | tf_op jit(solution)/shard_map/ppermute | solution.py:34
  474.5 3.9 collective-permute-done.126.refs_6_
  515.9 4.6 collective-permute-start.147
  530.6 4.3 collective-permute-done.149
  535.0 5.1 collective-permute-done.150
  551.1 5.9 collective-permute-done.144.refs_3_
  557.7 5.2 shard_map.153
  588.5 3.9 shard_map.154
  595.1 4.4 all-to-all-start.3
  638.8 6.1 collective-permute-done.173.refs_3_
  644.9 5.1 shard_map.157
  657.6 4.9 collective-permute-done.174
  (926 shorter events, 499.1 us)
Async XLA Ops:
  76.9 31.0 %all-to-all-start = ((bf16[128,4,1280]{2,0,1:T(8,128)(2,1)}), bf16[128,4,1280]{2,0,1:T(8,128)(2,1)S(1)}, u32[]{:S(2)}, u32[]{:S(2)}) async-start(bf16[128,4,1280]{2,0,1:T(8,128)(2,1)} %bitcast.153), calls=%async_computation | async-start | bytes 2621440 | tf_op jit(solution)/shard_map/all_to_all | solution.py:367
  82.6 17.3 %collective-permute-start.21 = (bf16[32,1280]{1,0:T(8,128)(2,1)S(1)}, bf16[32,1280]{1,0:T(8,128)(2,1)S(1)}, u32[]{:S(2)}, u32[]{:S(2)}) collective-permute-start(bf16[32,1280]{1,0:T(8,128)(2,1)S(1)} %copy-done.205), channel_id=1, source_target_pairs={{0,8},{1,9},{2,10},{3,11},{4,12},{5,13},{6,14},{7,15},{8,16},{9,17... | collective-permute-start | bytes 245768 | tf_op jit(solution)/shard_map/ppermute | solution.py:34
  85.8 17.5 %collective-permute-start.22 = (bf16[32,1280]{1,0:T(8,128)(2,1)S(1)}, bf16[32,1280]{1,0:T(8,128)(2,1)S(1)}, u32[]{:S(2)}, u32[]{:S(2)}) collective-permute-start(bf16[32,1280]{1,0:T(8,128)(2,1)S(1)} %copy-done.201), channel_id=1, source_target_pairs={{0,15},{1,8},{2,9},{3,10},{4,11},{5,12},{6,13},{7,14},{8,23},{9,16... | collective-permute-start | bytes 245768 | tf_op jit(solution)/shard_map/ppermute | solution.py:34
  89.9 14.6 %collective-permute-start.23 = (bf16[32,1280]{1,0:T(8,128)(2,1)S(1)}, bf16[32,1280]{1,0:T(8,128)(2,1)S(1)}, u32[]{:S(2)}, u32[]{:S(2)}) collective-permute-start(bf16[32,1280]{1,0:T(8,128)(2,1)S(1)} %copy-done.195), channel_id=1, source_target_pairs={{0,14},{1,15},{2,8},{3,9},{4,10},{5,11},{6,12},{7,13},{8,22},{9,23... | collective-permute-start | bytes 245768 | tf_op jit(solution)/shard_map/ppermute | solution.py:34
  118.9 13.2 %collective-permute-start.33 = (bf16[32,1280]{1,0:T(8,128)(2,1)}, bf16[32,1280]{1,0:T(8,128)(2,1)S(1)}, u32[]{:S(2)}, u32[]{:S(2)}) collective-permute-start(bf16[32,1280]{1,0:T(8,128)(2,1)} %get-tuple-element.321), channel_id=1, source_target_pairs={{0,4},{1,5},{2,6},{3,7},{4,0},{5,1},{6,2},{7,3},{8,12},{9,13},{10,... | collective-permute-start | bytes 245768 | tf_op jit(solution)/shard_map/ppermute | solution.py:17
  127.7 60.7 %collective-permute-start.29 = (bf16[512,1280]{1,0:T(8,128)(2,1)}, bf16[512,1280]{1,0:T(8,128)(2,1)}, u32[]{:S(2)}, u32[]{:S(2)}) collective-permute-start(bf16[512,1280]{1,0:T(8,128)(2,1)} %get-tuple-element.316), channel_id=1, source_target_pairs={{0,8},{8,16},{16,24},{1,9},{9,17},{17,25},{2,10},{10,18},{18,26},{... | collective-permute-start | bytes 3932168 | tf_op jit(solution)/shard_map/ppermute | solution.py:23
  213.8 18.0 %collective-permute-start.61 = (bf16[64,1664]{1,0:T(8,128)(2,1)}, bf16[64,1664]{1,0:T(8,128)(2,1)S(1)}, u32[]{:S(2)}, u32[]{:S(2)}) collective-permute-start(bf16[64,1664]{1,0:T(8,128)(2,1)} %get-tuple-element.356), channel_id=1, source_target_pairs={{0,32},{32,64},{64,96},{96,0},{1,33},{33,65},{65,97},{97,1},{2,34}... | collective-permute-start | bytes 638984 | tf_op jit(solution)/shard_map/ppermute | solution.py:17
  214.7 20.3 %collective-permute-start.62 = (bf16[64,1664]{1,0:T(8,128)(2,1)}, bf16[64,1664]{1,0:T(8,128)(2,1)S(1)}, u32[]{:S(2)}, u32[]{:S(2)}) collective-permute-start(bf16[64,1664]{1,0:T(8,128)(2,1)} %get-tuple-element.357), channel_id=1, source_target_pairs={{0,64},{32,96},{64,0},{96,32},{1,65},{33,97},{65,1},{97,33},{2,66}... | collective-permute-start | bytes 638984 | tf_op jit(solution)/shard_map/ppermute | solution.py:17
  217.0 18.0 %collective-permute-start.63 = (bf16[64,1664]{1,0:T(8,128)(2,1)}, bf16[64,1664]{1,0:T(8,128)(2,1)S(1)}, u32[]{:S(2)}, u32[]{:S(2)}) collective-permute-start(bf16[64,1664]{1,0:T(8,128)(2,1)} %get-tuple-element.358), channel_id=1, source_target_pairs={{0,96},{32,0},{64,32},{96,64},{1,97},{33,1},{65,33},{97,65},{2,98}... | collective-permute-start | bytes 638984 | tf_op jit(solution)/shard_map/ppermute | solution.py:17
  221.6 55.5 %collective-permute-start.74 = (bf16[512,1280]{1,0:T(8,128)(2,1)S(1)}, bf16[512,1280]{1,0:T(8,128)(2,1)}, u32[]{:S(2)}, u32[]{:S(2)}) collective-permute-start(bf16[512,1280]{1,0:T(8,128)(2,1)S(1)} %copy-done.16), channel_id=1, source_target_pairs={{0,8},{8,16},{16,24},{1,9},{9,17},{17,25},{2,10},{10,18},{18,26},{... | collective-permute-start | bytes 3932168 | tf_op jit(solution)/shard_map/ppermute | solution.py:23
  253.3 23.9 %all-to-all-start.1 = ((bf16[128,4,1280]{2,0,1:T(8,128)(2,1)}), bf16[128,4,1280]{2,0,1:T(8,128)(2,1)S(1)}, u32[]{:S(2)}, u32[]{:S(2)}) async-start(bf16[128,4,1280]{2,0,1:T(8,128)(2,1)} %bitcast.152), calls=%async_computation.1 | async-start | bytes 2621440 | tf_op jit(solution)/shard_map/all_to_all | solution.py:367
  285.6 13.9 %collective-permute-start.85 = (bf16[32,1280]{1,0:T(8,128)(2,1)}, bf16[32,1280]{1,0:T(8,128)(2,1)S(1)}, u32[]{:S(2)}, u32[]{:S(2)}) collective-permute-start(bf16[32,1280]{1,0:T(8,128)(2,1)} %get-tuple-element.401), channel_id=1, source_target_pairs={{0,3},{1,4},{2,5},{3,6},{4,7},{5,0},{6,1},{7,2},{8,11},{9,12},{10,... | collective-permute-start | bytes 245768 | tf_op jit(solution)/shard_map/ppermute | solution.py:17
  287.3 13.4 %collective-permute-start.86 = (bf16[32,1280]{1,0:T(8,128)(2,1)}, bf16[32,1280]{1,0:T(8,128)(2,1)S(1)}, u32[]{:S(2)}, u32[]{:S(2)}) collective-permute-start(bf16[32,1280]{1,0:T(8,128)(2,1)} %get-tuple-element.402), channel_id=1, source_target_pairs={{0,4},{1,5},{2,6},{3,7},{4,0},{5,1},{6,2},{7,3},{8,12},{9,13},{10,... | collective-permute-start | bytes 245768 | tf_op jit(solution)/shard_map/ppermute | solution.py:17
  310.7 13.0 %collective-permute-start.93 = (bf16[64,1664]{1,0:T(8,128)(2,1)}, bf16[64,1664]{1,0:T(8,128)(2,1)S(1)}, u32[]{:S(2)}, u32[]{:S(2)}) collective-permute-start(bf16[64,1664]{1,0:T(8,128)(2,1)} %get-tuple-element.430), channel_id=1, source_target_pairs={{0,32},{32,64},{64,96},{96,0},{1,33},{33,65},{65,97},{97,1},{2,34}... | collective-permute-start | bytes 638984 | tf_op jit(solution)/shard_map/ppermute | solution.py:17
  331.6 16.4 %collective-permute-start.96 = (bf16[64,2560]{1,0:T(8,128)(2,1)}, bf16[64,2560]{1,0:T(8,128)(2,1)S(1)}, u32[]{:S(2)}, u32[]{:S(2)}) collective-permute-start(bf16[64,2560]{1,0:T(8,128)(2,1)} %shard_map.143.refs_0_), channel_id=1, source_target_pairs={{0,96},{32,0},{64,32},{96,64},{1,97},{33,1},{65,33},{97,65},{2,98}... | collective-permute-start | bytes 983048 | tf_op jit(solution)/shard_map/ppermute | solution.py:17
  334.2 13.7 %collective-permute-start.97 = (bf16[64,2560]{1,0:T(8,128)(2,1)}, bf16[64,2560]{1,0:T(8,128)(2,1)S(1)}, u32[]{:S(2)}, u32[]{:S(2)}) collective-permute-start(bf16[64,2560]{1,0:T(8,128)(2,1)} %shard_map.143.refs_0_), channel_id=1, source_target_pairs={{0,64},{32,96},{64,0},{96,32},{1,65},{33,97},{65,1},{97,33},{2,66}... | collective-permute-start | bytes 983048 | tf_op jit(solution)/shard_map/ppermute | solution.py:17
  334.3 17.8 %collective-permute-start.98 = (bf16[64,2560]{1,0:T(8,128)(2,1)}, bf16[64,2560]{1,0:T(8,128)(2,1)S(1)}, u32[]{:S(2)}, u32[]{:S(2)}) collective-permute-start(bf16[64,2560]{1,0:T(8,128)(2,1)} %shard_map.143.refs_0_), channel_id=1, source_target_pairs={{0,32},{32,64},{64,96},{96,0},{1,33},{33,65},{65,97},{97,1},{2,34}... | collective-permute-start | bytes 983048 | tf_op jit(solution)/shard_map/ppermute | solution.py:17
  362.6 20.7 %all-to-all-start.2 = ((bf16[4,128,1280]{2,1,0:T(8,128)(2,1)}), bf16[4,128,1280]{2,1,0:T(8,128)(2,1)S(1)}, u32[]{:S(2)}, u32[]{:S(2)}) async-start(bf16[4,128,1280]{2,1,0:T(8,128)(2,1)} %bitcast.35), calls=%async_computation.2 | async-start | bytes 2621440 | tf_op jit(solution)/shard_map/all_to_all | solution.py:370
  425.5 58.3 %collective-permute-start.107 = (bf16[512,1280]{1,0:T(8,128)(2,1)S(1)}, bf16[512,1280]{1,0:T(8,128)(2,1)S(1)}, u32[]{:S(2)}, u32[]{:S(2)}) collective-permute-start(bf16[512,1280]{1,0:T(8,128)(2,1)S(1)} %copy-done.15), channel_id=1, source_target_pairs={{8,0},{16,8},{24,16},{9,1},{17,9},{25,17},{10,2},{18,10},{26,18},{... | collective-permute-start | bytes 3932168 | tf_op jit(solution)/shard_map/ppermute | solution.py:23
  442.5 21.9 %collective-permute-start.121 = (bf16[32,1280]{1,0:T(8,128)(2,1)}, bf16[32,1280]{1,0:T(8,128)(2,1)S(1)}, u32[]{:S(2)}, u32[]{:S(2)}) collective-permute-start(bf16[32,1280]{1,0:T(8,128)(2,1)} %get-tuple-element.483), channel_id=1, source_target_pairs={{8,0},{9,1},{10,2},{11,3},{12,4},{13,5},{14,6},{15,7},{16,8},{17,9... | collective-permute-start | bytes 245768 | tf_op jit(solution)/shard_map/ppermute | solution.py:34
  443.8 21.9 %collective-permute-start.122 = (bf16[32,1280]{1,0:T(8,128)(2,1)}, bf16[32,1280]{1,0:T(8,128)(2,1)S(1)}, u32[]{:S(2)}, u32[]{:S(2)}) collective-permute-start(bf16[32,1280]{1,0:T(8,128)(2,1)} %get-tuple-element.484), channel_id=1, source_target_pairs={{8,7},{9,0},{10,1},{11,2},{12,3},{13,4},{14,5},{15,6},{16,15},{17,... | collective-permute-start | bytes 245768 | tf_op jit(solution)/shard_map/ppermute | solution.py:34
  445.1 21.9 %collective-permute-start.123 = (bf16[32,1280]{1,0:T(8,128)(2,1)}, bf16[32,1280]{1,0:T(8,128)(2,1)S(1)}, u32[]{:S(2)}, u32[]{:S(2)}) collective-permute-start(bf16[32,1280]{1,0:T(8,128)(2,1)} %get-tuple-element.485), channel_id=1, source_target_pairs={{8,6},{9,7},{10,0},{11,1},{12,2},{13,3},{14,4},{15,5},{16,14},{17,... | collective-permute-start | bytes 245768 | tf_op jit(solution)/shard_map/ppermute | solution.py:34
  446.4 21.9 %collective-permute-start.124 = (bf16[32,1280]{1,0:T(8,128)(2,1)}, bf16[32,1280]{1,0:T(8,128)(2,1)S(1)}, u32[]{:S(2)}, u32[]{:S(2)}) collective-permute-start(bf16[32,1280]{1,0:T(8,128)(2,1)} %get-tuple-element.486), channel_id=1, source_target_pairs={{8,5},{9,6},{10,7},{11,0},{12,1},{13,2},{14,3},{15,4},{16,13},{17,... | collective-permute-start | bytes 245768 | tf_op jit(solution)/shard_map/ppermute | solution.py:34
  467.1 14.1 %collective-permute-start.127 = (bf16[32,1280]{1,0:T(8,128)(2,1)S(1)}, bf16[32,1280]{1,0:T(8,128)(2,1)S(1)}, u32[]{:S(2)}, u32[]{:S(2)}) collective-permute-start(bf16[32,1280]{1,0:T(8,128)(2,1)S(1)} %copy-done.168), channel_id=1, source_target_pairs={{8,2},{9,3},{10,4},{11,5},{12,6},{13,7},{14,0},{15,1},{16,10},{17,... | collective-permute-start | bytes 245768 | tf_op jit(solution)/shard_map/ppermute | solution.py:34
  468.4 14.7 %collective-permute-start.128 = (bf16[32,1280]{1,0:T(8,128)(2,1)S(1)}, bf16[32,1280]{1,0:T(8,128)(2,1)S(1)}, u32[]{:S(2)}, u32[]{:S(2)}) collective-permute-start(bf16[32,1280]{1,0:T(8,128)(2,1)S(1)} %copy-done.163), channel_id=1, source_target_pairs={{8,1},{9,2},{10,3},{11,4},{12,5},{13,6},{14,7},{15,0},{16,9},{17,1... | collective-permute-start | bytes 245768 | tf_op jit(solution)/shard_map/ppermute | solution.py:34
  473.6 17.6 %collective-permute-start.136 = (bf16[64,1280]{1,0:T(8,128)(2,1)}, bf16[64,1280]{1,0:T(8,128)(2,1)S(1)}, u32[]{:S(2)}, u32[]{:S(2)}) collective-permute-start(bf16[64,1280]{1,0:T(8,128)(2,1)} %get-tuple-element.603), channel_id=1, source_target_pairs={{0,32},{32,64},{64,96},{96,0},{1,33},{33,65},{65,97},{97,1},{2,34}... | collective-permute-start | bytes 491528 | tf_op jit(solution)/shard_map/ppermute | solution.py:17
  479.1 14.3 %collective-permute-start.137 = (bf16[64,1280]{1,0:T(8,128)(2,1)}, bf16[64,1280]{1,0:T(8,128)(2,1)S(1)}, u32[]{:S(2)}, u32[]{:S(2)}) collective-permute-start(bf16[64,1280]{1,0:T(8,128)(2,1)} %get-tuple-element.602), channel_id=1, source_target_pairs={{0,64},{32,96},{64,0},{96,32},{1,65},{33,97},{65,1},{97,33},{2,66}... | collective-permute-start | bytes 491528 | tf_op jit(solution)/shard_map/ppermute | solution.py:17
  506.7 80.1 %collective-permute-start.152 = (bf16[512,1280]{1,0:T(8,128)(2,1)}, bf16[512,1280]{1,0:T(8,128)(2,1)S(1)}, u32[]{:S(2)}, u32[]{:S(2)}) collective-permute-start(bf16[512,1280]{1,0:T(8,128)(2,1)} %get-tuple-element.525), channel_id=1, source_target_pairs={{8,0},{16,8},{24,16},{9,1},{17,9},{25,17},{10,2},{18,10},{26,18},{... | collective-permute-start | bytes 3932168 | tf_op jit(solution)/shard_map/ppermute | solution.py:23
  508.0 32.0 %collective-permute-start.139 = (bf16[64,768]{1,0:T(8,128)(2,1)S(1)}, bf16[64,768]{1,0:T(8,128)(2,1)S(1)}, u32[]{:S(2)}, u32[]{:S(2)}) collective-permute-start(bf16[64,768]{1,0:T(8,128)(2,1)S(1)} %copy-done.156), channel_id=1, source_target_pairs={{0,32},{32,64},{64,96},{96,0},{1,33},{33,65},{65,97},{97,1},{2,34}... | collective-permute-start | bytes 294920 | tf_op jit(solution)/shard_map/ppermute | solution.py:17
  508.7 31.4 %collective-permute-start.140 = (bf16[64,768]{1,0:T(8,128)(2,1)S(1)}, bf16[64,768]{1,0:T(8,128)(2,1)S(1)}, u32[]{:S(2)}, u32[]{:S(2)}) collective-permute-start(bf16[64,768]{1,0:T(8,128)(2,1)S(1)} %copy-done.155), channel_id=1, source_target_pairs={{0,64},{32,96},{64,0},{96,32},{1,65},{33,97},{65,1},{97,33},{2,66}... | collective-permute-start | bytes 294920 | tf_op jit(solution)/shard_map/ppermute | solution.py:17
  509.4 30.7 %collective-permute-start.141 = (bf16[64,768]{1,0:T(8,128)(2,1)S(1)}, bf16[64,768]{1,0:T(8,128)(2,1)S(1)}, u32[]{:S(2)}, u32[]{:S(2)}) collective-permute-start(bf16[64,768]{1,0:T(8,128)(2,1)S(1)} %copy-done.154), channel_id=1, source_target_pairs={{0,96},{32,0},{64,32},{96,64},{1,97},{33,1},{65,33},{97,65},{2,98}... | collective-permute-start | bytes 294920 | tf_op jit(solution)/shard_map/ppermute | solution.py:17
  595.1 30.9 %all-to-all-start.3 = ((bf16[4,128,1280]{2,1,0:T(8,128)(2,1)}), bf16[4,128,1280]{2,1,0:T(8,128)(2,1)}, u32[]{:S(2)}, u32[]{:S(2)}) async-start(bf16[4,128,1280]{2,1,0:T(8,128)(2,1)} %bitcast.47), calls=%async_computation.3 | async-start | bytes 2621440 | tf_op jit(solution)/shard_map/all_to_all | solution.py:370
  (386 other events, 2849.5 us)

commit v3 on v2

--- a/solution.py
+++ b/solution.py
@@ -1,3 +1,5 @@
+import math
+
 import jax
 import jax.numpy as jnp
 from jax import lax
@@ -15,6 +17,18 @@
 def ring(value, axis, steps):
     count = lax.axis_size(axis)
     return lax.ppermute(value, axis, [(i, (i + steps) % count) for i in range(count)])
+
+
+def ring_in(value, axis, steps, where):
+    count = lax.axis_size(axis)
+    sections = lax.axis_size("section")
+    if axis == "dp":
+        at = lambda s, i: (i % count) * sections + s
+        axes = (axis, "section")
+    else:
+        at = lambda s, i: s * count + i % count
+        axes = ("section", axis)
+    return lax.ppermute(value, axes, [(at(s, i), at(s, i + steps)) for s in where for i in range(count)])
 
 
 def hop(value, steps):
@@ -86,16 +100,25 @@
         ref[:, at : at + size] = jnp.concatenate(rows, axis=0).astype(BF)
 
 
+def near(x):
+    return pltpu.with_memory_space_constraint(x, pltpu.VMEM)
+
+
 def call(kernel, ins, outs, scratch=(), flops=0):
-    moved = sum(x.size * x.dtype.itemsize for x in ins) + sum(o.size * o.dtype.itemsize for o in outs)
+    moved = sum(math.prod(x.shape) * jnp.dtype(x.dtype).itemsize for x in [*ins, *outs])
     return pl.pallas_call(
         kernel,
         out_shape=tuple(outs),
         in_specs=[pl.BlockSpec(memory_space=pltpu.VMEM)] * len(ins),
         out_specs=tuple(pl.BlockSpec(memory_space=pltpu.VMEM) for _ in outs),
         scratch_shapes=list(scratch),
+        compiler_params=pltpu.CompilerParams(vmem_limit_bytes=16 << 20),
         cost_estimate=pl.CostEstimate(flops=flops, bytes_accessed=moved, transcendentals=0),
     )(*ins)
+
+
+def fast(dtype, *dims):
+    return pltpu.VMEM(dims, dtype)
 
 
 def shape(dtype, *dims):
@@ -129,8 +152,8 @@
             for k in range(experts):
                 out_refs[k][:, at : at + size] = picked[k * block : (k + 1) * block]
 
-    ins = [state, *back, *tables, send_table] + ([] if scale is None else [scale])
-    outs = [shape(BF, count, width)] + [shape(BF, block, width)] * experts
+    ins = [state, *map(near, back), *tables, send_table] + ([] if scale is None else [scale])
+    outs = [shape(BF, count, width)] + [fast(BF, block, width)] * experts
     res = call(kernel, ins, outs, flops=2 * count * slots * width * (1 + len(tables)))
     return res[0], res[1:]
 
@@ -161,11 +184,11 @@
         for j in range(1, groups):
             part_refs[j - 1][:, 2 * hidden :] = lane_pack(squares[j]).astype(BF)
 
-    outs = [shape(BF, slots, width), shape(F32, own, 2 * hidden + 128)]
-    outs += [shape(BF, own, 2 * hidden + 128)] * (groups - 1)
+    outs = [shape(BF, slots, width), fast(F32, own, 2 * hidden + 128)]
+    outs += [fast(BF, own, 2 * hidden + 128)] * (groups - 1)
     res = call(
         kernel,
-        [*blocks, gain, gate_w, up_w],
+        [*map(near, blocks), gain, gate_w, up_w],
         outs,
         [pltpu.VMEM((slots, width), BF)],
         flops=4 * slots * width * hidden,
@@ -197,8 +220,8 @@
             pay_ref[:, at : at + size] = (gate * jax.nn.sigmoid(gate) * up).astype(BF)
         pay_ref[:, hidden:] = lane_pack(inv).astype(BF)
 
-    outs = [shape(BF, own, hidden + 128), shape(F32, own, hidden), shape(F32, own, hidden)]
-    return call(kernel, [first, *parts], outs)
+    outs = [fast(BF, own, hidden + 128), shape(F32, own, hidden), shape(F32, own, hidden)]
+    return call(kernel, [near(first), *map(near, parts)], outs)
 
 
 def forward_out(gathered, down_w, experts):
@@ -218,8 +241,8 @@
             out_ref[:, at : at + size] = part.astype(BF)
             put_blocks(part, block_refs, at, size, groups)
 
-    outs = [shape(BF, slots, span), shape(BF, slots, width)] + [shape(BF, groups * CAP, width)] * experts
-    res = call(kernel, [*gathered, down_w], outs, flops=2 * slots * hidden * width)
+    outs = [shape(BF, slots, span), shape(BF, slots, width)] + [fast(BF, groups * CAP, width)] * experts
+    res = call(kernel, [*map(near, gathered), down_w], outs, flops=2 * slots * hidden * width)
     return res[0], res[1], res[2:]
 
 
@@ -242,8 +265,8 @@
             for j in range(1, groups):
                 part_refs[j - 1][:, at : at + size] = part[j * own : (j + 1) * own].astype(BF)
 
-    outs = [shape(BF, slots, width), shape(F32, own, hidden)] + [shape(BF, own, hidden)] * (groups - 1)
-    res = call(kernel, [*blocks, down_w], outs, flops=2 * slots * width * hidden)
+    outs = [shape(BF, slots, width), fast(F32, own, hidden)] + [fast(BF, own, hidden)] * (groups - 1)
+    res = call(kernel, [*map(near, blocks), down_w], outs, flops=2 * slots * width * hidden)
     return res[0], res[1], res[2:]
 
 
@@ -273,8 +296,8 @@
             inner = inner + jnp.sum(both, axis=1, keepdims=True)
         pay_ref[:, 2 * hidden :] = lane_pack(inner).astype(BF)
 
-    outs = [shape(BF, own, skip + 2 * hidden + 128)]
-    return call(kernel, [first, *parts] + ([] if lead is None else [lead]) + [gate_pre, up_pre], outs)[0]
+    outs = [fast(BF, own, skip + 2 * hidden + 128)]
+    return call(kernel, [near(first), *map(near, parts)] + ([] if lead is None else [near(lead)]) + [gate_pre, up_pre], outs)[0]
 
 
 def backward_out(gathered, kept, slot, gain, gate_w, up_w, experts, model):
@@ -300,9 +323,9 @@
             given_ref[:, at : at + size] = given.astype(BF)
             put_blocks(given, block_refs, at, size, groups)
 
-    outs = [shape(BF, slots, span), shape(BF, slots, width)] + [shape(BF, groups * CAP, width)] * experts
+    outs = [shape(BF, slots, span), shape(BF, slots, width)] + [fast(BF, groups * CAP, width)] * experts
     res = call(
-        kernel, [*gathered, kept, slot, gain, gate_w, up_w], outs, flops=4 * slots * hidden * width
+        kernel, [*map(near, gathered), kept, slot, gain, gate_w, up_w], outs, flops=4 * slots * hidden * width
     )
     return res[0], res[1], res[2:]
 
@@ -363,12 +386,6 @@
     def after(value, gate):
         return lax.optimization_barrier((value, gate))[0]
 
-    def narrow(value):
-        return lax.all_to_all(value, "dp", split_axis=1, concat_axis=0, tiled=True)
-
-    def broad(value):
-        return lax.all_to_all(value, "dp", split_axis=0, concat_axis=1, tiled=True)
-
     def cut(value, j):
         return lax.dynamic_slice_in_dim(value, ((d + j) % groups) * width, width, axis=1)
 
@@ -378,6 +395,12 @@
             out[groups - j] = ring(cut(value, j), "dp", j)
         return out
 
+    def narrow(value, where):
+        out = [cut(value, 0)] + [None] * (groups - 1)
+        for j in range(1, groups):
+            out[groups - j] = ring_in(cut(value, j), "dp", j, where)
+        return out
+
     def to_rows(parts):
         return [parts[0]] + [ring(parts[j], "dp", j) for j in range(1, groups)]
 
@@ -391,12 +414,16 @@
         shaped = value.reshape(groups, experts, CAP, value.shape[-1])
         return [shaped[:, k].reshape(block, value.shape[-1]) for k in range(experts)]
 
-    def to_experts(blocks):
-        return [blocks[0]] + [ring(blocks[k], "expert", k) for k in range(1, experts)]
+    def to_experts(blocks, where=None):
+        if where is None:
+            return [blocks[0]] + [ring(blocks[k], "expert", k) for k in range(1, experts)]
+        return [blocks[0]] + [ring_in(blocks[k], "expert", k, where) for k in range(1, experts)]
 
     def first_cut(value, scale):
         picked = mm(own_out, value)
-        return to_slices(picked.astype(BF) if scale is None else (scale * picked).astype(BF))
+        if scale is None:
+            return to_slices(picked.astype(BF))
+        return narrow((scale * picked).astype(BF), (sections - 1,))
 
     def first_blocks(parts):
         return by_expert(jnp.concatenate(parts, axis=0))
@@ -426,61 +453,56 @@
     def finish(base, rows_back, tables):
         return (base.astype(F32) + sum(mm(t, rows_back) for t in tables)).astype(BF)
 
+    lower = tuple(range(sections - 1))
     start_parts = first_cut(tokens, None)
     received = to_experts(first_blocks(start_parts))
     codes = after(mine, start_parts)
     codes = [codes] + [ring(codes, "dp", j) for j in range(1, groups)]
     received, codes = lax.optimization_barrier((received, codes))
-    stacked = jnp.stack(codes)
-    here = jnp.concatenate(
-        [lax.dynamic_index_in_dim(stacked, (d - b) % groups, 0, keepdims=False) for b in range(groups)], axis=0
-    )
-    behind, ahead = hop(here, 1), hop(here, -1)
-    hit_out, _, _, here_slot_weight = spread(here, block, slots, d)
+    here = jnp.concatenate([codes[(groups - j) % groups] for j in range(groups)], axis=0)
+    begin = after(tokens, start_parts)
+    begin = {j: ring_in(cut(begin, j), "dp", j, lower) for j in (1, 3)}
+    hit_out, _, _, here_slot_weight = spread(here, block, slots, 0)
     send_table = hit_out.astype(BF)
     send_r = here_slot_weight()
-    _, _, behind_weighted, _ = spread(behind, block, slots, d)
-    behind_w = behind_weighted()
-    _, hit_back, _, _ = spread(ahead, block, slots, d)
-    ahead_t = hit_back.astype(BF)
-
-    saved, base, back, fills = None, None, None, {}
+
+    saved, back, fills = None, None, {}
     for step in range(sections):
         final_step = step + 1 == sections
         if step:
             state, picked = owner(base, back, behind_w, send_table, None, experts)
             received = to_experts(picked)
-        if final_step:
-            grad0, first0, parts0 = backward_in(after(fills["early"], picked), down_w, groups)
-            parts0 = reduce_groups(parts0)
-            received, parts0 = lax.optimization_barrier((received, parts0))
-        elif step:
+        if step and not final_step:
             base = hop(state, 1)
-        if step == 2:
-            received, fills["cut"] = lax.optimization_barrier((received, fills["cut"]))
         slot, first, parts = forward_in(received, gain, gate_w, up_w, groups)
-        if step == 2:
+        if step == 1:
             fills["early"] = to_experts(first_blocks(after(fills["cut"], parts)))
         parts = reduce_groups(parts)
-        if step == 0:
-            parts, behind, ahead = lax.optimization_barrier((parts, behind, ahead))
         payload, gate_pre, up_pre = forward_act(first, parts, model)
         if final_step:
             break
         gathered = gather_groups(payload)
-        if step == 2:
+        if step == 1:
             gathered, fills["early"] = lax.optimization_barrier((gathered, fills["early"]))
+        if step == 0:
+            codes = after(here, payload)
+            behind, ahead = hop(codes, 1), hop(codes, -1)
+            _, _, behind_weighted, _ = spread(behind, block, slots, 0)
+            behind_w = behind_weighted()
+            _, hit_back, _, _ = spread(ahead, block, slots, 0)
+            ahead_t = hit_back.astype(BF)
+            fills["cut"] = first_cut(after(cotangent, payload), own_r)
         kept, out, blocks = forward_out(gathered, down_w, experts)
+        back = [hop_back(blocks[k], 1, k) for k in range(experts)]
         if step == 0:
-            base = narrow(after(tokens, blocks))
+            far = ring_in(cut(after(tokens, blocks), 2), "dp", 2, lower)
+            base = jnp.concatenate([cut(tokens, 0), begin[groups - 1], far, begin[1]], axis=0)
             state = base
         if step == 1:
-            fills["cut"] = first_cut(after(cotangent, blocks), own_r)
+            incoming = jnp.concatenate(narrow(after(cotangent, blocks), lower), axis=0)
         if step == 2:
-            incoming = narrow(after(cotangent, blocks))
-        back = [hop_back(blocks[k], 1, k) for k in range(experts)]
-        if step == 2:
-            back, incoming = lax.optimization_barrier((back, incoming))
+            grad0, first0, parts0 = backward_in(after(fills["early"], blocks), down_w, groups)
+            parts0 = [ring_in(part, "dp", j + 1, (sections - 1,)) for j, part in enumerate(parts0)]
         saved = keep(step, (slot, gate_pre, up_pre, kept, out, state), saved)
 
     at = sections - 1
@@ -500,15 +522,17 @@
             if step + 1 < sections:
                 base = hop(state, -1)
             else:
-                last = broad(jnp.where(section == at, state, final[-1]))
+                turn_back = jnp.where(section == at, state, final[-1])
+                turn_back = [turn_back[j * rows : (j + 1) * rows] for j in range(groups)]
+                near_parts = {j: ring_in(turn_back[j], "dp", j, lower) for j in (1, 3)}
+            if step == 1:
+                received, fills["base"] = lax.optimization_barrier((received, fills["base"]))
             if step == 2:
                 received, fills["out"] = lax.optimization_barrier((received, fills["out"]))
             grad, first, parts = backward_in(received, down_w, groups)
             if step == 2:
                 rows_back = own_rows(after(fills["out"], parts))
             parts = reduce_groups(parts)
-            if step == 3:
-                parts, last = lax.optimization_barrier((parts, last))
             payload = backward_act(first, parts, gate_pre, up_pre)
         gathered = gather_groups(payload)
         if step == 0:
@@ -519,17 +543,22 @@
         grads, given, blocks = backward_out(gathered, kept, slot, gain, gate_w, up_w, experts, model)
         if step + 1 < sections:
             if step == 0:
-                fills["base"] = broad(after(fwd_state, blocks))
+                held = after(fwd_state, blocks)
+                fills["base"] = to_rows([held[j * rows : (j + 1) * rows] for j in range(groups)])
             if step == 1:
                 fills["out"] = own_parts(after(fwd_out, blocks))
             back = [hop_back(blocks[k], -1, k) for k in range(experts)]
-            if step == 0:
-                back, fills["base"] = lax.optimization_barrier((back, fills["base"]))
         final = keep(at, (grad, grads, given, state), final)
 
-    layer_result = finish(fills["base"], rows_back, own_w)
+    layer_base = jnp.where(section == 0, tokens, absolute(fills["base"]))
+    layer_result = finish(layer_base, rows_back, own_w)
     grad, grads, given, state = final
-    grad_in = finish(last, own_rows(own_parts(given)), [own_back])
+    last_parts = own_parts(given)
+    last_back = own_rows(last_parts)
+    far_part = ring_in(after(turn_back[2], last_parts), "dp", 2, lower)
+    last = absolute([turn_back[0], near_parts[1], far_part, near_parts[3]])
+    last = jnp.where(section == sections - 1, cotangent, last)
+    grad_in = finish(last, last_back, [own_back])
     inv_all = from_lanes(kept, hidden)
     normed = (slot.astype(F32) * inv_all * gain).astype(BF)
     down_grad = mm(kept[:, :hidden], grad, 0, 0).astype(BF)

time: 692 us -> 656 us (0.948)
  the two profiles are of different devices: /device:TPU:1 before, /device:TPU:48 now
where the time goes in v3:
time: 656 us; the launch traced here: 645 us
  starting transfers between devices  321 us (49%)
  waiting for transfers between devices  201 us (31%)
  local copies, waits for them, and re-layouts  46.5 us (7%)
  Pallas kernels  38.1 us (6%)
  matrix products  24.2 us (4%)
  other arithmetic  10.6 us (2%)
    ppermute x127, waiting for transfers between devices, ring(): lax.ppermute(value, axis, [(i, (i + steps) % count) for i in range(count)])  159 us
    ppermute x127, starting transfers between devices, ring(): lax.ppermute(value, axis, [(i, (i + steps) % count) for i in range(count)])  157 us
    ppermute x48, starting transfers between devices, hop_back(): return lax.ppermute(value, ('section', 'expert'), pairs)  107 us
    ppermute x48, waiting for transfers between devices, hop_back(): return lax.ppermute(value, ('section', 'expert'), pairs)  41 us
    unnamed x373, local copies, waits for them, and re-layouts  39.4 us
    pallas_call x30, Pallas kernels, call(): pl.pallas_call(kernel, out_shape=tuple(outs), in_specs=[pl.BlockSpec(memo...  38.1 us
    ppermute x15, starting transfers between devices, ring_in(): lax.ppermute(value, axes, [(at(s, i), at(s, i + steps)) for s in where fo...  34.8 us
    dot_general x22, matrix products, mm(): lax.dot_general(a, b, (((ca,), (cb,)), ((), ())), preferred_element_type=...  24.2 us
  transfers between devices with their start and end apart: 196, of which 81 were waited for; matrix products, arithmetic and copies ran while one was open for 5% of the time, Pallas kernels for 4%

profile of v3, /device:TPU:48, one launch (start us, length us, event | category | flops | bytes accessed | tf_op | source)
XLA Modules:
  0.0 645.3 jit_solution(11135620410540874707)
XLA Ops:
  45.9 5.6 collective-permute-done.14.refs_1_
  68.4 4.9 collective-permute-start.20
  111.0 8.0 %collective-permute-start.57 = (bf16[512,1280]{1,0:T(8,128)(2,1)S(1)}, bf16[512,1280]{1,0:T(8,128)(2,1)S(1)}, u32[]{:S(2)}, u32[]{:S(2)}) collective-permute-start(bf16[512,1280]{1,0:T(8,128)(2,1)S(1)} %get-tuple-element.321), channel_id=1, source_target_pairs={{0,8},{8,16},{16,24},{1,9},{9,17},{17,25},{2,10},{10,18},{18,26},{... | collective-permute-start | bytes 3932168 | tf_op jit(solution)/shard_map/ppermute | solution.py:37
  130.2 5.4 collective-permute-done.48.refs_2_
  204.5 6.1 collective-permute-done.75.refs_3_
  243.2 6.0 collective-permute-start.112
  249.3 3.7 shard_map.140
  276.3 4.0 collective-permute-start.55
  284.9 9.4 %collective-permute-start.101 = (bf16[64,2560]{1,0:T(8,128)(2,1)S(1)}, bf16[64,2560]{1,0:T(8,128)(2,1)S(1)}, u32[]{:S(2)}, u32[]{:S(2)}) collective-permute-start(bf16[64,2560]{1,0:T(8,128)(2,1)S(1)} %shard_map.143.refs_0_), channel_id=1, source_target_pairs={{0,96},{32,0},{64,32},{96,64},{1,97},{33,1},{65,33},{97,65},{2,98}... | collective-permute-start | bytes 983048 | tf_op jit(solution)/shard_map/ppermute | solution.py:19
  296.0 6.8 %collective-permute-done.101.refs_1_ = bf16[64,2560]{1,0:T(8,128)(2,1)S(1)} collective-permute-done((bf16[64,2560]{1,0:T(8,128)(2,1)S(1)}, bf16[64,2560]{1,0:T(8,128)(2,1)S(1)}, u32[]{:S(2)}, u32[]{:S(2)}) %collective-permute-start.101) | collective-permute-done | bytes 327712 | tf_op jit(solution)/shard_map/ppermute | solution.py:19
  305.5 4.0 collective-permute-done.102.refs_2_
  314.8 5.0 collective-permute-start.104
  346.0 3.7 collective-permute-start.121
  350.9 5.4 collective-permute-done.114.refs_2_
  358.5 3.9 collective-permute-done.116.refs_4_
  386.7 4.2 collective-permute-done.128.refs_2_
  403.8 18.3 %collective-permute-done.130.refs_1_ = bf16[32,1280]{1,0:T(8,128)(2,1)S(1)} collective-permute-done((bf16[32,1280]{1,0:T(8,128)(2,1)S(1)}, bf16[32,1280]{1,0:T(8,128)(2,1)S(1)}, u32[]{:S(2)}, u32[]{:S(2)}) %collective-permute-start.130) | collective-permute-done | bytes 81952 | tf_op jit(solution)/shard_map/ppermute | solution.py:48
  470.4 4.1 collective-permute-done.155
  474.8 4.5 collective-permute-done.156
  479.3 5.9 collective-permute-done.157
  485.2 6.1 collective-permute-done.158
  491.4 5.6 collective-permute-done.159
  514.0 4.1 collective-permute-start.163
  555.8 4.1 fusion.4
  575.9 3.9 collective-permute-start.170
  589.9 5.5 collective-permute-done.181.refs_1_
  595.4 5.4 collective-permute-done.182.refs_2_
  613.2 3.8 collective-permute-start.189
  619.0 4.7 collective-permute-start.187
  624.4 4.7 collective-permute-done.190
  629.8 5.8 collective-permute-done.192
  636.2 5.4 collective-permute-done.194
  (848 shorter events, 462.9 us)
Async XLA Ops:
  32.5 45.0 %collective-permute-start.21 = (bf16[128,1280]{1,0:T(8,128)(2,1)S(1)}, bf16[128,1280]{1,0:T(8,128)(2,1)S(1)}, u32[]{:S(2)}, u32[]{:S(2)}) collective-permute-start(bf16[128,1280]{1,0:T(8,128)(2,1)S(1)} %get-tuple-element.526), channel_id=1, source_target_pairs={{0,32},{32,64},{64,96},{96,0},{8,40},{40,72},{72,104},{104,8},{16,... | collective-permute-start | bytes 983048 | tf_op jit(solution)/shard_map/ppermute | solution.py:31
  36.1 43.6 %collective-permute-start.3 = (bf16[128,1280]{1,0:T(8,128)(2,1)S(1)}, bf16[128,1280]{1,0:T(8,128)(2,1)S(1)}, u32[]{:S(2)}, u32[]{:S(2)}) collective-permute-start(bf16[128,1280]{1,0:T(8,128)(2,1)S(1)} %get-tuple-element.525), channel_id=1, source_target_pairs={{0,96},{32,0},{64,32},{96,64},{8,104},{40,8},{72,40},{104,72},{16,... | collective-permute-start | bytes 983048 | tf_op jit(solution)/shard_map/ppermute | solution.py:31
  68.4 19.1 %collective-permute-start.20 = (bf16[128,1280]{1,0:T(8,128)(2,1)S(1)}, bf16[128,1280]{1,0:T(8,128)(2,1)S(1)}, u32[]{:S(2)}, u32[]{:S(2)}) collective-permute-start(bf16[128,1280]{1,0:T(8,128)(2,1)S(1)} %constant_dynamic-slice_fusion.9), channel_id=1, source_target_pairs={{0,64},{32,96},{64,0},{96,32},{8,72},{40,104},{72,8},{104,40},{16,... | collective-permute-start | bytes 983048 | tf_op jit(solution)/shard_map/ppermute | solution.py:31
  111.0 66.2 %collective-permute-start.57 = (bf16[512,1280]{1,0:T(8,128)(2,1)S(1)}, bf16[512,1280]{1,0:T(8,128)(2,1)S(1)}, u32[]{:S(2)}, u32[]{:S(2)}) collective-permute-start(bf16[512,1280]{1,0:T(8,128)(2,1)S(1)} %get-tuple-element.321), channel_id=1, source_target_pairs={{0,8},{8,16},{16,24},{1,9},{9,17},{17,25},{2,10},{10,18},{18,26},{... | collective-permute-start | bytes 3932168 | tf_op jit(solution)/shard_map/ppermute | solution.py:37
  120.2 16.1 %collective-permute-start.38 = (bf16[64,1664]{1,0:T(8,128)(2,1)S(1)}, bf16[64,1664]{1,0:T(8,128)(2,1)S(1)}, u32[]{:S(2)}, u32[]{:S(2)}) collective-permute-start(bf16[64,1664]{1,0:T(8,128)(2,1)S(1)} %get-tuple-element.291), channel_id=1, source_target_pairs={{0,32},{32,64},{64,96},{96,0},{1,33},{33,65},{65,97},{97,1},{2,34}... | collective-permute-start | bytes 638984 | tf_op jit(solution)/shard_map/ppermute | solution.py:19
  120.3 16.6 %collective-permute-start.39 = (bf16[64,1664]{1,0:T(8,128)(2,1)S(1)}, bf16[64,1664]{1,0:T(8,128)(2,1)S(1)}, u32[]{:S(2)}, u32[]{:S(2)}) collective-permute-start(bf16[64,1664]{1,0:T(8,128)(2,1)S(1)} %get-tuple-element.292), channel_id=1, source_target_pairs={{0,64},{32,96},{64,0},{96,32},{1,65},{33,97},{65,1},{97,33},{2,66}... | collective-permute-start | bytes 638984 | tf_op jit(solution)/shard_map/ppermute | solution.py:19
  122.0 17.8 %collective-permute-start.40 = (bf16[64,1664]{1,0:T(8,128)(2,1)S(1)}, bf16[64,1664]{1,0:T(8,128)(2,1)S(1)}, u32[]{:S(2)}, u32[]{:S(2)}) collective-permute-start(bf16[64,1664]{1,0:T(8,128)(2,1)S(1)} %get-tuple-element.293), channel_id=1, source_target_pairs={{0,96},{32,0},{64,32},{96,64},{1,97},{33,1},{65,33},{97,65},{2,98}... | collective-permute-start | bytes 638984 | tf_op jit(solution)/shard_map/ppermute | solution.py:19
  179.6 69.6 %collective-permute-start.82 = (bf16[512,1280]{1,0:T(8,128)(2,1)S(1)}, bf16[512,1280]{1,0:T(8,128)(2,1)}, u32[]{:S(2)}, u32[]{:S(2)}) collective-permute-start(bf16[512,1280]{1,0:T(8,128)(2,1)S(1)} %get-tuple-element.355), channel_id=1, source_target_pairs={{0,8},{8,16},{16,24},{1,9},{9,17},{17,25},{2,10},{10,18},{18,26},{... | collective-permute-start | bytes 3932168 | tf_op jit(solution)/shard_map/ppermute | solution.py:37
  243.2 16.4 %collective-permute-start.112 = (bf16[512,16]{0,1:T(8,128)(2,1)}, bf16[512,16]{0,1:T(8,128)(2,1)}, u32[]{:S(2)}, u32[]{:S(2)}) collective-permute-start(bf16[512,16]{0,1:T(8,128)(2,1)} %convert.18), channel_id=1, source_target_pairs={{8,0},{16,8},{24,16},{9,1},{17,9},{25,17},{10,2},{18,10},{26,18},{... | collective-permute-start | bytes 49160 | tf_op jit(solution)/shard_map/ppermute | solution.py:37
  274.3 48.9 %collective-permute-start.54 = (bf16[128,1280]{1,0:T(8,128)(2,1)S(1)}, bf16[128,1280]{1,0:T(8,128)(2,1)S(1)}, u32[]{:S(2)}, u32[]{:S(2)}) collective-permute-start(bf16[128,1280]{1,0:T(8,128)(2,1)S(1)} %get-tuple-element.524), channel_id=1, source_target_pairs={{0,96},{32,0},{64,32},{96,64},{8,104},{40,8},{72,40},{104,72},{16,... | collective-permute-start | bytes 983048 | tf_op jit(solution)/shard_map/ppermute | solution.py:31
  276.3 49.7 %collective-permute-start.55 = (bf16[128,1280]{1,0:T(8,128)(2,1)S(1)}, bf16[128,1280]{1,0:T(8,128)(2,1)S(1)}, u32[]{:S(2)}, u32[]{:S(2)}) collective-permute-start(bf16[128,1280]{1,0:T(8,128)(2,1)S(1)} %get-tuple-element.523), channel_id=1, source_target_pairs={{0,64},{32,96},{64,0},{96,32},{8,72},{40,104},{72,8},{104,40},{16,... | collective-permute-start | bytes 983048 | tf_op jit(solution)/shard_map/ppermute | solution.py:31
  284.9 17.9 %collective-permute-start.101 = (bf16[64,2560]{1,0:T(8,128)(2,1)S(1)}, bf16[64,2560]{1,0:T(8,128)(2,1)S(1)}, u32[]{:S(2)}, u32[]{:S(2)}) collective-permute-start(bf16[64,2560]{1,0:T(8,128)(2,1)S(1)} %shard_map.143.refs_0_), channel_id=1, source_target_pairs={{0,96},{32,0},{64,32},{96,64},{1,97},{33,1},{65,33},{97,65},{2,98}... | collective-permute-start | bytes 983048 | tf_op jit(solution)/shard_map/ppermute | solution.py:19
  294.3 15.2 %collective-permute-start.102 = (bf16[64,2560]{1,0:T(8,128)(2,1)S(1)}, bf16[64,2560]{1,0:T(8,128)(2,1)S(1)}, u32[]{:S(2)}, u32[]{:S(2)}) collective-permute-start(bf16[64,2560]{1,0:T(8,128)(2,1)S(1)} %shard_map.143.refs_0_), channel_id=1, source_target_pairs={{0,64},{32,96},{64,0},{96,32},{1,65},{33,97},{65,1},{97,33},{2,66}... | collective-permute-start | bytes 983048 | tf_op jit(solution)/shard_map/ppermute | solution.py:19
  294.3 15.7 %collective-permute-start.103 = (bf16[64,2560]{1,0:T(8,128)(2,1)S(1)}, bf16[64,2560]{1,0:T(8,128)(2,1)S(1)}, u32[]{:S(2)}, u32[]{:S(2)}) collective-permute-start(bf16[64,2560]{1,0:T(8,128)(2,1)S(1)} %shard_map.143.refs_0_), channel_id=1, source_target_pairs={{0,32},{32,64},{64,96},{96,0},{1,33},{33,65},{65,97},{97,1},{2,34}... | collective-permute-start | bytes 983048 | tf_op jit(solution)/shard_map/ppermute | solution.py:19
  302.8 23.2 %collective-permute-start.56 = (bf16[128,1280]{1,0:T(8,128)(2,1)S(1)}, bf16[128,1280]{1,0:T(8,128)(2,1)S(1)}, u32[]{:S(2)}, u32[]{:S(2)}) collective-permute-start(bf16[128,1280]{1,0:T(8,128)(2,1)S(1)} %get-tuple-element.522), channel_id=1, source_target_pairs={{0,32},{32,64},{64,96},{96,0},{8,40},{40,72},{72,104},{104,8},{16,... | collective-permute-start | bytes 983048 | tf_op jit(solution)/shard_map/ppermute | solution.py:31
  314.8 16.0 %collective-permute-start.104 = (bf16[32,1280]{1,0:T(8,128)(2,1)S(1)}, bf16[32,1280]{1,0:T(8,128)(2,1)S(1)}, u32[]{:S(2)}, u32[]{:S(2)}) collective-permute-start(bf16[32,1280]{1,0:T(8,128)(2,1)S(1)} %get-tuple-element.385), channel_id=1, source_target_pairs={{8,0},{9,1},{10,2},{11,3},{12,4},{13,5},{14,6},{15,7},{16,8},{17,9... | collective-permute-start | bytes 245768 | tf_op jit(solution)/shard_map/ppermute | solution.py:48
  345.1 21.9 %collective-permute-start.120 = (bf16[128,1280]{1,0:T(8,128)(2,1)S(1)}, bf16[128,1280]{1,0:T(8,128)(2,1)S(1)}, u32[]{:S(2)}, u32[]{:S(2)}) collective-permute-start(bf16[128,1280]{1,0:T(8,128)(2,1)S(1)} %get-tuple-element.519), channel_id=1, source_target_pairs={{0,32},{32,64},{64,96},{96,0},{1,33},{33,65},{65,97},{97,1},{2,34}... | collective-permute-start | bytes 983048 | tf_op jit(solution)/shard_map/ppermute | solution.py:19
  346.0 20.9 %collective-permute-start.121 = (bf16[128,1280]{1,0:T(8,128)(2,1)S(1)}, bf16[128,1280]{1,0:T(8,128)(2,1)S(1)}, u32[]{:S(2)}, u32[]{:S(2)}) collective-permute-start(bf16[128,1280]{1,0:T(8,128)(2,1)S(1)} %get-tuple-element.518), channel_id=1, source_target_pairs={{0,64},{32,96},{64,0},{96,32},{1,65},{33,97},{65,1},{97,33},{2,66}... | collective-permute-start | bytes 983048 | tf_op jit(solution)/shard_map/ppermute | solution.py:19
  349.7 17.2 %collective-permute-start.122 = (bf16[128,1280]{1,0:T(8,128)(2,1)S(1)}, bf16[128,1280]{1,0:T(8,128)(2,1)S(1)}, u32[]{:S(2)}, u32[]{:S(2)}) collective-permute-start(bf16[128,1280]{1,0:T(8,128)(2,1)S(1)} %get-tuple-element.517), channel_id=1, source_target_pairs={{0,96},{32,0},{64,32},{96,64},{1,97},{33,1},{65,33},{97,65},{2,98}... | collective-permute-start | bytes 983048 | tf_op jit(solution)/shard_map/ppermute | solution.py:19
  383.5 54.2 %collective-permute-start.123 = (bf16[512,1280]{1,0:T(8,128)(2,1)S(1)}, bf16[512,1280]{1,0:T(8,128)(2,1)S(1)}, u32[]{:S(2)}, u32[]{:S(2)}) collective-permute-start(bf16[512,1280]{1,0:T(8,128)(2,1)S(1)} %get-tuple-element.407), channel_id=1, source_target_pairs={{8,0},{16,8},{24,16},{9,1},{17,9},{25,17},{10,2},{18,10},{26,18},{... | collective-permute-start | bytes 3932168 | tf_op jit(solution)/shard_map/ppermute | solution.py:37
  394.3 27.8 %collective-permute-start.130 = (bf16[32,1280]{1,0:T(8,128)(2,1)S(1)}, bf16[32,1280]{1,0:T(8,128)(2,1)S(1)}, u32[]{:S(2)}, u32[]{:S(2)}) collective-permute-start(bf16[32,1280]{1,0:T(8,128)(2,1)S(1)} %get-tuple-element.420), channel_id=1, source_target_pairs={{8,0},{9,1},{10,2},{11,3},{12,4},{13,5},{14,6},{15,7},{16,8},{17,9... | collective-permute-start | bytes 245768 | tf_op jit(solution)/shard_map/ppermute | solution.py:48
  396.2 28.5 %collective-permute-start.131 = (bf16[32,1280]{1,0:T(8,128)(2,1)S(1)}, bf16[32,1280]{1,0:T(8,128)(2,1)S(1)}, u32[]{:S(2)}, u32[]{:S(2)}) collective-permute-start(bf16[32,1280]{1,0:T(8,128)(2,1)S(1)} %get-tuple-element.421), channel_id=1, source_target_pairs={{8,7},{9,0},{10,1},{11,2},{12,3},{13,4},{14,5},{15,6},{16,15},{17,... | collective-permute-start | bytes 245768 | tf_op jit(solution)/shard_map/ppermute | solution.py:48
  398.4 28.3 %collective-permute-start.132 = (bf16[32,1280]{1,0:T(8,128)(2,1)S(1)}, bf16[32,1280]{1,0:T(8,128)(2,1)S(1)}, u32[]{:S(2)}, u32[]{:S(2)}) collective-permute-start(bf16[32,1280]{1,0:T(8,128)(2,1)S(1)} %get-tuple-element.422), channel_id=1, source_target_pairs={{8,6},{9,7},{10,0},{11,1},{12,2},{13,3},{14,4},{15,5},{16,14},{17,... | collective-permute-start | bytes 245768 | tf_op jit(solution)/shard_map/ppermute | solution.py:48
  401.7 28.1 %collective-permute-start.133 = (bf16[32,1280]{1,0:T(8,128)(2,1)S(1)}, bf16[32,1280]{1,0:T(8,128)(2,1)S(1)}, u32[]{:S(2)}, u32[]{:S(2)}) collective-permute-start(bf16[32,1280]{1,0:T(8,128)(2,1)S(1)} %get-tuple-element.423), channel_id=1, source_target_pairs={{8,5},{9,6},{10,7},{11,0},{12,1},{13,2},{14,3},{15,4},{16,13},{17,... | collective-permute-start | bytes 245768 | tf_op jit(solution)/shard_map/ppermute | solution.py:48
  463.4 78.0 %collective-permute-start.161 = (bf16[512,1280]{1,0:T(8,128)(2,1)}, bf16[512,1280]{1,0:T(8,128)(2,1)}, u32[]{:S(2)}, u32[]{:S(2)}) collective-permute-start(bf16[512,1280]{1,0:T(8,128)(2,1)} %get-tuple-element.462), channel_id=1, source_target_pairs={{8,0},{16,8},{24,16},{9,1},{17,9},{25,17},{10,2},{18,10},{26,18},{... | collective-permute-start | bytes 3932168 | tf_op jit(solution)/shard_map/ppermute | solution.py:37
  465.6 31.4 %collective-permute-start.148 = (bf16[64,768]{1,0:T(8,128)(2,1)S(1)}, bf16[64,768]{1,0:T(8,128)(2,1)S(1)}, u32[]{:S(2)}, u32[]{:S(2)}) collective-permute-start(bf16[64,768]{1,0:T(8,128)(2,1)S(1)} %get-tuple-element.450), channel_id=1, source_target_pairs={{0,32},{32,64},{64,96},{96,0},{1,33},{33,65},{65,97},{97,1},{2,34}... | collective-permute-start | bytes 294920 | tf_op jit(solution)/shard_map/ppermute | solution.py:19
  466.1 30.9 %collective-permute-start.149 = (bf16[64,768]{1,0:T(8,128)(2,1)S(1)}, bf16[64,768]{1,0:T(8,128)(2,1)S(1)}, u32[]{:S(2)}, u32[]{:S(2)}) collective-permute-start(bf16[64,768]{1,0:T(8,128)(2,1)S(1)} %get-tuple-element.451), channel_id=1, source_target_pairs={{0,64},{32,96},{64,0},{96,32},{1,65},{33,97},{65,1},{97,33},{2,66}... | collective-permute-start | bytes 294920 | tf_op jit(solution)/shard_map/ppermute | solution.py:19
  469.0 28.0 %collective-permute-start.150 = (bf16[64,768]{1,0:T(8,128)(2,1)S(1)}, bf16[64,768]{1,0:T(8,128)(2,1)S(1)}, u32[]{:S(2)}, u32[]{:S(2)}) collective-permute-start(bf16[64,768]{1,0:T(8,128)(2,1)S(1)} %get-tuple-element.452), channel_id=1, source_target_pairs={{0,96},{32,0},{64,32},{96,64},{1,97},{33,1},{65,33},{97,65},{2,98}... | collective-permute-start | bytes 294920 | tf_op jit(solution)/shard_map/ppermute | solution.py:19
  575.9 65.7 %collective-permute-start.170 = (bf16[128,1280]{1,0:T(8,128)(2,1)S(1)}, bf16[128,1280]{1,0:T(8,128)(2,1)S(1)}, u32[]{:S(2)}, u32[]{:S(2)}) collective-permute-start(bf16[128,1280]{1,0:T(8,128)(2,1)S(1)} %get-tuple-element.512), channel_id=1, source_target_pairs={{0,32},{32,64},{64,96},{96,0},{8,40},{40,72},{72,104},{104,8},{16,... | collective-permute-start | bytes 983048 | tf_op jit(solution)/shard_map/ppermute | solution.py:31
  579.8 61.8 %collective-permute-start.188 = (bf16[128,1280]{1,0:T(8,128)(2,1)S(1)}, bf16[128,1280]{1,0:T(8,128)(2,1)S(1)}, u32[]{:S(2)}, u32[]{:S(2)}) collective-permute-start(bf16[128,1280]{1,0:T(8,128)(2,1)S(1)} %get-tuple-element.510), channel_id=1, source_target_pairs={{0,96},{32,0},{64,32},{96,64},{8,104},{40,8},{72,40},{104,72},{16,... | collective-permute-start | bytes 983048 | tf_op jit(solution)/shard_map/ppermute | solution.py:31
  586.0 14.8 %collective-permute-start.182 = (bf16[64,1664]{1,0:T(8,128)(2,1)S(1)}, bf16[64,1664]{1,0:T(8,128)(2,1)S(1)}, u32[]{:S(2)}, u32[]{:S(2)}) collective-permute-start(bf16[64,1664]{1,0:T(8,128)(2,1)S(1)} %shard_map.156.refs_0_), channel_id=1, source_target_pairs={{0,64},{32,96},{64,0},{96,32},{1,65},{33,97},{65,1},{97,33},{2,66}... | collective-permute-start | bytes 638984 | tf_op jit(solution)/shard_map/ppermute | solution.py:19
  619.0 22.6 %collective-permute-start.187 = (bf16[128,1280]{1,0:T(8,128)(2,1)S(1)}, bf16[128,1280]{1,0:T(8,128)(2,1)S(1)}, u32[]{:S(2)}, u32[]{:S(2)}) collective-permute-start(bf16[128,1280]{1,0:T(8,128)(2,1)S(1)} %get-tuple-element.492), channel_id=1, source_target_pairs={{0,64},{32,96},{64,0},{96,32},{8,72},{40,104},{72,8},{104,40},{16,... | collective-permute-start | bytes 983048 | tf_op jit(solution)/shard_map/ppermute | solution.py:31
  (342 other events, 3561.5 us)

commit v4 on v3

--- a/solution.py
+++ b/solution.py
@@ -491,16 +491,14 @@
             behind_w = behind_weighted()
             _, hit_back, _, _ = spread(ahead, block, slots, 0)
             ahead_t = hit_back.astype(BF)
+            far = ring_in(cut(after(tokens, payload), 2), "dp", 2, lower)
             fills["cut"] = first_cut(after(cotangent, payload), own_r)
         kept, out, blocks = forward_out(gathered, down_w, experts)
         back = [hop_back(blocks[k], 1, k) for k in range(experts)]
         if step == 0:
-            far = ring_in(cut(after(tokens, blocks), 2), "dp", 2, lower)
             base = jnp.concatenate([cut(tokens, 0), begin[groups - 1], far, begin[1]], axis=0)
             state = base
         if step == 1:
-            incoming = jnp.concatenate(narrow(after(cotangent, blocks), lower), axis=0)
-        if step == 2:
             grad0, first0, parts0 = backward_in(after(fills["early"], blocks), down_w, groups)
             parts0 = [ring_in(part, "dp", j + 1, (sections - 1,)) for j, part in enumerate(parts0)]
         saved = keep(step, (slot, gate_pre, up_pre, kept, out, state), saved)
@@ -509,13 +507,13 @@
     slot, gate_pre, up_pre, fwd_state = keep(
         at, (slot, gate_pre, up_pre, state), (saved[0], saved[1], saved[2], saved[5])
     )
-    final = None
-    base, state = incoming, incoming
+    final, base = None, None
     for step in range(sections):
         at = sections - 1 - step
         if step == 0:
             grad = grad0
             payload = backward_act(first0, parts0, gate_pre, up_pre, payload)
+            state = jnp.zeros_like(fwd_state)
         else:
             state, picked = owner(base, back, [ahead_t], send_table, send_r, experts)
             received = to_experts(picked)
@@ -536,6 +534,7 @@
             payload = backward_act(first, parts, gate_pre, up_pre)
         gathered = gather_groups(payload)
         if step == 0:
+            base = jnp.concatenate(narrow(after(cotangent, payload), lower), axis=0)
             kept, out, _ = forward_out(gathered, down_w, experts)
             kept, fwd_out = keep(at, (kept, out), saved[3:5])
         if step == 2:

time: 656 us -> 663 us (1.011)
  local copies, waits for them, and re-layouts: 46.5 us -> 58 us
    unnamed x373 -> x411, local copies, waits for them, and re-layouts: 39.4 us -> 50.9 us
    ppermute x48, waiting for transfers between devices: 41 us -> 50.9 us  [hop_back(): return lax.ppermute(value, ('section', 'expert'), pairs)]
    ppermute x127, waiting for transfers between devices: 159 us -> 151 us  [ring(): lax.ppermute(value, axis, [(i, (i + steps) % count) for i in range(count)])]
  transfers between devices with their start and end apart: 196 -> 196, of which waited for: 81 -> 80; matrix products, arithmetic and copies ran while one was open for 5% -> 5% of each run, Pallas kernels for 4% -> 3%
where the time goes in v4:
time: 663 us; the launch traced here: 652 us
  starting transfers between devices  316 us (48%)
  waiting for transfers between devices  206 us (31%)
  local copies, waits for them, and re-layouts  58 us (9%)
  Pallas kernels  37.1 us (6%)
  matrix products  22.8 us (3%)
  other arithmetic  8.19 us (1%)
    ppermute x127, starting transfers between devices, ring(): lax.ppermute(value, axis, [(i, (i + steps) % count) for i in range(count)])  156 us
    ppermute x127, waiting for transfers between devices, ring(): lax.ppermute(value, axis, [(i, (i + steps) % count) for i in range(count)])  151 us
    ppermute x48, starting transfers between devices, hop_back(): return lax.ppermute(value, ('section', 'expert'), pairs)  101 us
    ppermute x48, waiting for transfers between devices, hop_back(): return lax.ppermute(value, ('section', 'expert'), pairs)  50.9 us
    unnamed x411, local copies, waits for them, and re-layouts  50.9 us
    ppermute x15, starting transfers between devices, ring_in(): lax.ppermute(value, axes, [(at(s, i), at(s, i + steps)) for s in where fo...  39.8 us
    pallas_call x30, Pallas kernels, call(): pl.pallas_call(kernel, out_shape=tuple(outs), in_specs=[pl.BlockSpec(memo...  37.1 us
    dot_general x22, matrix products, mm(): lax.dot_general(a, b, (((ca,), (cb,)), ((), ())), preferred_element_type=...  22.8 us
  transfers between devices with their start and end apart: 196, of which 80 were waited for; matrix products, arithmetic and copies ran while one was open for 5% of the time, Pallas kernels for 3%

profile of v4, /device:TPU:48, one launch (start us, length us, event | category | flops | bytes accessed | tf_op | source)
XLA Modules:
  0.0 652.4 jit_solution(10515476502130162012)
XLA Ops:
  32.5 3.6 collective-permute-start.18
  46.3 5.1 collective-permute-done.14.refs_1_
  60.7 3.8 collective-permute-done.30
  70.4 5.5 collective-permute-done.21.refs_3_
  116.0 6.2 collective-permute-start.57
  135.7 5.3 collective-permute-done.48.refs_2_
  201.3 4.3 collective-permute-start.75
  209.5 5.8 collective-permute-done.76.refs_3_
  258.0 3.8 shard_map.140
  271.8 4.6 collective-permute-start.112
  291.0 5.5 collective-permute-done.97.refs_3_
  306.4 3.9 collective-permute-start.98
  310.4 10.9 %collective-permute-start.99 = (bf16[128,1280]{1,0:T(8,128)(2,1)S(1)}, bf16[128,1280]{1,0:T(8,128)(2,1)S(1)}, u32[]{:S(2)}, u32[]{:S(2)}) collective-permute-start(bf16[128,1280]{1,0:T(8,128)(2,1)S(1)} %get-tuple-element.523), channel_id=1, source_target_pairs={{0,64},{32,96},{64,0},{96,32},{8,72},{40,104},{72,8},{104,40},{16,... | collective-permute-start | bytes 983048 | tf_op jit(solution)/shard_map/ppermute | solution.py:31
  332.5 3.9 collective-permute-start.106
  358.9 4.6 collective-permute-done.114.refs_2_
  365.6 3.9 collective-permute-done.116.refs_4_
  394.2 5.0 collective-permute-done.128.refs_2_
  411.3 19.5 %collective-permute-done.130.refs_1_ = bf16[32,1280]{1,0:T(8,128)(2,1)S(1)} collective-permute-done((bf16[32,1280]{1,0:T(8,128)(2,1)S(1)}, bf16[32,1280]{1,0:T(8,128)(2,1)S(1)}, u32[]{:S(2)}, u32[]{:S(2)}) %collective-permute-start.130) | collective-permute-done | bytes 81952 | tf_op jit(solution)/shard_map/ppermute | solution.py:48
  478.3 3.8 collective-permute-done.155
  482.3 4.4 collective-permute-done.156
  487.0 5.7 collective-permute-done.157
  492.7 5.5 collective-permute-done.158
  498.5 5.8 collective-permute-done.159
  512.3 4.4 collective-permute-done.152.refs_2_
  521.7 3.7 collective-permute-start.163
  561.6 4.2 fusion.4
  584.2 3.9 collective-permute-start.170
  597.6 7.0 %collective-permute-done.181.refs_1_ = bf16[64,1664]{1,0:T(8,128)(2,1)S(1)} collective-permute-done((bf16[64,1664]{1,0:T(8,128)(2,1)S(1)}, bf16[64,1664]{1,0:T(8,128)(2,1)S(1)}, u32[]{:S(2)}, u32[]{:S(2)}) %collective-permute-start.181) | collective-permute-done | bytes 213024 | tf_op jit(solution)/shard_map/ppermute | solution.py:19
  626.1 4.6 collective-permute-start.187
  631.5 4.4 collective-permute-done.190
  636.9 5.8 collective-permute-done.192
  643.3 5.4 collective-permute-done.194
  (886 shorter events, 474.0 us)
Async XLA Ops:
  32.5 49.6 %collective-permute-start.18 = (bf16[128,1280]{1,0:T(8,128)(2,1)S(1)}, bf16[128,1280]{1,0:T(8,128)(2,1)S(1)}, u32[]{:S(2)}, u32[]{:S(2)}) collective-permute-start(bf16[128,1280]{1,0:T(8,128)(2,1)S(1)} %get-tuple-element.526), channel_id=1, source_target_pairs={{0,32},{32,64},{64,96},{96,0},{8,40},{40,72},{72,104},{104,8},{16,... | collective-permute-start | bytes 983048 | tf_op jit(solution)/shard_map/ppermute | solution.py:31
  36.1 48.2 %collective-permute-start.3 = (bf16[128,1280]{1,0:T(8,128)(2,1)S(1)}, bf16[128,1280]{1,0:T(8,128)(2,1)S(1)}, u32[]{:S(2)}, u32[]{:S(2)}) collective-permute-start(bf16[128,1280]{1,0:T(8,128)(2,1)S(1)} %get-tuple-element.525), channel_id=1, source_target_pairs={{0,96},{32,0},{64,32},{96,64},{8,104},{40,8},{72,40},{104,72},{16,... | collective-permute-start | bytes 983048 | tf_op jit(solution)/shard_map/ppermute | solution.py:31
  67.5 24.7 %collective-permute-start.17 = (bf16[128,1280]{1,0:T(8,128)(2,1)S(1)}, bf16[128,1280]{1,0:T(8,128)(2,1)S(1)}, u32[]{:S(2)}, u32[]{:S(2)}) collective-permute-start(bf16[128,1280]{1,0:T(8,128)(2,1)S(1)} %constant_dynamic-slice_fusion.9), channel_id=1, source_target_pairs={{0,64},{32,96},{64,0},{96,32},{8,72},{40,104},{72,8},{104,40},{16,... | collective-permute-start | bytes 983048 | tf_op jit(solution)/shard_map/ppermute | solution.py:31
  114.5 14.5 %collective-permute-start.46 = (bf16[64,1280]{1,0:T(8,128)(2,1)S(1)}, bf16[64,1280]{1,0:T(8,128)(2,1)S(1)}, u32[]{:S(2)}, u32[]{:S(2)}) collective-permute-start(bf16[64,1280]{1,0:T(8,128)(2,1)S(1)} %get-tuple-element.567), channel_id=1, source_target_pairs={{24,56},{56,88},{88,120},{120,24},{25,57},{57,89},{89,121},{121,25... | collective-permute-start | bytes 491528 | tf_op jit(solution)/shard_map/ppermute | solution.py:31
  116.0 66.5 %collective-permute-start.57 = (bf16[512,1280]{1,0:T(8,128)(2,1)S(1)}, bf16[512,1280]{1,0:T(8,128)(2,1)S(1)}, u32[]{:S(2)}, u32[]{:S(2)}) collective-permute-start(bf16[512,1280]{1,0:T(8,128)(2,1)S(1)} %get-tuple-element.332), channel_id=1, source_target_pairs={{0,8},{8,16},{16,24},{1,9},{9,17},{17,25},{2,10},{10,18},{18,26},{... | collective-permute-start | bytes 3932168 | tf_op jit(solution)/shard_map/ppermute | solution.py:37
  123.5 18.2 %collective-permute-start.38 = (bf16[64,1664]{1,0:T(8,128)(2,1)S(1)}, bf16[64,1664]{1,0:T(8,128)(2,1)S(1)}, u32[]{:S(2)}, u32[]{:S(2)}) collective-permute-start(bf16[64,1664]{1,0:T(8,128)(2,1)S(1)} %get-tuple-element.291), channel_id=1, source_target_pairs={{0,32},{32,64},{64,96},{96,0},{1,33},{33,65},{65,97},{97,1},{2,34}... | collective-permute-start | bytes 638984 | tf_op jit(solution)/shard_map/ppermute | solution.py:19
  124.1 18.1 %collective-permute-start.39 = (bf16[64,1664]{1,0:T(8,128)(2,1)S(1)}, bf16[64,1664]{1,0:T(8,128)(2,1)S(1)}, u32[]{:S(2)}, u32[]{:S(2)}) collective-permute-start(bf16[64,1664]{1,0:T(8,128)(2,1)S(1)} %get-tuple-element.292), channel_id=1, source_target_pairs={{0,64},{32,96},{64,0},{96,32},{1,65},{33,97},{65,1},{97,33},{2,66}... | collective-permute-start | bytes 638984 | tf_op jit(solution)/shard_map/ppermute | solution.py:19
  127.6 17.5 %collective-permute-start.40 = (bf16[64,1664]{1,0:T(8,128)(2,1)S(1)}, bf16[64,1664]{1,0:T(8,128)(2,1)S(1)}, u32[]{:S(2)}, u32[]{:S(2)}) collective-permute-start(bf16[64,1664]{1,0:T(8,128)(2,1)S(1)} %get-tuple-element.293), channel_id=1, source_target_pairs={{0,96},{32,0},{64,32},{96,64},{1,97},{33,1},{65,33},{97,65},{2,98}... | collective-permute-start | bytes 638984 | tf_op jit(solution)/shard_map/ppermute | solution.py:19
  184.9 71.2 %collective-permute-start.66 = (bf16[512,1280]{1,0:T(8,128)(2,1)S(1)}, bf16[512,1280]{1,0:T(8,128)(2,1)}, u32[]{:S(2)}, u32[]{:S(2)}) collective-permute-start(bf16[512,1280]{1,0:T(8,128)(2,1)S(1)} %get-tuple-element.333), channel_id=1, source_target_pairs={{0,8},{8,16},{16,24},{1,9},{9,17},{17,25},{2,10},{10,18},{18,26},{... | collective-permute-start | bytes 3932168 | tf_op jit(solution)/shard_map/ppermute | solution.py:37
  271.8 14.6 %collective-permute-start.112 = (bf16[512,16]{0,1:T(8,128)(2,1)S(1)}, bf16[512,16]{0,1:T(8,128)(2,1)S(1)}, u32[]{:S(2)}, u32[]{:S(2)}) collective-permute-start(bf16[512,16]{0,1:T(8,128)(2,1)S(1)} %convert.18), channel_id=1, source_target_pairs={{8,0},{16,8},{24,16},{9,1},{17,9},{25,17},{10,2},{18,10},{26,18},{... | collective-permute-start | bytes 49160 | tf_op jit(solution)/shard_map/ppermute | solution.py:37
  298.5 22.7 %collective-permute-start.102 = (bf16[64,2560]{1,0:T(8,128)(2,1)S(1)}, bf16[64,2560]{1,0:T(8,128)(2,1)S(1)}, u32[]{:S(2)}, u32[]{:S(2)}) collective-permute-start(bf16[64,2560]{1,0:T(8,128)(2,1)S(1)} %shard_map.143.refs_0_), channel_id=1, source_target_pairs={{0,64},{32,96},{64,0},{96,32},{1,65},{33,97},{65,1},{97,33},{2,66}... | collective-permute-start | bytes 983048 | tf_op jit(solution)/shard_map/ppermute | solution.py:19
  300.5 20.8 %collective-permute-start.103 = (bf16[64,2560]{1,0:T(8,128)(2,1)S(1)}, bf16[64,2560]{1,0:T(8,128)(2,1)S(1)}, u32[]{:S(2)}, u32[]{:S(2)}) collective-permute-start(bf16[64,2560]{1,0:T(8,128)(2,1)S(1)} %shard_map.143.refs_0_), channel_id=1, source_target_pairs={{0,32},{32,64},{64,96},{96,0},{1,33},{33,65},{65,97},{97,1},{2,34}... | collective-permute-start | bytes 983048 | tf_op jit(solution)/shard_map/ppermute | solution.py:19
  304.5 28.0 %collective-permute-start.100 = (bf16[128,1280]{1,0:T(8,128)(2,1)S(1)}, bf16[128,1280]{1,0:T(8,128)(2,1)S(1)}, u32[]{:S(2)}, u32[]{:S(2)}) collective-permute-start(bf16[128,1280]{1,0:T(8,128)(2,1)S(1)} %get-tuple-element.522), channel_id=1, source_target_pairs={{0,32},{32,64},{64,96},{96,0},{8,40},{40,72},{72,104},{104,8},{16,... | collective-permute-start | bytes 983048 | tf_op jit(solution)/shard_map/ppermute | solution.py:31
  306.4 30.7 %collective-permute-start.98 = (bf16[128,1280]{1,0:T(8,128)(2,1)S(1)}, bf16[128,1280]{1,0:T(8,128)(2,1)S(1)}, u32[]{:S(2)}, u32[]{:S(2)}) collective-permute-start(bf16[128,1280]{1,0:T(8,128)(2,1)S(1)} %get-tuple-element.524), channel_id=1, source_target_pairs={{0,96},{32,0},{64,32},{96,64},{8,104},{40,8},{72,40},{104,72},{16,... | collective-permute-start | bytes 983048 | tf_op jit(solution)/shard_map/ppermute | solution.py:31
  310.4 28.7 %collective-permute-start.99 = (bf16[128,1280]{1,0:T(8,128)(2,1)S(1)}, bf16[128,1280]{1,0:T(8,128)(2,1)S(1)}, u32[]{:S(2)}, u32[]{:S(2)}) collective-permute-start(bf16[128,1280]{1,0:T(8,128)(2,1)S(1)} %get-tuple-element.523), channel_id=1, source_target_pairs={{0,64},{32,96},{64,0},{96,32},{8,72},{40,104},{72,8},{104,40},{16,... | collective-permute-start | bytes 983048 | tf_op jit(solution)/shard_map/ppermute | solution.py:31
  355.2 18.8 %collective-permute-start.120 = (bf16[128,1280]{1,0:T(8,128)(2,1)S(1)}, bf16[128,1280]{1,0:T(8,128)(2,1)S(1)}, u32[]{:S(2)}, u32[]{:S(2)}) collective-permute-start(bf16[128,1280]{1,0:T(8,128)(2,1)S(1)} %get-tuple-element.519), channel_id=1, source_target_pairs={{0,32},{32,64},{64,96},{96,0},{1,33},{33,65},{65,97},{97,1},{2,34}... | collective-permute-start | bytes 983048 | tf_op jit(solution)/shard_map/ppermute | solution.py:19
  355.2 18.8 %collective-permute-start.121 = (bf16[128,1280]{1,0:T(8,128)(2,1)S(1)}, bf16[128,1280]{1,0:T(8,128)(2,1)S(1)}, u32[]{:S(2)}, u32[]{:S(2)}) collective-permute-start(bf16[128,1280]{1,0:T(8,128)(2,1)S(1)} %get-tuple-element.518), channel_id=1, source_target_pairs={{0,64},{32,96},{64,0},{96,32},{1,65},{33,97},{65,1},{97,33},{2,66}... | collective-permute-start | bytes 983048 | tf_op jit(solution)/shard_map/ppermute | solution.py:19
  355.6 18.5 %collective-permute-start.122 = (bf16[128,1280]{1,0:T(8,128)(2,1)S(1)}, bf16[128,1280]{1,0:T(8,128)(2,1)S(1)}, u32[]{:S(2)}, u32[]{:S(2)}) collective-permute-start(bf16[128,1280]{1,0:T(8,128)(2,1)S(1)} %get-tuple-element.517), channel_id=1, source_target_pairs={{0,96},{32,0},{64,32},{96,64},{1,97},{33,1},{65,33},{97,65},{2,98}... | collective-permute-start | bytes 983048 | tf_op jit(solution)/shard_map/ppermute | solution.py:19
  392.2 54.0 %collective-permute-start.123 = (bf16[512,1280]{1,0:T(8,128)(2,1)S(1)}, bf16[512,1280]{1,0:T(8,128)(2,1)S(1)}, u32[]{:S(2)}, u32[]{:S(2)}) collective-permute-start(bf16[512,1280]{1,0:T(8,128)(2,1)S(1)} %get-tuple-element.407), channel_id=1, source_target_pairs={{8,0},{16,8},{24,16},{9,1},{17,9},{25,17},{10,2},{18,10},{26,18},{... | collective-permute-start | bytes 3932168 | tf_op jit(solution)/shard_map/ppermute | solution.py:37
  402.4 28.4 %collective-permute-start.130 = (bf16[32,1280]{1,0:T(8,128)(2,1)S(1)}, bf16[32,1280]{1,0:T(8,128)(2,1)S(1)}, u32[]{:S(2)}, u32[]{:S(2)}) collective-permute-start(bf16[32,1280]{1,0:T(8,128)(2,1)S(1)} %get-tuple-element.420), channel_id=1, source_target_pairs={{8,0},{9,1},{10,2},{11,3},{12,4},{13,5},{14,6},{15,7},{16,8},{17,9... | collective-permute-start | bytes 245768 | tf_op jit(solution)/shard_map/ppermute | solution.py:48
  404.3 29.2 %collective-permute-start.131 = (bf16[32,1280]{1,0:T(8,128)(2,1)S(1)}, bf16[32,1280]{1,0:T(8,128)(2,1)S(1)}, u32[]{:S(2)}, u32[]{:S(2)}) collective-permute-start(bf16[32,1280]{1,0:T(8,128)(2,1)S(1)} %get-tuple-element.421), channel_id=1, source_target_pairs={{8,7},{9,0},{10,1},{11,2},{12,3},{13,4},{14,5},{15,6},{16,15},{17,... | collective-permute-start | bytes 245768 | tf_op jit(solution)/shard_map/ppermute | solution.py:48
  406.2 29.2 %collective-permute-start.132 = (bf16[32,1280]{1,0:T(8,128)(2,1)S(1)}, bf16[32,1280]{1,0:T(8,128)(2,1)S(1)}, u32[]{:S(2)}, u32[]{:S(2)}) collective-permute-start(bf16[32,1280]{1,0:T(8,128)(2,1)S(1)} %get-tuple-element.422), channel_id=1, source_target_pairs={{8,6},{9,7},{10,0},{11,1},{12,2},{13,3},{14,4},{15,5},{16,14},{17,... | collective-permute-start | bytes 245768 | tf_op jit(solution)/shard_map/ppermute | solution.py:48
  409.2 29.1 %collective-permute-start.133 = (bf16[32,1280]{1,0:T(8,128)(2,1)S(1)}, bf16[32,1280]{1,0:T(8,128)(2,1)S(1)}, u32[]{:S(2)}, u32[]{:S(2)}) collective-permute-start(bf16[32,1280]{1,0:T(8,128)(2,1)S(1)} %get-tuple-element.423), channel_id=1, source_target_pairs={{8,5},{9,6},{10,7},{11,0},{12,1},{13,2},{14,3},{15,4},{16,13},{17,... | collective-permute-start | bytes 245768 | tf_op jit(solution)/shard_map/ppermute | solution.py:48
  471.8 75.4 %collective-permute-start.161 = (bf16[512,1280]{1,0:T(8,128)(2,1)}, bf16[512,1280]{1,0:T(8,128)(2,1)}, u32[]{:S(2)}, u32[]{:S(2)}) collective-permute-start(bf16[512,1280]{1,0:T(8,128)(2,1)} %get-tuple-element.462), channel_id=1, source_target_pairs={{8,0},{16,8},{24,16},{9,1},{17,9},{25,17},{10,2},{18,10},{26,18},{... | collective-permute-start | bytes 3932168 | tf_op jit(solution)/shard_map/ppermute | solution.py:37
  474.0 30.2 %collective-permute-start.148 = (bf16[64,768]{1,0:T(8,128)(2,1)S(1)}, bf16[64,768]{1,0:T(8,128)(2,1)S(1)}, u32[]{:S(2)}, u32[]{:S(2)}) collective-permute-start(bf16[64,768]{1,0:T(8,128)(2,1)S(1)} %get-tuple-element.450), channel_id=1, source_target_pairs={{0,32},{32,64},{64,96},{96,0},{1,33},{33,65},{65,97},{97,1},{2,34}... | collective-permute-start | bytes 294920 | tf_op jit(solution)/shard_map/ppermute | solution.py:19
  474.7 29.5 %collective-permute-start.149 = (bf16[64,768]{1,0:T(8,128)(2,1)S(1)}, bf16[64,768]{1,0:T(8,128)(2,1)S(1)}, u32[]{:S(2)}, u32[]{:S(2)}) collective-permute-start(bf16[64,768]{1,0:T(8,128)(2,1)S(1)} %get-tuple-element.451), channel_id=1, source_target_pairs={{0,64},{32,96},{64,0},{96,32},{1,65},{33,97},{65,1},{97,33},{2,66}... | collective-permute-start | bytes 294920 | tf_op jit(solution)/shard_map/ppermute | solution.py:19
  476.8 27.4 %collective-permute-start.150 = (bf16[64,768]{1,0:T(8,128)(2,1)S(1)}, bf16[64,768]{1,0:T(8,128)(2,1)S(1)}, u32[]{:S(2)}, u32[]{:S(2)}) collective-permute-start(bf16[64,768]{1,0:T(8,128)(2,1)S(1)} %get-tuple-element.452), channel_id=1, source_target_pairs={{0,96},{32,0},{64,32},{96,64},{1,97},{33,1},{65,33},{97,65},{2,98}... | collective-permute-start | bytes 294920 | tf_op jit(solution)/shard_map/ppermute | solution.py:19
  584.2 64.6 %collective-permute-start.170 = (bf16[128,1280]{1,0:T(8,128)(2,1)S(1)}, bf16[128,1280]{1,0:T(8,128)(2,1)S(1)}, u32[]{:S(2)}, u32[]{:S(2)}) collective-permute-start(bf16[128,1280]{1,0:T(8,128)(2,1)S(1)} %get-tuple-element.512), channel_id=1, source_target_pairs={{0,32},{32,64},{64,96},{96,0},{8,40},{40,72},{72,104},{104,8},{16,... | collective-permute-start | bytes 983048 | tf_op jit(solution)/shard_map/ppermute | solution.py:31
  588.1 60.6 %collective-permute-start.188 = (bf16[128,1280]{1,0:T(8,128)(2,1)S(1)}, bf16[128,1280]{1,0:T(8,128)(2,1)S(1)}, u32[]{:S(2)}, u32[]{:S(2)}) collective-permute-start(bf16[128,1280]{1,0:T(8,128)(2,1)S(1)} %get-tuple-element.510), channel_id=1, source_target_pairs={{0,96},{32,0},{64,32},{96,64},{8,104},{40,8},{72,40},{104,72},{16,... | collective-permute-start | bytes 983048 | tf_op jit(solution)/shard_map/ppermute | solution.py:31
  593.6 14.5 %collective-permute-start.182 = (bf16[64,1664]{1,0:T(8,128)(2,1)S(1)}, bf16[64,1664]{1,0:T(8,128)(2,1)S(1)}, u32[]{:S(2)}, u32[]{:S(2)}) collective-permute-start(bf16[64,1664]{1,0:T(8,128)(2,1)S(1)} %shard_map.156.refs_0_), channel_id=1, source_target_pairs={{0,64},{32,96},{64,0},{96,32},{1,65},{33,97},{65,1},{97,33},{2,66}... | collective-permute-start | bytes 638984 | tf_op jit(solution)/shard_map/ppermute | solution.py:19
  593.9 14.3 %collective-permute-start.183 = (bf16[64,1664]{1,0:T(8,128)(2,1)S(1)}, bf16[64,1664]{1,0:T(8,128)(2,1)S(1)}, u32[]{:S(2)}, u32[]{:S(2)}) collective-permute-start(bf16[64,1664]{1,0:T(8,128)(2,1)S(1)} %shard_map.156.refs_0_), channel_id=1, source_target_pairs={{0,32},{32,64},{64,96},{96,0},{1,33},{33,65},{65,97},{97,1},{2,34}... | collective-permute-start | bytes 638984 | tf_op jit(solution)/shard_map/ppermute | solution.py:19
  626.1 22.6 %collective-permute-start.187 = (bf16[128,1280]{1,0:T(8,128)(2,1)S(1)}, bf16[128,1280]{1,0:T(8,128)(2,1)S(1)}, u32[]{:S(2)}, u32[]{:S(2)}) collective-permute-start(bf16[128,1280]{1,0:T(8,128)(2,1)S(1)} %get-tuple-element.492), channel_id=1, source_target_pairs={{0,64},{32,96},{64,0},{96,32},{8,72},{40,104},{72,8},{104,40},{16,... | collective-permute-start | bytes 983048 | tf_op jit(solution)/shard_map/ppermute | solution.py:31
  (361 other events, 3525.2 us)

commit v5 on v4

--- a/solution.py
+++ b/solution.py
@@ -448,7 +448,10 @@
     def own_rows(parts):
         whole = absolute(parts)
         blocks = [whole[k * CAP : (k + 1) * CAP] for k in range(experts)]
-        return jnp.concatenate([blocks[0]] + [ring(blocks[k], "expert", -k) for k in range(1, experts)], axis=0)
+        return blocks[:1] + send_back(blocks, 1, experts)
+
+    def send_back(blocks, first, last):
+        return [ring(blocks[k], "expert", -k) for k in range(first, last)]
 
     def finish(base, rows_back, tables):
         return (base.astype(F32) + sum(mm(t, rows_back) for t in tables)).astype(BF)
@@ -483,7 +486,8 @@
             break
         gathered = gather_groups(payload)
         if step == 1:
-            gathered, fills["early"] = lax.optimization_barrier((gathered, fills["early"]))
+            grad0, first0, parts0 = backward_in(after(fills["early"], payload), down_w, groups)
+            parts0 = [ring_in(part, "dp", j + 1, (sections - 1,)) for j, part in enumerate(parts0)]
         if step == 0:
             codes = after(here, payload)
             behind, ahead = hop(codes, 1), hop(codes, -1)
@@ -498,9 +502,6 @@
         if step == 0:
             base = jnp.concatenate([cut(tokens, 0), begin[groups - 1], far, begin[1]], axis=0)
             state = base
-        if step == 1:
-            grad0, first0, parts0 = backward_in(after(fills["early"], blocks), down_w, groups)
-            parts0 = [ring_in(part, "dp", j + 1, (sections - 1,)) for j, part in enumerate(parts0)]
         saved = keep(step, (slot, gate_pre, up_pre, kept, out, state), saved)
 
     at = sections - 1
@@ -522,14 +523,16 @@
             else:
                 turn_back = jnp.where(section == at, state, final[-1])
                 turn_back = [turn_back[j * rows : (j + 1) * rows] for j in range(groups)]
-                near_parts = {j: ring_in(turn_back[j], "dp", j, lower) for j in (1, 3)}
+                near_parts = {j: ring_in(turn_back[j], "dp", j, lower) for j in (2, 3)}
             if step == 1:
                 received, fills["base"] = lax.optimization_barrier((received, fills["base"]))
             if step == 2:
                 received, fills["out"] = lax.optimization_barrier((received, fills["out"]))
             grad, first, parts = backward_in(received, down_w, groups)
             if step == 2:
-                rows_back = own_rows(after(fills["out"], parts))
+                whole = absolute(after(fills["out"], parts))
+                blocks = [whole[k * CAP : (k + 1) * CAP] for k in range(experts)]
+                rows_back = blocks[:1] + send_back(blocks, 1, experts // 2)
             parts = reduce_groups(parts)
             payload = backward_act(first, parts, gate_pre, up_pre)
         gathered = gather_groups(payload)
@@ -538,7 +541,7 @@
             kept, out, _ = forward_out(gathered, down_w, experts)
             kept, fwd_out = keep(at, (kept, out), saved[3:5])
         if step == 2:
-            gathered, rows_back = lax.optimization_barrier((gathered, rows_back))
+            rows_back += send_back(after(blocks, payload), experts // 2, experts)
         grads, given, blocks = backward_out(gathered, kept, slot, gain, gate_w, up_w, experts, model)
         if step + 1 < sections:
             if step == 0:
@@ -550,14 +553,14 @@
         final = keep(at, (grad, grads, given, state), final)
 
     layer_base = jnp.where(section == 0, tokens, absolute(fills["base"]))
-    layer_result = finish(layer_base, rows_back, own_w)
+    layer_result = finish(layer_base, jnp.concatenate(rows_back, axis=0), own_w)
     grad, grads, given, state = final
     last_parts = own_parts(given)
     last_back = own_rows(last_parts)
-    far_part = ring_in(after(turn_back[2], last_parts), "dp", 2, lower)
-    last = absolute([turn_back[0], near_parts[1], far_part, near_parts[3]])
+    far_part = ring_in(after(turn_back[1], last_parts), "dp", 1, lower)
+    last = absolute([turn_back[0], far_part, near_parts[2], near_parts[3]])
     last = jnp.where(section == sections - 1, cotangent, last)
-    grad_in = finish(last, last_back, [own_back])
+    grad_in = finish(last, jnp.concatenate(last_back, axis=0), [own_back])
     inv_all = from_lanes(kept, hidden)
     normed = (slot.astype(F32) * inv_all * gain).astype(BF)
     down_grad = mm(kept[:, :hidden], grad, 0, 0).astype(BF)

time: 663 us -> 656 us (0.989)
  the two profiles are of different devices: /device:TPU:48 before, /device:TPU:1 now
where the time goes in v5:
time: 656 us; the launch traced here: 644 us
  starting transfers between devices  313 us (48%)
  waiting for transfers between devices  191 us (29%)
  local copies, waits for them, and re-layouts  63.2 us (10%)
  Pallas kernels  39.9 us (6%)
  matrix products  23.5 us (4%)
  other arithmetic  8.76 us (1%)
    ppermute x127, starting transfers between devices, ring(): lax.ppermute(value, axis, [(i, (i + steps) % count) for i in range(count)])  165 us
    ppermute x127, waiting for transfers between devices, ring(): lax.ppermute(value, axis, [(i, (i + steps) % count) for i in range(count)])  142 us
    ppermute x48, starting transfers between devices, hop_back(): return lax.ppermute(value, ('section', 'expert'), pairs)  98.1 us
    unnamed x417, local copies, waits for them, and re-layouts  56 us
    ppermute x48, waiting for transfers between devices, hop_back(): return lax.ppermute(value, ('section', 'expert'), pairs)  44.8 us
    pallas_call x30, Pallas kernels, call(): pl.pallas_call(kernel, out_shape=tuple(outs), in_specs=[pl.BlockSpec(memo...  39.9 us
    ppermute x15, starting transfers between devices, ring_in(): lax.ppermute(value, axes, [(at(s, i), at(s, i + steps)) for s in where fo...  31.9 us
    dot_general x22, matrix products, mm(): lax.dot_general(a, b, (((ca,), (cb,)), ((), ())), preferred_element_type=...  23.5 us
  transfers between devices with their start and end apart: 196, of which 77 were waited for; matrix products, arithmetic and copies ran while one was open for 5% of the time, Pallas kernels for 4%

profile of v5, /device:TPU:1, one launch (start us, length us, event | category | flops | bytes accessed | tf_op | source)
XLA Modules:
  0.0 644.2 jit_solution(12783041350774000023)
XLA Ops:
  33.0 5.0 collective-permute-start.19
  46.5 12.7 %collective-permute-done.13.refs_1_ = bf16[64,1664]{1,0:T(8,128)(2,1)S(1)} collective-permute-done((bf16[64,1664]{1,0:T(8,128)(2,1)S(1)}, bf16[64,1664]{1,0:T(8,128)(2,1)S(1)}, u32[]{:S(2)}, u32[]{:S(2)}) %collective-permute-start.13) | collective-permute-done | bytes 213024 | tf_op jit(solution)/shard_map/ppermute | solution.py:19
  73.7 3.6 collective-permute-start.25
  77.3 5.7 collective-permute-start.26
  101.1 6.1 collective-permute-start.54
  114.2 3.9 collective-permute-done.36.refs_3_
  118.0 3.8 collective-permute-done.40.refs_7_
  132.2 5.2 collective-permute-done.49.refs_2_
  188.6 4.9 collective-permute-start.66
  210.2 5.5 collective-permute-done.75.refs_2_
  234.1 4.1 collective-permute-start.81
  238.2 8.2 %collective-permute-start.82 = (bf16[32,1280]{1,0:T(8,128)(2,1)S(1)}, bf16[32,1280]{1,0:T(8,128)(2,1)S(1)}, u32[]{:S(2)}, u32[]{:S(2)}) collective-permute-start(bf16[32,1280]{1,0:T(8,128)(2,1)S(1)} %get-tuple-element.324), channel_id=1, source_target_pairs={{0,14},{1,15},{2,8},{3,9},{4,10},{5,11},{6,12},{7,13},{8,22},{9,23... | collective-permute-start | bytes 245768 | tf_op jit(solution)/shard_map/ppermute | solution.py:48
  270.9 4.0 shard_map.140
  302.8 4.8 collective-permute-done.96.refs_2_
  319.3 3.8 collective-permute-start.98
  346.9 3.7 collective-permute-done.107.refs_4_
  375.3 3.7 collective-permute-done.119.refs_7_
  402.5 4.4 collective-permute-done.128.refs_2_
  418.1 9.2 %collective-permute-done.130.refs_1_ = bf16[32,1280]{1,0:T(8,128)(2,1)S(1)} collective-permute-done((bf16[32,1280]{1,0:T(8,128)(2,1)S(1)}, bf16[32,1280]{1,0:T(8,128)(2,1)S(1)}, u32[]{:S(2)}, u32[]{:S(2)}) %collective-permute-start.130) | collective-permute-done | bytes 81952 | tf_op jit(solution)/shard_map/ppermute | solution.py:48
  434.9 5.3 collective-permute-done.135.refs_6_
  469.7 5.1 collective-permute-start.150
  484.2 4.3 collective-permute-done.155
  488.5 5.2 collective-permute-done.156
  540.2 4.0 collective-permute-start.171
  544.2 4.6 fusion.4
  566.4 3.8 collective-permute-start.187
  576.0 8.9 %collective-permute-done.182.refs_3_ = bf16[64,1664]{1,0:T(8,128)(2,1)S(1)} collective-permute-done((bf16[64,1664]{1,0:T(8,128)(2,1)S(1)}, bf16[64,1664]{1,0:T(8,128)(2,1)S(1)}, u32[]{:S(2)}, u32[]{:S(2)}) %collective-permute-start.182) | collective-permute-done | bytes 213024 | tf_op jit(solution)/shard_map/ppermute | solution.py:19
  587.6 4.9 collective-permute-done.180.refs_1_
  603.5 4.2 collective-permute-done.183
  613.8 3.6 collective-permute-start.190
  626.1 3.5 collective-permute-done.192
  635.5 5.3 collective-permute-done.194
  (892 shorter events, 475.0 us)
Async XLA Ops:
  33.0 50.1 %collective-permute-start.19 = (bf16[128,1280]{1,0:T(8,128)(2,1)S(1)}, bf16[128,1280]{1,0:T(8,128)(2,1)S(1)}, u32[]{:S(2)}, u32[]{:S(2)}) collective-permute-start(bf16[128,1280]{1,0:T(8,128)(2,1)S(1)} %get-tuple-element.499), channel_id=1, source_target_pairs={{0,96},{32,0},{64,32},{96,64},{8,104},{40,8},{72,40},{104,72},{16,... | collective-permute-start | bytes 983048 | tf_op jit(solution)/shard_map/ppermute | solution.py:31
  38.0 48.7 %collective-permute-start.21 = (bf16[128,1280]{1,0:T(8,128)(2,1)S(1)}, bf16[128,1280]{1,0:T(8,128)(2,1)S(1)}, u32[]{:S(2)}, u32[]{:S(2)}) collective-permute-start(bf16[128,1280]{1,0:T(8,128)(2,1)S(1)} %get-tuple-element.500), channel_id=1, source_target_pairs={{0,32},{32,64},{64,96},{96,0},{8,40},{40,72},{72,104},{104,8},{16,... | collective-permute-start | bytes 983048 | tf_op jit(solution)/shard_map/ppermute | solution.py:31
  41.4 17.8 %collective-permute-start.13 = (bf16[64,1664]{1,0:T(8,128)(2,1)S(1)}, bf16[64,1664]{1,0:T(8,128)(2,1)S(1)}, u32[]{:S(2)}, u32[]{:S(2)}) collective-permute-start(bf16[64,1664]{1,0:T(8,128)(2,1)S(1)} %get-tuple-element.250), channel_id=1, source_target_pairs={{0,32},{32,64},{64,96},{96,0},{1,33},{33,65},{65,97},{97,1},{2,34}... | collective-permute-start | bytes 638984 | tf_op jit(solution)/shard_map/ppermute | solution.py:19
  42.0 17.2 %collective-permute-start.14 = (bf16[64,1664]{1,0:T(8,128)(2,1)S(1)}, bf16[64,1664]{1,0:T(8,128)(2,1)S(1)}, u32[]{:S(2)}, u32[]{:S(2)}) collective-permute-start(bf16[64,1664]{1,0:T(8,128)(2,1)S(1)} %get-tuple-element.251), channel_id=1, source_target_pairs={{0,64},{32,96},{64,0},{96,32},{1,65},{33,97},{65,1},{97,33},{2,66}... | collective-permute-start | bytes 638984 | tf_op jit(solution)/shard_map/ppermute | solution.py:19
  67.8 27.1 %collective-permute-start.20 = (bf16[128,1280]{1,0:T(8,128)(2,1)S(1)}, bf16[128,1280]{1,0:T(8,128)(2,1)S(1)}, u32[]{:S(2)}, u32[]{:S(2)}) collective-permute-start(bf16[128,1280]{1,0:T(8,128)(2,1)S(1)} %constant_dynamic-slice_fusion.5), channel_id=1, source_target_pairs={{0,64},{32,96},{64,0},{96,32},{8,72},{40,104},{72,8},{104,40},{16,... | collective-permute-start | bytes 983048 | tf_op jit(solution)/shard_map/ppermute | solution.py:31
  73.7 15.3 %collective-permute-start.25 = (bf16[32,1280]{1,0:T(8,128)(2,1)S(1)}, bf16[32,1280]{1,0:T(8,128)(2,1)S(1)}, u32[]{:S(2)}, u32[]{:S(2)}) collective-permute-start(bf16[32,1280]{1,0:T(8,128)(2,1)S(1)} %get-tuple-element.257), channel_id=1, source_target_pairs={{0,8},{1,9},{2,10},{3,11},{4,12},{5,13},{6,14},{7,15},{8,16},{9,17... | collective-permute-start | bytes 245768 | tf_op jit(solution)/shard_map/ppermute | solution.py:48
  101.1 69.7 %collective-permute-start.54 = (bf16[512,1280]{1,0:T(8,128)(2,1)S(1)}, bf16[512,1280]{1,0:T(8,128)(2,1)S(1)}, u32[]{:S(2)}, u32[]{:S(2)}) collective-permute-start(bf16[512,1280]{1,0:T(8,128)(2,1)S(1)} %get-tuple-element.299), channel_id=1, source_target_pairs={{0,8},{8,16},{16,24},{1,9},{9,17},{17,25},{2,10},{10,18},{18,26},{... | collective-permute-start | bytes 3932168 | tf_op jit(solution)/shard_map/ppermute | solution.py:37
  179.4 14.8 %collective-permute-start.70 = (bf16[32,1280]{1,0:T(8,128)(2,1)}, bf16[32,1280]{1,0:T(8,128)(2,1)}, u32[]{:S(2)}, u32[]{:S(2)}) collective-permute-start(bf16[32,1280]{1,0:T(8,128)(2,1)} %get-tuple-element.313), channel_id=1, source_target_pairs={{0,4},{1,5},{2,6},{3,7},{4,0},{5,1},{6,2},{7,3},{8,12},{9,13},{10,... | collective-permute-start | bytes 245768 | tf_op jit(solution)/shard_map/ppermute | solution.py:19
  188.6 76.9 %collective-permute-start.66 = (bf16[512,1280]{1,0:T(8,128)(2,1)S(1)}, bf16[512,1280]{1,0:T(8,128)(2,1)}, u32[]{:S(2)}, u32[]{:S(2)}) collective-permute-start(bf16[512,1280]{1,0:T(8,128)(2,1)S(1)} %get-tuple-element.308), channel_id=1, source_target_pairs={{0,8},{8,16},{16,24},{1,9},{9,17},{17,25},{2,10},{10,18},{18,26},{... | collective-permute-start | bytes 3932168 | tf_op jit(solution)/shard_map/ppermute | solution.py:37
  222.0 16.1 %collective-permute-start.17 = (bf16[64,1280]{1,0:T(8,128)(2,1)S(1)}, bf16[64,1280]{1,0:T(8,128)(2,1)S(1)}, u32[]{:S(2)}, u32[]{:S(2)}) collective-permute-start(bf16[64,1280]{1,0:T(8,128)(2,1)S(1)} %get-tuple-element.542), channel_id=1, source_target_pairs={{24,88},{56,120},{88,24},{120,56},{25,89},{57,121},{89,25},{121,57... | collective-permute-start | bytes 491528 | tf_op jit(solution)/shard_map/ppermute | solution.py:31
  222.7 23.7 %collective-permute-start.16 = (bf16[64,1280]{1,0:T(8,128)(2,1)S(1)}, bf16[64,1280]{1,0:T(8,128)(2,1)S(1)}, u32[]{:S(2)}, u32[]{:S(2)}) collective-permute-start(bf16[64,1280]{1,0:T(8,128)(2,1)S(1)} %get-tuple-element.543), channel_id=1, source_target_pairs={{24,120},{56,24},{88,56},{120,88},{25,121},{57,25},{89,57},{121,89... | collective-permute-start | bytes 491528 | tf_op jit(solution)/shard_map/ppermute | solution.py:31
  232.6 16.0 %collective-permute-start.80 = (bf16[32,1280]{1,0:T(8,128)(2,1)S(1)}, bf16[32,1280]{1,0:T(8,128)(2,1)S(1)}, u32[]{:S(2)}, u32[]{:S(2)}) collective-permute-start(bf16[32,1280]{1,0:T(8,128)(2,1)S(1)} %get-tuple-element.322), channel_id=1, source_target_pairs={{0,8},{1,9},{2,10},{3,11},{4,12},{5,13},{6,14},{7,15},{8,16},{9,17... | collective-permute-start | bytes 245768 | tf_op jit(solution)/shard_map/ppermute | solution.py:48
  234.1 17.9 %collective-permute-start.81 = (bf16[32,1280]{1,0:T(8,128)(2,1)S(1)}, bf16[32,1280]{1,0:T(8,128)(2,1)S(1)}, u32[]{:S(2)}, u32[]{:S(2)}) collective-permute-start(bf16[32,1280]{1,0:T(8,128)(2,1)S(1)} %get-tuple-element.323), channel_id=1, source_target_pairs={{0,15},{1,8},{2,9},{3,10},{4,11},{5,12},{6,13},{7,14},{8,23},{9,16... | collective-permute-start | bytes 245768 | tf_op jit(solution)/shard_map/ppermute | solution.py:48
  238.2 17.6 %collective-permute-start.82 = (bf16[32,1280]{1,0:T(8,128)(2,1)S(1)}, bf16[32,1280]{1,0:T(8,128)(2,1)S(1)}, u32[]{:S(2)}, u32[]{:S(2)}) collective-permute-start(bf16[32,1280]{1,0:T(8,128)(2,1)S(1)} %get-tuple-element.324), channel_id=1, source_target_pairs={{0,14},{1,15},{2,8},{3,9},{4,10},{5,11},{6,12},{7,13},{8,22},{9,23... | collective-permute-start | bytes 245768 | tf_op jit(solution)/shard_map/ppermute | solution.py:48
  249.2 14.9 %collective-permute-start.84 = (bf16[32,1280]{1,0:T(8,128)(2,1)}, bf16[32,1280]{1,0:T(8,128)(2,1)}, u32[]{:S(2)}, u32[]{:S(2)}) collective-permute-start(bf16[32,1280]{1,0:T(8,128)(2,1)} %get-tuple-element.326), channel_id=1, source_target_pairs={{0,12},{1,13},{2,14},{3,15},{4,8},{5,9},{6,10},{7,11},{8,20},{9,21... | collective-permute-start | bytes 245768 | tf_op jit(solution)/shard_map/ppermute | solution.py:48
  309.6 16.7 %collective-permute-start.102 = (bf16[64,2560]{1,0:T(8,128)(2,1)S(1)}, bf16[64,2560]{1,0:T(8,128)(2,1)S(1)}, u32[]{:S(2)}, u32[]{:S(2)}) collective-permute-start(bf16[64,2560]{1,0:T(8,128)(2,1)S(1)} %shard_map.143.refs_0_), channel_id=1, source_target_pairs={{0,64},{32,96},{64,0},{96,32},{1,65},{33,97},{65,1},{97,33},{2,66}... | collective-permute-start | bytes 983048 | tf_op jit(solution)/shard_map/ppermute | solution.py:19
  313.5 21.3 %collective-permute-start.100 = (bf16[128,1280]{1,0:T(8,128)(2,1)S(1)}, bf16[128,1280]{1,0:T(8,128)(2,1)S(1)}, u32[]{:S(2)}, u32[]{:S(2)}) collective-permute-start(bf16[128,1280]{1,0:T(8,128)(2,1)S(1)} %get-tuple-element.496), channel_id=1, source_target_pairs={{0,32},{32,64},{64,96},{96,0},{8,40},{40,72},{72,104},{104,8},{16,... | collective-permute-start | bytes 983048 | tf_op jit(solution)/shard_map/ppermute | solution.py:31
  316.7 23.6 %collective-permute-start.99 = (bf16[128,1280]{1,0:T(8,128)(2,1)S(1)}, bf16[128,1280]{1,0:T(8,128)(2,1)S(1)}, u32[]{:S(2)}, u32[]{:S(2)}) collective-permute-start(bf16[128,1280]{1,0:T(8,128)(2,1)S(1)} %get-tuple-element.497), channel_id=1, source_target_pairs={{0,64},{32,96},{64,0},{96,32},{8,72},{40,104},{72,8},{104,40},{16,... | collective-permute-start | bytes 983048 | tf_op jit(solution)/shard_map/ppermute | solution.py:31
  319.3 22.2 %collective-permute-start.98 = (bf16[128,1280]{1,0:T(8,128)(2,1)S(1)}, bf16[128,1280]{1,0:T(8,128)(2,1)S(1)}, u32[]{:S(2)}, u32[]{:S(2)}) collective-permute-start(bf16[128,1280]{1,0:T(8,128)(2,1)S(1)} %get-tuple-element.498), channel_id=1, source_target_pairs={{0,96},{32,0},{64,32},{96,64},{8,104},{40,8},{72,40},{104,72},{16,... | collective-permute-start | bytes 983048 | tf_op jit(solution)/shard_map/ppermute | solution.py:31
  359.8 19.2 %collective-permute-start.122 = (bf16[128,1280]{1,0:T(8,128)(2,1)S(1)}, bf16[128,1280]{1,0:T(8,128)(2,1)S(1)}, u32[]{:S(2)}, u32[]{:S(2)}) collective-permute-start(bf16[128,1280]{1,0:T(8,128)(2,1)S(1)} %get-tuple-element.491), channel_id=1, source_target_pairs={{0,96},{32,0},{64,32},{96,64},{1,97},{33,1},{65,33},{97,65},{2,98}... | collective-permute-start | bytes 983048 | tf_op jit(solution)/shard_map/ppermute | solution.py:19
  360.7 18.3 %collective-permute-start.121 = (bf16[128,1280]{1,0:T(8,128)(2,1)S(1)}, bf16[128,1280]{1,0:T(8,128)(2,1)S(1)}, u32[]{:S(2)}, u32[]{:S(2)}) collective-permute-start(bf16[128,1280]{1,0:T(8,128)(2,1)S(1)} %get-tuple-element.492), channel_id=1, source_target_pairs={{0,64},{32,96},{64,0},{96,32},{1,65},{33,97},{65,1},{97,33},{2,66}... | collective-permute-start | bytes 983048 | tf_op jit(solution)/shard_map/ppermute | solution.py:19
  361.2 17.8 %collective-permute-start.120 = (bf16[128,1280]{1,0:T(8,128)(2,1)S(1)}, bf16[128,1280]{1,0:T(8,128)(2,1)S(1)}, u32[]{:S(2)}, u32[]{:S(2)}) collective-permute-start(bf16[128,1280]{1,0:T(8,128)(2,1)S(1)} %get-tuple-element.493), channel_id=1, source_target_pairs={{0,32},{32,64},{64,96},{96,0},{1,33},{33,65},{65,97},{97,1},{2,34}... | collective-permute-start | bytes 983048 | tf_op jit(solution)/shard_map/ppermute | solution.py:19
  388.5 55.3 %collective-permute-start.123 = (bf16[512,1280]{1,0:T(8,128)(2,1)}, bf16[512,1280]{1,0:T(8,128)(2,1)S(1)}, u32[]{:S(2)}, u32[]{:S(2)}) collective-permute-start(bf16[512,1280]{1,0:T(8,128)(2,1)} %copy-done.25), channel_id=1, source_target_pairs={{8,0},{16,8},{24,16},{9,1},{17,9},{25,17},{10,2},{18,10},{26,18},{... | collective-permute-start | bytes 3932168 | tf_op jit(solution)/shard_map/ppermute | solution.py:37
  461.3 64.0 %collective-permute-start.158 = (bf16[512,1280]{1,0:T(8,128)(2,1)}, bf16[512,1280]{1,0:T(8,128)(2,1)}, u32[]{:S(2)}, u32[]{:S(2)}) collective-permute-start(bf16[512,1280]{1,0:T(8,128)(2,1)} %get-tuple-element.440), channel_id=1, source_target_pairs={{8,0},{16,8},{24,16},{9,1},{17,9},{25,17},{10,2},{18,10},{26,18},{... | collective-permute-start | bytes 3932168 | tf_op jit(solution)/shard_map/ppermute | solution.py:37
  476.7 17.1 %collective-permute-start.161 = (bf16[64,1664]{1,0:T(8,128)(2,1)S(1)}, bf16[64,1664]{1,0:T(8,128)(2,1)S(1)}, u32[]{:S(2)}, u32[]{:S(2)}) collective-permute-start(bf16[64,1664]{1,0:T(8,128)(2,1)S(1)} %shard_map.152.refs_0_), channel_id=1, source_target_pairs={{0,32},{32,64},{64,96},{96,0},{1,33},{33,65},{65,97},{97,1},{2,34}... | collective-permute-start | bytes 638984 | tf_op jit(solution)/shard_map/ppermute | solution.py:19
  477.8 16.0 %collective-permute-start.160 = (bf16[64,1664]{1,0:T(8,128)(2,1)S(1)}, bf16[64,1664]{1,0:T(8,128)(2,1)S(1)}, u32[]{:S(2)}, u32[]{:S(2)}) collective-permute-start(bf16[64,1664]{1,0:T(8,128)(2,1)S(1)} %shard_map.152.refs_0_), channel_id=1, source_target_pairs={{0,64},{32,96},{64,0},{96,32},{1,65},{33,97},{65,1},{97,33},{2,66}... | collective-permute-start | bytes 638984 | tf_op jit(solution)/shard_map/ppermute | solution.py:19
  563.9 77.0 %collective-permute-start.188 = (bf16[128,1280]{1,0:T(8,128)(2,1)S(1)}, bf16[128,1280]{1,0:T(8,128)(2,1)S(1)}, u32[]{:S(2)}, u32[]{:S(2)}) collective-permute-start(bf16[128,1280]{1,0:T(8,128)(2,1)S(1)} %get-tuple-element.484), channel_id=1, source_target_pairs={{0,96},{32,0},{64,32},{96,64},{8,104},{40,8},{72,40},{104,72},{16,... | collective-permute-start | bytes 983048 | tf_op jit(solution)/shard_map/ppermute | solution.py:31
  566.4 74.5 %collective-permute-start.187 = (bf16[128,1280]{1,0:T(8,128)(2,1)S(1)}, bf16[128,1280]{1,0:T(8,128)(2,1)S(1)}, u32[]{:S(2)}, u32[]{:S(2)}) collective-permute-start(bf16[128,1280]{1,0:T(8,128)(2,1)S(1)} %get-tuple-element.485), channel_id=1, source_target_pairs={{0,64},{32,96},{64,0},{96,32},{8,72},{40,104},{72,8},{104,40},{16,... | collective-permute-start | bytes 983048 | tf_op jit(solution)/shard_map/ppermute | solution.py:31
  571.2 16.4 %collective-permute-start.181 = (bf16[64,1664]{1,0:T(8,128)(2,1)S(1)}, bf16[64,1664]{1,0:T(8,128)(2,1)S(1)}, u32[]{:S(2)}, u32[]{:S(2)}) collective-permute-start(bf16[64,1664]{1,0:T(8,128)(2,1)S(1)} %shard_map.156.refs_0_), channel_id=1, source_target_pairs={{0,64},{32,96},{64,0},{96,32},{1,65},{33,97},{65,1},{97,33},{2,66}... | collective-permute-start | bytes 638984 | tf_op jit(solution)/shard_map/ppermute | solution.py:19
  573.1 19.3 %collective-permute-start.180 = (bf16[64,1664]{1,0:T(8,128)(2,1)S(1)}, bf16[64,1664]{1,0:T(8,128)(2,1)S(1)}, u32[]{:S(2)}, u32[]{:S(2)}) collective-permute-start(bf16[64,1664]{1,0:T(8,128)(2,1)S(1)} %shard_map.156.refs_0_), channel_id=1, source_target_pairs={{0,96},{32,0},{64,32},{96,64},{1,97},{33,1},{65,33},{97,65},{2,98}... | collective-permute-start | bytes 638984 | tf_op jit(solution)/shard_map/ppermute | solution.py:19
  610.9 29.9 %collective-permute-start.186 = (bf16[128,1280]{1,0:T(8,128)(2,1)S(1)}, bf16[128,1280]{1,0:T(8,128)(2,1)S(1)}, u32[]{:S(2)}, u32[]{:S(2)}) collective-permute-start(bf16[128,1280]{1,0:T(8,128)(2,1)S(1)} %get-tuple-element.466), channel_id=1, source_target_pairs={{0,32},{32,64},{64,96},{96,0},{8,40},{40,72},{72,104},{104,8},{16,... | collective-permute-start | bytes 983048 | tf_op jit(solution)/shard_map/ppermute | solution.py:31
  612.8 28.0 %collective-permute-start.195 = (bf16[8,5120]{1,0:T(8,128)(2,1)S(1)}, bf16[8,5120]{1,0:T(8,128)(2,1)S(1)}, u32[]{:S(2)}, u32[]{:S(2)}) collective-permute-start(bf16[8,5120]{1,0:T(8,128)(2,1)S(1)} %get-tuple-element.501), channel_id=1, source_target_pairs={{0,1},{1,2},{2,3},{3,4},{4,5},{5,6},{6,7},{7,0},{8,9},{9,10},{10,1... | collective-permute-start | bytes 245768 | tf_op jit(solution)/shard_map/ppermute | solution.py:19
  (364 other events, 3607.8 us)
